TPU v7x, 128 devices: a whole 4x4x4 slice. The times are simulated.
128 devices in a mesh: shard: 32 (over z, x, core), tensor: 4 (over y).
Axes of the slice: x: 4, y: 4, z: 4, core: 2. Of those that a mesh axis runs over, the one named last changes fastest.
Arguments:
- weights: float32 [48, 640, 1280], P(None, 'shard', 'tensor'), may hold values from -40 to 40
- grads: bfloat16 [48, 640, 1280], P(None, 'shard', 'tensor'), may hold values from -13 to 13
- owner_slot: int32 [96], replicated, may hold values from 0 to 255, as said below
- left_stats: float32 [256, 640, 640], P(('shard', 'tensor')), may hold values from -0.15 to 2, as said below
- right_stats: float32 [256, 640, 640], P(('shard', 'tensor')), may hold values from -0.15 to 2, as said below
- left_root: bfloat16 [256, 640, 640], P(('shard', 'tensor')), may hold values from -0.15 to 1.5, as said below
- right_root: bfloat16 [256, 640, 640], P(('shard', 'tensor')), may hold values from -0.15 to 1.5, as said below
- moment: float32 [256, 640, 640], P(('shard', 'tensor')), may hold values from 1e-05 to 0.001
Outputs:
- new_weights: float32 [48, 640, 1280], P(None, 'shard', 'tensor')
- new_left: float32 [256, 640, 640], P(('shard', 'tensor'))
- new_right: float32 [256, 640, 640], P(('shard', 'tensor'))
- new_moment: float32 [256, 640, 640], P(('shard', 'tensor'))
Inputs may be any that keep to these rules, and one draw needn't show every extreme that they name: `owner_slot`: the values are distinct; the slots g with g // 2 equal to one device are that device's, and some device holds 2 blocks in every draw. `left_stats`: Symmetric. `right_stats`: Symmetric. `left_root`: Symmetric. `right_root`: Symmetric.
All inputs are finite; a program needn't handle non-finite values.
Results may differ from a plain program's by a relative error of at most 0.0017.
Values may be sent and summed in bfloat16 or wider, within the bound.
A program may use at most 128 MiB of HBM per device.

v0:
```python
import jax
import jax.numpy as jnp
from jax import lax
from jax.sharding import PartitionSpec as P

stat_decay = 0.9
step_size = 0.2


def route_out(outgoing):
    arrived = lax.all_to_all(outgoing, ("shard", "tensor"), split_axis=0, concat_axis=0, tiled=True)
    return arrived


def route_back(outgoing):
    arrived = lax.all_to_all(outgoing, ("shard", "tensor"), split_axis=0, concat_axis=0, tiled=True)
    return arrived


def refresh(block_grads, left_stats, right_stats):
    gram_left = jnp.einsum(
        "kij,klj->kil", block_grads, block_grads, preferred_element_type=jnp.float32
    )
    gram_right = jnp.einsum(
        "kji,kjl->kil", block_grads, block_grads, preferred_element_type=jnp.float32
    )
    new_left = stat_decay * left_stats + (1.0 - stat_decay) * gram_left
    new_right = stat_decay * right_stats + (1.0 - stat_decay) * gram_right
    return (new_left, new_right)


def direction(block_grads, left_root, right_root, moment):
    half = jnp.einsum(
        "kij,kjl->kil", left_root, block_grads, preferred_element_type=jnp.float32
    ).astype(jnp.bfloat16)
    precond = jnp.einsum("kij,kjl->kil", half, right_root, preferred_element_type=jnp.float32)
    grad_full = block_grads.astype(jnp.float32)
    new_moment = stat_decay * moment + (1.0 - stat_decay) * grad_full * grad_full
    adam = grad_full / (jnp.sqrt(new_moment) + 1e-08)
    graft = jnp.sqrt(jnp.mean(adam * adam, axis=(1, 2))) / jnp.sqrt(
        jnp.mean(precond * precond, axis=(1, 2)) + 1e-06
    )
    delta = (graft[:, None, None] * precond).astype(jnp.bfloat16)
    return (delta, new_moment)


def body(weights, grads, owner_slot, left_stats, right_stats, left_root, right_root, moment):
    n_shard = lax.axis_size("shard")
    n_tensor = lax.axis_size("tensor")
    row_blocks, shard_rows, shard_cols = grads.shape
    order_size = left_stats.shape[1]
    width = shard_cols * n_tensor
    col_blocks = width // order_size
    per_block = n_tensor // col_blocks
    slots = left_stats.shape[0]
    owners = n_shard * n_tensor
    total_slots = owners * slots
    block_count = owner_slot.shape[0]
    mine_col = lax.axis_index("tensor") // per_block
    table = owner_slot.reshape(row_blocks, col_blocks)
    chosen = jnp.arange(col_blocks) == mine_col
    targets = jnp.sum(jnp.where(chosen[None, :], table, 0), axis=1)
    outgoing = jnp.zeros((total_slots, shard_rows, shard_cols), jnp.bfloat16).at[targets].set(grads)
    arrived = route_out(outgoing)
    arrived = arrived.reshape(n_shard, col_blocks, per_block, slots, shard_rows, shard_cols)
    owner_index = lax.axis_index(("shard", "tensor"))
    global_ids = owner_index * slots + jnp.arange(slots)
    matches = owner_slot[None, :] == global_ids[:, None]
    block_ids = jnp.sum(jnp.where(matches, jnp.arange(block_count)[None, :], 0), axis=1)
    slot_col = block_ids % col_blocks
    picker = jnp.arange(col_blocks)[:, None] == slot_col[None, :]
    picked = jnp.sum(jnp.where(picker[None, :, None, :, None, None], arrived, 0), axis=1)
    block_grads = picked.transpose(2, 0, 3, 1, 4).reshape(slots, order_size, order_size)
    new_left, new_right = refresh(block_grads, left_stats, right_stats)
    delta, new_moment = direction(block_grads, left_root, right_root, moment)
    pieces = delta.reshape(slots, n_shard, shard_rows, per_block, shard_cols).transpose(
        1, 3, 0, 2, 4
    )
    pieces = jnp.broadcast_to(
        pieces[:, None], (n_shard, col_blocks, per_block, slots, shard_rows, shard_cols)
    )
    sendback = pieces.reshape(total_slots, shard_rows, shard_cols)
    returned = route_back(sendback)
    my_delta = returned[targets]
    updated = weights - step_size * my_delta.astype(jnp.float32)
    squares = lax.psum(jnp.sum(updated * updated, axis=2), "tensor")
    new_weights = updated * lax.rsqrt(squares / width + 1e-06)[:, :, None]
    return (new_weights, new_left, new_right, new_moment)


def solution(mesh):
    placed = (
        P(None, "shard", "tensor"),
        P(None, "shard", "tensor"),
        P(),
        P(("shard", "tensor"), None, None),
        P(("shard", "tensor"), None, None),
        P(("shard", "tensor"), None, None),
        P(("shard", "tensor"), None, None),
        P(("shard", "tensor"), None, None),
    )
    return jax.shard_map(
        body,
        mesh=mesh,
        in_specs=placed,
        out_specs=(
            P(None, "shard", "tensor"),
            P(("shard", "tensor"), None, None),
            P(("shard", "tensor"), None, None),
            P(("shard", "tensor"), None, None),
        ),
        check_vma=False,
    )
```

profile of v0, /device:TPU:0, one launch (start us, length us, event | category | flops | bytes accessed | tf_op | source)
XLA Modules:
  0.0 205.2 jit_solution(5529651684544861352)
XLA Ops:
  0.6 0.0 copy-start
  0.7 0.9 reshape.91
  1.6 0.1 select_reduce_fusion.1
  1.7 1.3 copy.27
  3.0 2.6 %broadcast_in_dim.59 = bf16[256,20,320]{2,1,0:T(8,128)(2,1)} broadcast(bf16[]{:T(256)} %constant.54.clone.1), dimensions={} | broadcast | bytes 3276802 | tf_op jit(solution)/shard_map/broadcast_in_dim | solution.py:63
  5.6 6.3 %scatter_fusion = bf16[256,20,320]{2,1,0:T(8,128)(2,1)} fusion(bf16[256,20,320]{2,1,0:T(8,128)(2,1)} %broadcast_in_dim.59, s32[48]{0:T(128)S(1)} %fusion.7, bf16[48,20,320]{2,1,0:T(8,128)(2,1)S(1)} %copy.27), kind=kCustom, calls=%fused_computation.1 | custom fusion | bytes 1843392 | tf_op jit(solution)/shard_map/scatter | solution.py:63
  11.9 0.0 copy-start.2
  11.9 11.6 %all-to-all-start = ((bf16[256,20,320]{2,1,0:T(8,128)(2,1)}), bf16[256,20,320]{2,1,0:T(8,128)(2,1)}, u32[]{:S(2)}, u32[]{:S(2)}) async-start(bf16[256,20,320]{2,1,0:T(8,128)(2,1)} %scatter_fusion), calls=%async_computation | async-start | bytes 9437184 | tf_op jit(solution)/shard_map/all_to_all | solution.py:11
  23.5 0.0 copy-done.2
  23.5 0.2 fusion.5
  23.7 56.8 %all-to-all-done = bf16[256,20,320]{2,1,0:T(8,128)(2,1)} async-done(((bf16[256,20,320]{2,1,0:T(8,128)(2,1)}), bf16[256,20,320]{2,1,0:T(8,128)(2,1)}, u32[]{:S(2)}, u32[]{:S(2)}) %all-to-all-start) | async-done | bytes 3276832 | tf_op jit(solution)/shard_map/all_to_all | solution.py:11
  80.6 4.7 %select_reduce_fusion = bf16[32,2,2,20,320]{4,3,2,1,0:T(8,128)(2,1)S(1)} fusion(bf16[32,2,2,2,20,320]{5,4,3,2,1,0:T(8,128)(2,1)} %bitcast.2, pred[2,2]{1,0:T(4,128)(4,1)S(1)} %iota_compare_fusion), kind=kLoop, calls=%fused_computation.3 | loop fusion | flops 2457600 | bytes 4915204 | tf_op jit(solution)/shard_map/reduce_sum | solution.py:72
  85.3 2.8 %copy.28 = bf16[2,32,20,2,320]{4,3,2,1,0:T(2,128)(2,1)} copy(bf16[2,32,20,2,320]{4,2,0,3,1:T(8,128)(2,1)S(1)} %bitcast.16) | data formatting | bytes 3276800 | tf_op jit(solution)/shard_map/transpose | solution.py:73
  88.1 4.2 %reshape.93 = bf16[2,640,640]{2,1,0:T(8,128)(2,1)S(1)} reshape(bf16[2,32,20,2,320]{4,3,2,1,0:T(2,128)(2,1)} %copy.28) | data formatting | bytes 3276800 | tf_op jit(solution)/shard_map/reshape | solution.py:73
  92.3 5.4 %fusion.2 = (f32[2]{0:T(128)S(1)}, f32[2,640,640]{2,1,0:T(8,128)}) fusion(bf16[2,640,640]{2,1,0:T(8,128)(2,1)S(1)} %reshape.93, f32[2,640,640]{2,1,0:T(8,128)} %param.15), kind=kLoop, calls=%fused_computation.11 | loop fusion | flops 7372798 | bytes 8192008 | tf_op jit(solution)/shard_map/reduce_sum | solution.py:40
  97.8 0.0 copy-done
  97.8 6.3 %multiply_reduce_fusion = (f32[2]{0:T(128)S(1)}, f32[2,640,640]{2,1,0:T(8,128)}) fusion(bf16[2,640,640]{2,1,0:T(8,128)(2,1)S(1)} %copy-done, bf16[2,640,640]{2,1,0:T(8,128)(2,1)S(1)} %reshape.93, bf16[2,640,640]{2,1,0:T(8,128)(2,1)} %param.13), kind=kOutput, calls=%fused_computation.10 | convolution fusion | flops 2099609600 | bytes 8192008 | tf_op jit(solution)/shard_map/kij,kjl->kil/dot_general | solution.py:36
  104.1 3.4 %multiply_convert_fusion = bf16[2,640,640]{2,1,0:T(8,128)(2,1)} fusion(f32[2,640,640]{2,1,0:T(8,128)} %get-tuple-element.19, f32[2]{0:T(128)S(1)} %rsqrt_multiply_fusion), kind=kLoop, calls=%fused_computation.9 | loop fusion | flops 1638400 | bytes 4915208 | tf_op jit(solution)/shard_map/convert_element_type | solution.py:43
  107.5 5.3 %reshape.94 = bf16[2,32,20,2,320]{4,3,2,1,0:T(2,128)(2,1)} reshape(bf16[2,640,640]{2,1,0:T(8,128)(2,1)} %multiply_convert_fusion) | data formatting | bytes 3276800 | tf_op jit(solution)/shard_map/reshape | solution.py:76
  112.8 1.9 copy.31
  114.7 2.7 %broadcast_in_dim.63 = bf16[32,2,2,2,20,320]{5,4,3,2,1,0:T(8,128)(2,1)} broadcast(bf16[32,2,2,20,320]{4,3,2,1,0:T(8,128)(2,1)S(1)} %copy.31), dimensions={0,2,3,4,5} | broadcast | bytes 4915200 | tf_op jit(solution)/shard_map/broadcast_in_dim | solution.py:79
  117.4 5.9 %all-to-all-start.1 = ((bf16[256,20,320]{2,1,0:T(8,128)(2,1)}), bf16[256,20,320]{2,1,0:T(8,128)(2,1)}, u32[]{:S(2)}, u32[]{:S(2)}) async-start(bf16[256,20,320]{2,1,0:T(8,128)(2,1)} %bitcast.15), calls=%async_computation.1 | async-start | bytes 9437184 | tf_op jit(solution)/shard_map/all_to_all | solution.py:16
  123.3 0.0 copy-start.1
  123.3 5.5 %multiply_add_fusion = f32[2,640,640]{2,1,0:T(8,128)} fusion(f32[2,640,640]{2,1,0:T(8,128)} %param.12, bf16[2,640,640]{2,1,0:T(8,128)(2,1)S(1)} %reshape.93), kind=kOutput, calls=%fused_computation.7 | convolution fusion | flops 1051033600 | bytes 8192000 | tf_op jit(solution)/shard_map/kji,kjl->kil/dot_general | solution.py:24
  128.8 0.0 copy-done.1
  128.8 3.5 %multiply_add_fusion.1 = f32[2,640,640]{2,1,0:T(8,128)} fusion(f32[2,640,640]{2,1,0:T(8,128)S(1)} %copy-done.1, bf16[2,640,640]{2,1,0:T(8,128)(2,1)S(1)} %reshape.93), kind=kOutput, calls=%fused_computation.8 | convolution fusion | flops 1051033600 | bytes 8192000 | tf_op jit(solution)/shard_map/kij,klj->kil/dot_general | solution.py:21
  132.2 48.1 %all-to-all-done.1 = bf16[256,20,320]{2,1,0:T(8,128)(2,1)} async-done(((bf16[256,20,320]{2,1,0:T(8,128)(2,1)}), bf16[256,20,320]{2,1,0:T(8,128)(2,1)}, u32[]{:S(2)}, u32[]{:S(2)}) %all-to-all-start.1) | async-done | bytes 3276832 | tf_op jit(solution)/shard_map/all_to_all | solution.py:16
  180.3 3.1 %gather_fusion = bf16[48,20,320]{2,1,0:T(8,128)(2,1)S(1)} fusion(bf16[256,20,320]{2,1,0:T(8,128)(2,1)} %all-to-all-done.1, s32[1024]{0:T(1024)S(1)} %pad_clamp_fusion), kind=kCustom, calls=%fused_computation | custom fusion | bytes 1228992 | tf_op jit(solution)/shard_map/gather | solution.py:84
  183.5 2.0 multiply_reduce_fusion.1
  185.5 16.4 %psum.7 = f32[48,20]{1,0:T(8,128)S(1)} all-reduce(f32[48,20]{1,0:T(8,128)S(1)} %multiply_reduce_fusion.1), channel_id=1, replica_groups=mesh['shard'=32,'tensor'=4] {'tensor'}, use_global_device_ids=true, to_apply=%region_7.8 | all-reduce | flops 960 | bytes 7680 | tf_op jit(solution)/shard_map/psum | solution.py:86
  201.9 2.0 fusion.3
  203.8 1.4 copy.34
  (8 shorter events, 0.1 us)
Async XLA Ops:
  0.6 97.1 %copy-start = (bf16[2,640,640]{2,1,0:T(8,128)(2,1)S(1)}, bf16[2,640,640]{2,1,0:T(8,128)(2,1)}, u32[]{:S(2)}) copy-start(bf16[2,640,640]{2,1,0:T(8,128)(2,1)} %param.14) | copy-start | bytes 4915204
  11.9 11.6 %copy-start.2 = (s32[96]{0:T(128)S(1)}, s32[96]{0:T(128)}, u32[]{:S(2)}) copy-start(s32[96]{0:T(128)} %param.10) | copy-start | bytes 1156
  11.9 68.7 %all-to-all-start = ((bf16[256,20,320]{2,1,0:T(8,128)(2,1)}), bf16[256,20,320]{2,1,0:T(8,128)(2,1)}, u32[]{:S(2)}, u32[]{:S(2)}) async-start(bf16[256,20,320]{2,1,0:T(8,128)(2,1)} %scatter_fusion), calls=%async_computation | async-start | bytes 9437184 | tf_op jit(solution)/shard_map/all_to_all | solution.py:11
  117.4 63.0 %all-to-all-start.1 = ((bf16[256,20,320]{2,1,0:T(8,128)(2,1)}), bf16[256,20,320]{2,1,0:T(8,128)(2,1)}, u32[]{:S(2)}, u32[]{:S(2)}) async-start(bf16[256,20,320]{2,1,0:T(8,128)(2,1)} %bitcast.15), calls=%async_computation.1 | async-start | bytes 9437184 | tf_op jit(solution)/shard_map/all_to_all | solution.py:16
  123.3 5.5 %copy-start.1 = (f32[2,640,640]{2,1,0:T(8,128)S(1)}, f32[2,640,640]{2,1,0:T(8,128)}, u32[]{:S(2)}) copy-start(f32[2,640,640]{2,1,0:T(8,128)} %param.11) | copy-start | bytes 9830404
where the time goes:
time: 206 us; the launch traced here: 205 us
  waiting for transfers between devices  105 us (51%)
  local copies, waits for them, and re-layouts  32.5 us (16%)
  other arithmetic  17.9 us (9%)
  starting transfers between devices  17.5 us (8%)
  blocking collectives  16.4 us (8%)
  matrix products  15.3 us (7%)
    all_to_all x1, waiting for transfers between devices, route_out(): lax.all_to_all(outgoing, ('shard', 'tensor'), split_axis=0, concat_axis=0...  56.8 us
    all_to_all x1, waiting for transfers between devices, route_back(): lax.all_to_all(outgoing, ('shard', 'tensor'), split_axis=0, concat_axis=0...  48.1 us
    psum x1, blocking collectives, body(): squares = lax.psum(jnp.sum(updated * updated, axis=2), 'tensor')  16.4 us
    all_to_all x1, starting transfers between devices, route_out(): lax.all_to_all(outgoing, ('shard', 'tensor'), split_axis=0, concat_axis=0...  11.6 us
    dot_general x1, matrix products, direction(): jnp.einsum('kij,kjl->kil', half, right_root, preferred_element_type=jnp.f...  6.34 us
    scatter x1, local copies, waits for them, and re-layouts, body(): jnp.zeros((total_slots, shard_rows, shard_cols), jnp.bfloat16).at[targets]  6.31 us
    all_to_all x1, starting transfers between devices, route_back(): lax.all_to_all(outgoing, ('shard', 'tensor'), split_axis=0, concat_axis=0...  5.89 us
    dot_general x1, matrix products, refresh(): jnp.einsum('kji,kjl->kil', block_grads, block_grads, preferred_element_ty...  5.46 us
  transfers between devices with their start and end apart: 2, of which 2 were waited for; matrix products, arithmetic and copies ran while one was open for 4% of the time, Pallas kernels for 0%

commit v1 on v0

--- a/solution.py
+++ b/solution.py
@@ -55,33 +55,33 @@
     slots = left_stats.shape[0]
     owners = n_shard * n_tensor
     total_slots = owners * slots
-    block_count = owner_slot.shape[0]
+    half = shard_rows // col_blocks
     mine_col = lax.axis_index("tensor") // per_block
-    table = owner_slot.reshape(row_blocks, col_blocks)
-    chosen = jnp.arange(col_blocks) == mine_col
-    targets = jnp.sum(jnp.where(chosen[None, :], table, 0), axis=1)
-    outgoing = jnp.zeros((total_slots, shard_rows, shard_cols), jnp.bfloat16).at[targets].set(grads)
+    partner = [(i, (i + per_block) % n_tensor) for i in range(n_tensor)]
+    keep = lax.dynamic_slice_in_dim(grads, mine_col * half, half, axis=1)
+    give = lax.dynamic_slice_in_dim(grads, (1 - mine_col) * half, half, axis=1)
+    got = lax.ppermute(give, "tensor", partner)
+    first = jnp.where(mine_col == 0, keep, got)
+    second = jnp.where(mine_col == 0, got, keep)
+    slabs = jnp.stack([first, second], axis=1).reshape(row_blocks * col_blocks, half, shard_cols)
+    outgoing = jnp.zeros((total_slots, half, shard_cols), jnp.bfloat16).at[owner_slot].set(slabs)
     arrived = route_out(outgoing)
-    arrived = arrived.reshape(n_shard, col_blocks, per_block, slots, shard_rows, shard_cols)
-    owner_index = lax.axis_index(("shard", "tensor"))
-    global_ids = owner_index * slots + jnp.arange(slots)
-    matches = owner_slot[None, :] == global_ids[:, None]
-    block_ids = jnp.sum(jnp.where(matches, jnp.arange(block_count)[None, :], 0), axis=1)
-    slot_col = block_ids % col_blocks
-    picker = jnp.arange(col_blocks)[:, None] == slot_col[None, :]
-    picked = jnp.sum(jnp.where(picker[None, :, None, :, None, None], arrived, 0), axis=1)
-    block_grads = picked.transpose(2, 0, 3, 1, 4).reshape(slots, order_size, order_size)
+    arrived = arrived.reshape(n_shard, col_blocks, per_block, slots, half, shard_cols)
+    block_grads = arrived.transpose(3, 0, 1, 4, 2, 5).reshape(slots, order_size, order_size)
     new_left, new_right = refresh(block_grads, left_stats, right_stats)
     delta, new_moment = direction(block_grads, left_root, right_root, moment)
-    pieces = delta.reshape(slots, n_shard, shard_rows, per_block, shard_cols).transpose(
-        1, 3, 0, 2, 4
+    pieces = delta.reshape(slots, n_shard, col_blocks, half, per_block, shard_cols).transpose(
+        1, 2, 4, 0, 3, 5
     )
-    pieces = jnp.broadcast_to(
-        pieces[:, None], (n_shard, col_blocks, per_block, slots, shard_rows, shard_cols)
-    )
-    sendback = pieces.reshape(total_slots, shard_rows, shard_cols)
+    sendback = pieces.reshape(total_slots, half, shard_cols)
     returned = route_back(sendback)
-    my_delta = returned[targets]
+    back = returned[owner_slot].reshape(row_blocks, col_blocks, half, shard_cols)
+    own_part = jnp.where(mine_col == 0, back[:, 0], back[:, 1])
+    other_part = jnp.where(mine_col == 0, back[:, 1], back[:, 0])
+    other_back = lax.ppermute(other_part, "tensor", partner)
+    top = jnp.where(mine_col == 0, own_part, other_back)
+    bottom = jnp.where(mine_col == 0, other_back, own_part)
+    my_delta = jnp.concatenate([top, bottom], axis=1)
     updated = weights - step_size * my_delta.astype(jnp.float32)
     squares = lax.psum(jnp.sum(updated * updated, axis=2), "tensor")
     new_weights = updated * lax.rsqrt(squares / width + 1e-06)[:, :, None]

time: 206 us -> 197 us (0.956)
  waiting for transfers between devices: 105 us -> 50.7 us
  blocking collectives: 16.4 us -> 66.6 us
  starting transfers between devices: 17.5 us -> 10.4 us
  local copies, waits for them, and re-layouts: 32.5 us -> 37.3 us
  other arithmetic: 17.9 us -> 15.1 us
    all_to_all x1 -> x0, waiting for transfers between devices: 56.8 us -> none  [route_out(): lax.all_to_all(outgoing, ('shard', 'tensor'), split_axis=0, concat_axis=0...]
    all_to_all x0 -> x1, blocking collectives: none -> 51.9 us  [route_out(): lax.all_to_all(outgoing, ('shard', 'tensor'), split_axis=0, concat_axis=0...]
    ppermute x0 -> x2, waiting for transfers between devices: none -> 15.8 us  [the longest x1 7.93 us: body(): got = lax.ppermute(give, 'tensor', partner)]
    all_to_all x1, waiting for transfers between devices: 48.1 us -> 34.9 us  [route_back(): lax.all_to_all(outgoing, ('shard', 'tensor'), split_axis=0, concat_axis=0...]
    all_to_all x1 -> x0, starting transfers between devices: 11.6 us -> none  [route_out(): lax.all_to_all(outgoing, ('shard', 'tensor'), split_axis=0, concat_axis=0...]
    scatter x1, local copies, waits for them, and re-layouts: 6.31 us -> 11.8 us  [body(): jnp.zeros((total_slots, half, shard_cols), jnp.bfloat16).at[owner_slot]]
    reduce_sum x3 -> x0, other arithmetic: 5.02 us -> none  [the longest x1 4.73 us: body(): jnp.sum(jnp.where(picker[None, :, None, :, None, None], arrived, 0), axis=1)]
    ppermute x0 -> x2, starting transfers between devices: none -> 4.43 us  [the longest x1 3.39 us: body(): got = lax.ppermute(give, 'tensor', partner)]
  transfers between devices with their start and end apart: 2 -> 3, of which waited for: 2 -> 3; matrix products, arithmetic and copies ran while one was open for 4% -> 5% of each run, Pallas kernels for 0% -> 0%
where the time goes in v1:
time: 197 us; the launch traced here: 196 us
  blocking collectives  66.6 us (34%)
  waiting for transfers between devices  50.7 us (26%)
  local copies, waits for them, and re-layouts  37.3 us (19%)
  other arithmetic  15.1 us (8%)
  matrix products  15.1 us (8%)
  starting transfers between devices  10.4 us (5%)
    all_to_all x1, blocking collectives, route_out(): lax.all_to_all(outgoing, ('shard', 'tensor'), split_axis=0, concat_axis=0...  51.9 us
    all_to_all x1, waiting for transfers between devices, route_back(): lax.all_to_all(outgoing, ('shard', 'tensor'), split_axis=0, concat_axis=0...  34.9 us
    psum x1, blocking collectives, body(): squares = lax.psum(jnp.sum(updated * updated, axis=2), 'tensor')  14.7 us
    scatter x1, local copies, waits for them, and re-layouts, body(): jnp.zeros((total_slots, half, shard_cols), jnp.bfloat16).at[owner_slot]  11.8 us
    ppermute x1, waiting for transfers between devices, body(): got = lax.ppermute(give, 'tensor', partner)  7.93 us
    ppermute x1, waiting for transfers between devices, body(): other_back = lax.ppermute(other_part, 'tensor', partner)  7.92 us
    dot_general x1, matrix products, direction(): jnp.einsum('kij,kjl->kil', half, right_root, preferred_element_type=jnp.f...  6.34 us
    all_to_all x1, starting transfers between devices, route_back(): lax.all_to_all(outgoing, ('shard', 'tensor'), split_axis=0, concat_axis=0...  5.96 us
  transfers between devices with their start and end apart: 3, of which 3 were waited for; matrix products, arithmetic and copies ran while one was open for 5% of the time, Pallas kernels for 0%

profile of v1, /device:TPU:0, one launch (start us, length us, event | category | flops | bytes accessed | tf_op | source)
XLA Modules:
  0.0 195.9 jit_solution(1598067226432760051)
XLA Ops:
  0.6 0.0 copy-start
  0.7 1.1 constant_dynamic-slice_fusion
  1.8 3.4 %collective-permute-start = (bf16[48,10,320]{2,0,1:T(8,128)(2,1)S(1)}, bf16[48,10,320]{2,0,1:T(8,128)(2,1)S(1)}, u32[]{:S(2)}, u32[]{:S(2)}) collective-permute-start(bf16[48,10,320]{2,0,1:T(8,128)(2,1)S(1)} %constant_dynamic-slice_fusion), channel_id=1, source_target_pairs={{0,2},{1,3},{2,0},{3,1},{4,6},{5,7},{6,4},{7,5},{8,10},{9,11},{10,... | collective-permute-start | bytes 921608 | tf_op jit(solution)/shard_map/ppermute | solution.py:63
  5.2 0.7 compare_select_fusion
  5.9 7.9 %collective-permute-done = bf16[48,10,320]{2,0,1:T(8,128)(2,1)S(1)} collective-permute-done((bf16[48,10,320]{2,0,1:T(8,128)(2,1)S(1)}, bf16[48,10,320]{2,0,1:T(8,128)(2,1)S(1)}, u32[]{:S(2)}, u32[]{:S(2)}) %collective-permute-start) | collective-permute-done | bytes 307232 | tf_op jit(solution)/shard_map/ppermute | solution.py:63
  13.8 1.1 select_bitcast_fusion.1
  14.9 0.1 pad_maximum_fusion
  15.0 0.2 copy.53
  15.2 1.9 broadcast_in_dim.4
  17.2 11.8 %scatter_fusion = bf16[256,10,320]{2,1,0:T(8,128)(2,1)} fusion(bf16[256,10,320]{2,1,0:T(8,128)(2,1)} %broadcast_in_dim.4, s32[96]{0:T(128)S(1)} %compare_select_fusion, bf16[96,10,320]{2,1,0:T(8,128)(2,1)S(1)} %bitcast.32), kind=kCustom, calls=%fused_computation.1 | custom fusion | bytes 1843584 | tf_op jit(solution)/shard_map/scatter | solution.py:67
  29.0 51.9 %all_to_all.10 = bf16[256,10,320]{2,1,0:T(8,128)(2,1)S(1)} all-to-all(bf16[256,10,320]{2,1,0:T(8,128)(2,1)} %scatter_fusion), channel_id=1, replica_groups=mesh['shard'=32,'tensor'=4] {'shard','tensor'}, dimensions={0} | all-to-all | bytes 3276800 | tf_op jit(solution)/shard_map/all_to_all | solution.py:11
  80.9 2.8 %copy.72 = bf16[32,2,2,2,10,320]{5,2,4,1,0,3:T(2,128)(2,1)} copy(bf16[32,2,2,2,10,320]{5,4,3,2,1,0:T(8,128)(2,1)S(1)} %bitcast.28) | data formatting | bytes 3276800 | tf_op jit(solution)/shard_map/transpose | solution.py:70
  83.7 4.2 %reshape.43 = bf16[2,640,640]{2,1,0:T(8,128)(2,1)S(1)} reshape(bf16[2,32,2,10,2,320]{5,4,3,2,1,0:T(2,128)(2,1)} %bitcast.29) | data formatting | bytes 3276800 | tf_op jit(solution)/shard_map/reshape | solution.py:70
  87.9 5.4 %fusion.2 = (f32[2]{0:T(128)S(1)}, f32[2,640,640]{2,1,0:T(8,128)}) fusion(bf16[2,640,640]{2,1,0:T(8,128)(2,1)S(1)} %reshape.43, f32[2,640,640]{2,1,0:T(8,128)} %param.15), kind=kLoop, calls=%fused_computation.10 | loop fusion | flops 7372798 | bytes 8192008 | tf_op jit(solution)/shard_map/reduce_sum | solution.py:40
  93.3 0.0 copy-done
  93.3 6.3 %multiply_reduce_fusion = (f32[2]{0:T(128)S(1)}, f32[2,640,640]{2,1,0:T(8,128)}) fusion(bf16[2,640,640]{2,1,0:T(8,128)(2,1)S(1)} %copy-done, bf16[2,640,640]{2,1,0:T(8,128)(2,1)S(1)} %reshape.43, bf16[2,640,640]{2,1,0:T(8,128)(2,1)} %param.13), kind=kOutput, calls=%fused_computation.9 | convolution fusion | flops 2099609600 | bytes 8192008 | tf_op jit(solution)/shard_map/kij,kjl->kil/dot_general | solution.py:36
  99.7 3.4 %multiply_convert_fusion = bf16[2,640,640]{2,1,0:T(8,128)(2,1)} fusion(f32[2,640,640]{2,1,0:T(8,128)} %get-tuple-element.19, f32[2]{0:T(128)S(1)} %rsqrt_multiply_fusion), kind=kLoop, calls=%fused_computation.8 | loop fusion | flops 1638400 | bytes 4915208 | tf_op jit(solution)/shard_map/convert_element_type | solution.py:43
  103.1 5.3 %reshape.44 = bf16[2,32,2,10,2,320]{5,4,3,2,1,0:T(2,128)(2,1)} reshape(bf16[2,640,640]{2,1,0:T(8,128)(2,1)} %multiply_convert_fusion) | data formatting | bytes 3276800 | tf_op jit(solution)/shard_map/reshape | solution.py:73
  108.4 3.9 %copy.56 = bf16[32,2,2,2,10,320]{5,4,3,2,1,0:T(8,128)(2,1)} copy(bf16[32,2,2,2,10,320]{5,2,4,1,0,3:T(2,128)(2,1)} %bitcast.30) | data formatting | bytes 3276800 | tf_op jit(solution)/shard_map/reshape | solution.py:76
  112.3 6.0 %all-to-all-start.1 = ((bf16[256,10,320]{2,1,0:T(8,128)(2,1)}), bf16[256,10,320]{2,1,0:T(8,128)(2,1)}, u32[]{:S(2)}, u32[]{:S(2)}) async-start(bf16[256,10,320]{2,1,0:T(8,128)(2,1)} %bitcast.27), calls=%async_computation.1 | async-start | bytes 6291456 | tf_op jit(solution)/shard_map/all_to_all | solution.py:16
  118.3 5.3 %multiply_add_fusion = f32[2,640,640]{2,1,0:T(8,128)} fusion(f32[2,640,640]{2,1,0:T(8,128)} %param.12, bf16[2,640,640]{2,1,0:T(8,128)(2,1)S(1)} %reshape.43), kind=kOutput, calls=%fused_computation.6 | convolution fusion | flops 1051033600 | bytes 8192000 | tf_op jit(solution)/shard_map/kji,kjl->kil/dot_general | solution.py:24
  123.6 34.9 %all-to-all-done.1 = bf16[256,10,320]{2,1,0:T(8,128)(2,1)} async-done(((bf16[256,10,320]{2,1,0:T(8,128)(2,1)}), bf16[256,10,320]{2,1,0:T(8,128)(2,1)}, u32[]{:S(2)}, u32[]{:S(2)}) %all-to-all-start.1) | async-done | bytes 1638432 | tf_op jit(solution)/shard_map/all_to_all | solution.py:16
  158.5 3.7 %gather_fusion = bf16[96,10,320]{2,1,0:T(8,128)(2,1)} fusion(bf16[256,10,320]{2,1,0:T(8,128)(2,1)} %all-to-all-done.1, s32[1024]{0:T(1024)S(1)} %pad_clamp_fusion), kind=kCustom, calls=%fused_computation | custom fusion | bytes 1229184 | tf_op jit(solution)/shard_map/gather | solution.py:78
  162.2 1.4 fusion.6
  163.6 0.0 copy-start.3
  163.6 1.5 broadcast_select_fusion.1
  165.1 0.1 copy.73
  165.2 1.0 collective-permute-start.1
  166.2 0.0 copy-done.3
  166.2 3.5 %multiply_add_fusion.1 = f32[2,640,640]{2,1,0:T(8,128)} fusion(f32[2,640,640]{2,1,0:T(8,128)S(1)} %copy-done.3, bf16[2,640,640]{2,1,0:T(8,128)(2,1)S(1)} %reshape.43), kind=kOutput, calls=%fused_computation.7 | convolution fusion | flops 1051033600 | bytes 8192000 | tf_op jit(solution)/shard_map/kij,klj->kil/dot_general | solution.py:21
  169.7 0.0 copy-start.1
  169.7 7.9 %collective-permute-done.1 = bf16[48,10,320]{2,0,1:T(8,128)(2,1)S(1)} collective-permute-done((bf16[48,10,320]{2,0,1:T(8,128)(2,1)S(1)}, bf16[48,10,320]{2,0,1:T(8,128)(2,1)S(1)}, u32[]{:S(2)}, u32[]{:S(2)}) %collective-permute-start.1) | collective-permute-done | bytes 307232 | tf_op jit(solution)/shard_map/ppermute | solution.py:81
  177.6 0.1 bitcast_select_fusion.1
  177.7 0.0 copy-start.2
  177.7 0.7 copy-done.2
  178.4 0.0 copy-done.1
  178.4 0.3 multiply_reduce_fusion.1
  178.8 14.7 %psum.7 = f32[48,20]{0,1:T(8,128)S(1)} all-reduce(f32[48,20]{0,1:T(8,128)S(1)} %multiply_reduce_fusion.1), channel_id=1, replica_groups=mesh['shard'=32,'tensor'=4] {'tensor'}, use_global_device_ids=true, to_apply=%region_4.5 | all-reduce | flops 960 | bytes 7680 | tf_op jit(solution)/shard_map/psum | solution.py:86
  193.5 2.4 %fusion.4 = f32[48,20,320]{2,0,1:T(8,128)} fusion(f32[48,20,320]{2,0,1:T(8,128)S(1)} %copy-done.1, f32[48,20]{0,1:T(8,128)S(1)} %add_rsqrt_fusion, bf16[48,10,320]{2,0,1:T(8,128)(2,1)} %copy-done.2, bf16[48,10,320]{2,0,1:T(8,128)(2,1)S(1)} %get-tuple-element.14), kind=kLoop, calls=%fused_computation.18 | loop fusion | flops 1536000 | bytes 3075840 | tf_op jit(solution)/shard_map/mul | solution.py:87
  (3 shorter events, 0.0 us)
Async XLA Ops:
  0.6 92.7 %copy-start = (bf16[2,640,640]{2,1,0:T(8,128)(2,1)S(1)}, bf16[2,640,640]{2,1,0:T(8,128)(2,1)}, u32[]{:S(2)}) copy-start(bf16[2,640,640]{2,1,0:T(8,128)(2,1)} %param.14) | copy-start | bytes 4915204
  1.8 12.0 %collective-permute-start = (bf16[48,10,320]{2,0,1:T(8,128)(2,1)S(1)}, bf16[48,10,320]{2,0,1:T(8,128)(2,1)S(1)}, u32[]{:S(2)}, u32[]{:S(2)}) collective-permute-start(bf16[48,10,320]{2,0,1:T(8,128)(2,1)S(1)} %constant_dynamic-slice_fusion), channel_id=1, source_target_pairs={{0,2},{1,3},{2,0},{3,1},{4,6},{5,7},{6,4},{7,5},{8,10},{9,11},{10,... | collective-permute-start | bytes 921608 | tf_op jit(solution)/shard_map/ppermute | solution.py:63
  112.3 46.2 %all-to-all-start.1 = ((bf16[256,10,320]{2,1,0:T(8,128)(2,1)}), bf16[256,10,320]{2,1,0:T(8,128)(2,1)}, u32[]{:S(2)}, u32[]{:S(2)}) async-start(bf16[256,10,320]{2,1,0:T(8,128)(2,1)} %bitcast.27), calls=%async_computation.1 | async-start | bytes 6291456 | tf_op jit(solution)/shard_map/all_to_all | solution.py:16
  163.6 2.7 %copy-start.3 = (f32[2,640,640]{2,1,0:T(8,128)S(1)}, f32[2,640,640]{2,1,0:T(8,128)}, u32[]{:S(2)}) copy-start(f32[2,640,640]{2,1,0:T(8,128)} %param.11) | copy-start | bytes 9830404
  165.2 12.4 %collective-permute-start.1 = (bf16[48,10,320]{2,0,1:T(8,128)(2,1)S(1)}, bf16[48,10,320]{2,0,1:T(8,128)(2,1)S(1)}, u32[]{:S(2)}, u32[]{:S(2)}) collective-permute-start(bf16[48,10,320]{2,0,1:T(8,128)(2,1)S(1)} %bitcast.33), channel_id=1, source_target_pairs={{0,2},{1,3},{2,0},{3,1},{4,6},{5,7},{6,4},{7,5},{8,10},{9,11},{10,... | collective-permute-start | bytes 921608 | tf_op jit(solution)/shard_map/ppermute | solution.py:81
  169.7 8.8 %copy-start.1 = (f32[48,20,320]{2,0,1:T(8,128)S(1)}, f32[48,20,320]{2,0,1:T(8,128)}, u32[]{:S(2)}) copy-start(f32[48,20,320]{2,0,1:T(8,128)} %param.8) | copy-start | bytes 3686404
  177.7 0.7 copy-start.2

commit v2 on v1

--- a/solution.py
+++ b/solution.py
@@ -8,13 +8,16 @@
 
 
 def route_out(outgoing):
-    arrived = lax.all_to_all(outgoing, ("shard", "tensor"), split_axis=0, concat_axis=0, tiled=True)
-    return arrived
+    n_shard = lax.axis_size("shard")
+    n_tensor = lax.axis_size("tensor")
+    staged = outgoing.reshape((n_shard, n_tensor, -1) + outgoing.shape[1:])
+    staged = lax.all_to_all(staged, "shard", split_axis=0, concat_axis=0, tiled=True)
+    arrived = lax.all_to_all(staged, "tensor", split_axis=1, concat_axis=1, tiled=True)
+    return arrived.reshape(outgoing.shape)
 
 
 def route_back(outgoing):
-    arrived = lax.all_to_all(outgoing, ("shard", "tensor"), split_axis=0, concat_axis=0, tiled=True)
-    return arrived
+    return route_out(outgoing)
 
 
 def refresh(block_grads, left_stats, right_stats):

time: 197 us -> 230 us (1.17)
  blocking collectives: 66.6 us -> 111 us
  waiting for transfers between devices: 50.7 us -> 35.3 us
  local copies, waits for them, and re-layouts: 37.3 us -> 43.9 us
    all_to_all x1 -> x3, blocking collectives: 51.9 us -> 95.6 us  [the longest x2 66.1 us: route_out(): lax.all_to_all(staged, 'shard', split_axis=0, concat_axis=0, tiled=True)]
    all_to_all x1, waiting for transfers between devices: 34.9 us -> 20.2 us  [route_out(): lax.all_to_all(staged, 'tensor', split_axis=1, concat_axis=1, tiled=True)]
    all_to_all x0 -> x3, local copies, waits for them, and re-layouts: none -> 4.11 us  [the longest x2 3.78 us: route_out(): lax.all_to_all(staged, 'shard', split_axis=0, concat_axis=0, tiled=True)]
    reshape x1 -> x2, local copies, waits for them, and re-layouts: 3.94 us -> 7.56 us  [the longest x1 4.15 us: route_out(): return arrived.reshape(outgoing.shape)]
    reshape x1 -> x2, local copies, waits for them, and re-layouts: 5.29 us -> 4.41 us  [body(): delta.reshape(slots, n_shard, col_blocks, half, per_block, shard_cols)]
  transfers between devices with their start and end apart: 3 -> 3, of which waited for: 3 -> 3; matrix products, arithmetic and copies ran while one was open for 5% -> 4% of each run, Pallas kernels for 0% -> 0%
where the time goes in v2:
time: 230 us; the launch traced here: 228 us
  blocking collectives  111 us (48%)
  local copies, waits for them, and re-layouts  43.9 us (19%)
  waiting for transfers between devices  35.3 us (15%)
  matrix products  15.1 us (7%)
  other arithmetic  14 us (6%)
  starting transfers between devices  8.44 us (4%)
    all_to_all x2, blocking collectives, route_out(): lax.all_to_all(staged, 'shard', split_axis=0, concat_axis=0, tiled=True)  66.1 us
    all_to_all x1, blocking collectives, route_out(): lax.all_to_all(staged, 'tensor', split_axis=1, concat_axis=1, tiled=True)  29.4 us
    all_to_all x1, waiting for transfers between devices, route_out(): lax.all_to_all(staged, 'tensor', split_axis=1, concat_axis=1, tiled=True)  20.2 us
    psum x1, blocking collectives, body(): squares = lax.psum(jnp.sum(updated * updated, axis=2), 'tensor')  15.4 us
    scatter x1, local copies, waits for them, and re-layouts, body(): jnp.zeros((total_slots, half, shard_cols), jnp.bfloat16).at[owner_slot]  11.8 us
    ppermute x1, waiting for transfers between devices, body(): got = lax.ppermute(give, 'tensor', partner)  7.93 us
    ppermute x1, waiting for transfers between devices, body(): other_back = lax.ppermute(other_part, 'tensor', partner)  7.19 us
    dot_general x1, matrix products, direction(): jnp.einsum('kij,kjl->kil', half, right_root, preferred_element_type=jnp.f...  6.34 us
  transfers between devices with their start and end apart: 3, of which 3 were waited for; matrix products, arithmetic and copies ran while one was open for 4% of the time, Pallas kernels for 0%

profile of v2, /device:TPU:0, one launch (start us, length us, event | category | flops | bytes accessed | tf_op | source)
XLA Modules:
  0.0 228.4 jit_solution(14755460040944215261)
XLA Ops:
  0.6 0.0 copy-start
  0.7 1.1 constant_dynamic-slice_fusion
  1.8 3.4 %collective-permute-start = (bf16[48,10,320]{2,0,1:T(8,128)(2,1)S(1)}, bf16[48,10,320]{2,0,1:T(8,128)(2,1)S(1)}, u32[]{:S(2)}, u32[]{:S(2)}) collective-permute-start(bf16[48,10,320]{2,0,1:T(8,128)(2,1)S(1)} %constant_dynamic-slice_fusion), channel_id=1, source_target_pairs={{0,2},{1,3},{2,0},{3,1},{4,6},{5,7},{6,4},{7,5},{8,10},{9,11},{10,... | collective-permute-start | bytes 921608 | tf_op jit(solution)/shard_map/ppermute | solution.py:66
  5.2 0.7 compare_select_fusion
  5.9 7.9 %collective-permute-done = bf16[48,10,320]{2,0,1:T(8,128)(2,1)S(1)} collective-permute-done((bf16[48,10,320]{2,0,1:T(8,128)(2,1)S(1)}, bf16[48,10,320]{2,0,1:T(8,128)(2,1)S(1)}, u32[]{:S(2)}, u32[]{:S(2)}) %collective-permute-start) | collective-permute-done | bytes 307232 | tf_op jit(solution)/shard_map/ppermute | solution.py:66
  13.8 1.1 select_bitcast_fusion.1
  14.9 0.1 pad_maximum_fusion
  15.0 0.2 copy.88
  15.2 1.9 broadcast_in_dim.4
  17.2 11.8 %scatter_fusion = bf16[256,10,320]{2,1,0:T(8,128)(2,1)} fusion(bf16[256,10,320]{2,1,0:T(8,128)(2,1)} %broadcast_in_dim.4, s32[96]{0:T(128)S(1)} %compare_select_fusion, bf16[96,10,320]{2,1,0:T(8,128)(2,1)S(1)} %bitcast.32), kind=kCustom, calls=%fused_computation.1 | custom fusion | bytes 1843584 | tf_op jit(solution)/shard_map/scatter | solution.py:70
  29.0 3.4 %copy.72 = bf16[32,4,2,10,320]{4,2,1,3,0:T(2,128)(2,1)S(1)} copy(bf16[32,4,2,10,320]{4,3,2,1,0:T(8,128)(2,1)} %bitcast.27) | data formatting | bytes 3276800 | tf_op jit(solution)/shard_map/reshape | solution.py:13
  32.4 35.1 %all_to_all.20 = bf16[32,4,2,10,320]{4,2,1,3,0:T(2,128)(2,1)S(1)} all-to-all(bf16[32,4,2,10,320]{4,2,1,3,0:T(2,128)(2,1)S(1)} %copy.72), channel_id=1, replica_groups=mesh['shard'=32,'tensor'=4] {'shard'}, dimensions={0} | all-to-all | bytes 3276800 | tf_op jit(solution)/shard_map/all_to_all | solution.py:14
  67.5 2.1 copy.73
  69.6 29.4 %all_to_all.21 = bf16[32,4,2,10,320]{4,2,0,3,1:T(2,128)(2,1)S(1)} all-to-all(bf16[32,4,2,10,320]{4,2,0,3,1:T(2,128)(2,1)S(1)} %copy.73), channel_id=1, replica_groups=mesh['shard'=32,'tensor'=4] {'tensor'}, dimensions={1} | all-to-all | bytes 3276800 | tf_op jit(solution)/shard_map/all_to_all | solution.py:15
  99.0 0.3 copy.74
  99.4 3.3 %copy.75 = bf16[2,32,2,10,2,320]{5,4,3,2,1,0:T(2,128)(2,1)} copy(bf16[2,32,2,10,2,320]{5,1,3,0,4,2:T(8,128)(2,1)S(1)} %bitcast.28) | data formatting | bytes 3276800 | tf_op jit(solution)/shard_map/transpose | solution.py:73
  102.7 4.2 %reshape.43 = bf16[2,640,640]{2,1,0:T(8,128)(2,1)S(1)} reshape(bf16[2,32,2,10,2,320]{5,4,3,2,1,0:T(2,128)(2,1)} %copy.75) | data formatting | bytes 3276800 | tf_op jit(solution)/shard_map/reshape | solution.py:73
  106.9 5.4 %fusion.2 = (f32[2]{0:T(128)S(1)}, f32[2,640,640]{2,1,0:T(8,128)}) fusion(bf16[2,640,640]{2,1,0:T(8,128)(2,1)S(1)} %reshape.43, f32[2,640,640]{2,1,0:T(8,128)} %param.15), kind=kLoop, calls=%fused_computation.10 | loop fusion | flops 7372798 | bytes 8192008 | tf_op jit(solution)/shard_map/reduce_sum | solution.py:43
  112.3 0.0 copy-done
  112.3 6.3 %multiply_reduce_fusion = (f32[2]{0:T(128)S(1)}, f32[2,640,640]{2,1,0:T(8,128)}) fusion(bf16[2,640,640]{2,1,0:T(8,128)(2,1)S(1)} %copy-done, bf16[2,640,640]{2,1,0:T(8,128)(2,1)S(1)} %reshape.43, bf16[2,640,640]{2,1,0:T(8,128)(2,1)} %param.13), kind=kOutput, calls=%fused_computation.9 | convolution fusion | flops 2099609600 | bytes 8192008 | tf_op jit(solution)/shard_map/kij,kjl->kil/dot_general | solution.py:39
  118.6 2.2 multiply_convert_fusion
  120.9 2.6 %reshape.44 = bf16[2,32,2,10,2,320]{5,4,3,2,1,0:T(2,128)(2,1)} reshape(bf16[2,640,640]{2,1,0:T(8,128)(2,1)S(1)} %multiply_convert_fusion) | data formatting | bytes 3276800 | tf_op jit(solution)/shard_map/reshape | solution.py:76
  123.4 1.8 copy.78
  125.3 1.5 copy.79
  126.8 31.0 %all_to_all.22 = bf16[32,4,2,10,320]{4,1,3,2,0:T(4,128)(2,1)S(1)} all-to-all(bf16[32,4,2,10,320]{4,1,3,2,0:T(4,128)(2,1)S(1)} %copy.79), channel_id=1, replica_groups=mesh['shard'=32,'tensor'=4] {'shard'}, dimensions={0} | all-to-all | bytes 3276800 | tf_op jit(solution)/shard_map/all_to_all | solution.py:14
  157.8 1.7 copy.80
  159.5 4.4 %all-to-all-start.3 = ((bf16[32,4,2,10,320]{4,0,3,2,1:T(8,128)(2,1)}), bf16[32,4,2,10,320]{4,0,3,2,1:T(8,128)(2,1)}, u32[]{:S(2)}, u32[]{:S(2)}) async-start(bf16[32,4,2,10,320]{4,0,3,2,1:T(8,128)(2,1)} %copy.80), calls=%async_computation.3 | async-start | bytes 3932160 | tf_op jit(solution)/shard_map/all_to_all | solution.py:15
  164.0 5.3 %multiply_add_fusion = f32[2,640,640]{2,1,0:T(8,128)} fusion(f32[2,640,640]{2,1,0:T(8,128)} %param.12, bf16[2,640,640]{2,1,0:T(8,128)(2,1)S(1)} %reshape.43), kind=kOutput, calls=%fused_computation.6 | convolution fusion | flops 1051033600 | bytes 8192000 | tf_op jit(solution)/shard_map/kji,kjl->kil/dot_general | solution.py:27
  169.3 20.2 %all-to-all-done.3 = bf16[32,4,2,10,320]{4,0,3,2,1:T(8,128)(2,1)} async-done(((bf16[32,4,2,10,320]{4,0,3,2,1:T(8,128)(2,1)}), bf16[32,4,2,10,320]{4,0,3,2,1:T(8,128)(2,1)}, u32[]{:S(2)}, u32[]{:S(2)}) %all-to-all-start.3) | async-done | bytes 1638432 | tf_op jit(solution)/shard_map/all_to_all | solution.py:15
  189.5 4.1 %copy.91 = bf16[32,4,2,10,320]{4,3,2,1,0:T(8,128)(2,1)} copy(bf16[32,4,2,10,320]{4,0,3,2,1:T(8,128)(2,1)} %all-to-all-done.3) | data formatting | bytes 3276800 | tf_op jit(solution)/shard_map/reshape | solution.py:16
  193.6 2.7 %gather_fusion = bf16[96,10,320]{2,1,0:T(8,128)(2,1)S(1)} fusion(bf16[256,10,320]{2,1,0:T(8,128)(2,1)} %bitcast.30, s32[1024]{0:T(1024)S(1)} %pad_clamp_fusion), kind=kCustom, calls=%fused_computation | custom fusion | bytes 1229184 | tf_op jit(solution)/shard_map/gather | solution.py:81
  196.4 0.1 fusion.6
  196.5 0.0 copy-start.4
  196.5 1.5 broadcast_select_fusion.1
  198.0 0.1 copy.106
  198.1 0.6 collective-permute-start.1
  198.8 0.0 copy-done.4
  198.8 3.5 %multiply_add_fusion.1 = f32[2,640,640]{2,1,0:T(8,128)} fusion(f32[2,640,640]{2,1,0:T(8,128)S(1)} %copy-done.4, bf16[2,640,640]{2,1,0:T(8,128)(2,1)S(1)} %reshape.43), kind=kOutput, calls=%fused_computation.7 | convolution fusion | flops 1051033600 | bytes 8192000 | tf_op jit(solution)/shard_map/kij,klj->kil/dot_general | solution.py:24
  202.2 0.0 copy-start.2
  202.2 7.2 %collective-permute-done.1 = bf16[48,10,320]{2,0,1:T(8,128)(2,1)S(1)} collective-permute-done((bf16[48,10,320]{2,0,1:T(8,128)(2,1)S(1)}, bf16[48,10,320]{2,0,1:T(8,128)(2,1)S(1)}, u32[]{:S(2)}, u32[]{:S(2)}) %collective-permute-start.1) | collective-permute-done | bytes 307232 | tf_op jit(solution)/shard_map/ppermute | solution.py:84
  209.4 0.1 bitcast_select_fusion.1
  209.5 0.0 copy-start.3
  209.5 0.7 copy-done.3
  210.2 0.0 copy-done.2
  210.2 0.3 multiply_reduce_fusion.1
  210.6 15.4 %psum.7 = f32[48,20]{0,1:T(8,128)S(1)} all-reduce(f32[48,20]{0,1:T(8,128)S(1)} %multiply_reduce_fusion.1), channel_id=1, replica_groups=mesh['shard'=32,'tensor'=4] {'tensor'}, use_global_device_ids=true, to_apply=%region_4.5 | all-reduce | flops 960 | bytes 7680 | tf_op jit(solution)/shard_map/psum | solution.py:89
  226.0 2.4 %fusion.4 = f32[48,20,320]{2,0,1:T(8,128)} fusion(f32[48,20,320]{2,0,1:T(8,128)S(1)} %copy-done.2, f32[48,20]{0,1:T(8,128)S(1)} %add_rsqrt_fusion, bf16[48,10,320]{2,0,1:T(8,128)(2,1)} %copy-done.3, bf16[48,10,320]{2,0,1:T(8,128)(2,1)S(1)} %get-tuple-element.14), kind=kLoop, calls=%fused_computation.17 | loop fusion | flops 1536000 | bytes 3075840 | tf_op jit(solution)/shard_map/mul | solution.py:90
  228.4 0.0 copy-done.1
  (4 shorter events, 0.0 us)
Async XLA Ops:
  0.6 111.7 %copy-start = (bf16[2,640,640]{2,1,0:T(8,128)(2,1)S(1)}, bf16[2,640,640]{2,1,0:T(8,128)(2,1)}, u32[]{:S(2)}) copy-start(bf16[2,640,640]{2,1,0:T(8,128)(2,1)} %param.14) | copy-start | bytes 4915204
  1.8 12.0 %collective-permute-start = (bf16[48,10,320]{2,0,1:T(8,128)(2,1)S(1)}, bf16[48,10,320]{2,0,1:T(8,128)(2,1)S(1)}, u32[]{:S(2)}, u32[]{:S(2)}) collective-permute-start(bf16[48,10,320]{2,0,1:T(8,128)(2,1)S(1)} %constant_dynamic-slice_fusion), channel_id=1, source_target_pairs={{0,2},{1,3},{2,0},{3,1},{4,6},{5,7},{6,4},{7,5},{8,10},{9,11},{10,... | collective-permute-start | bytes 921608 | tf_op jit(solution)/shard_map/ppermute | solution.py:66
  159.5 29.9 %all-to-all-start.3 = ((bf16[32,4,2,10,320]{4,0,3,2,1:T(8,128)(2,1)}), bf16[32,4,2,10,320]{4,0,3,2,1:T(8,128)(2,1)}, u32[]{:S(2)}, u32[]{:S(2)}) async-start(bf16[32,4,2,10,320]{4,0,3,2,1:T(8,128)(2,1)} %copy.80), calls=%async_computation.3 | async-start | bytes 3932160 | tf_op jit(solution)/shard_map/all_to_all | solution.py:15
  196.5 2.2 copy-start.4
  198.1 11.3 %collective-permute-start.1 = (bf16[48,10,320]{2,0,1:T(8,128)(2,1)S(1)}, bf16[48,10,320]{2,0,1:T(8,128)(2,1)S(1)}, u32[]{:S(2)}, u32[]{:S(2)}) collective-permute-start(bf16[48,10,320]{2,0,1:T(8,128)(2,1)S(1)} %bitcast.33), channel_id=1, source_target_pairs={{0,2},{1,3},{2,0},{3,1},{4,6},{5,7},{6,4},{7,5},{8,10},{9,11},{10,... | collective-permute-start | bytes 921608 | tf_op jit(solution)/shard_map/ppermute | solution.py:84
  202.2 8.0 %copy-start.2 = (f32[48,20,320]{2,0,1:T(8,128)S(1)}, f32[48,20,320]{2,0,1:T(8,128)}, u32[]{:S(2)}) copy-start(f32[48,20,320]{2,0,1:T(8,128)} %param.8) | copy-start | bytes 3686404
  209.5 0.7 copy-start.3
  210.2 18.2 %copy-start.1 = (bf16[2,640,640]{2,1,0:T(8,128)(2,1)S(1)}, bf16[2,640,640]{2,1,0:T(8,128)(2,1)}, u32[]{:S(2)}) copy-start(bf16[2,640,640]{2,1,0:T(8,128)(2,1)} %param.14) | copy-start | bytes 4915204

commit v3 on v1

--- a/solution.py
+++ b/solution.py
@@ -83,7 +83,12 @@
     bottom = jnp.where(mine_col == 0, other_back, own_part)
     my_delta = jnp.concatenate([top, bottom], axis=1)
     updated = weights - step_size * my_delta.astype(jnp.float32)
-    squares = lax.psum(jnp.sum(updated * updated, axis=2), "tensor")
+    squares = jnp.sum(updated * updated, axis=2)
+    step = 1
+    while step < n_tensor:
+        pairs = [(i, i ^ step) for i in range(n_tensor)]
+        squares = squares + lax.ppermute(squares, "tensor", pairs)
+        step *= 2
     new_weights = updated * lax.rsqrt(squares / width + 1e-06)[:, :, None]
     return (new_weights, new_left, new_right, new_moment)
 

time: 197 us -> 191 us (0.970)
  blocking collectives: 66.6 us -> 51.9 us
  waiting for transfers between devices: 50.7 us -> 60.9 us
    psum x1 -> x0, blocking collectives: 14.7 us -> none  [body(): squares = lax.psum(jnp.sum(updated * updated, axis=2), 'tensor')]
    all_to_all x1, waiting for transfers between devices: 34.9 us -> 40.2 us  [route_back(): lax.all_to_all(outgoing, ('shard', 'tensor'), split_axis=0, concat_axis=0...]
    ppermute x1, waiting for transfers between devices: 7.92 us -> 11.4 us  [body(): other_back = lax.ppermute(other_part, 'tensor', partner)]
  transfers between devices with their start and end apart: 3 -> 5, of which waited for: 3 -> 4; matrix products, arithmetic and copies ran while one was open for 5% -> 4% of each run, Pallas kernels for 0% -> 0%
where the time goes in v3:
time: 191 us; the launch traced here: 190 us
  waiting for transfers between devices  60.9 us (32%)
  blocking collectives  51.9 us (27%)
  local copies, waits for them, and re-layouts  37.3 us (20%)
  other arithmetic  14.2 us (7%)
  matrix products  13.3 us (7%)
  starting transfers between devices  11.4 us (6%)
    all_to_all x1, blocking collectives, route_out(): lax.all_to_all(outgoing, ('shard', 'tensor'), split_axis=0, concat_axis=0...  51.9 us
    all_to_all x1, waiting for transfers between devices, route_back(): lax.all_to_all(outgoing, ('shard', 'tensor'), split_axis=0, concat_axis=0...  40.2 us
    scatter x1, local copies, waits for them, and re-layouts, body(): jnp.zeros((total_slots, half, shard_cols), jnp.bfloat16).at[owner_slot]  11.8 us
    ppermute x1, waiting for transfers between devices, body(): other_back = lax.ppermute(other_part, 'tensor', partner)  11.4 us
    ppermute x1, waiting for transfers between devices, body(): got = lax.ppermute(give, 'tensor', partner)  7.93 us
    dot_general x1, matrix products, direction(): jnp.einsum('kij,kjl->kil', half, right_root, preferred_element_type=jnp.f...  6.34 us
    all_to_all x1, starting transfers between devices, route_back(): lax.all_to_all(outgoing, ('shard', 'tensor'), split_axis=0, concat_axis=0...  5.96 us
    reduce_sum x1, other arithmetic, direction(): jnp.mean(adam * adam, axis=(1, 2))  5.42 us
  transfers between devices with their start and end apart: 5, of which 4 were waited for; matrix products, arithmetic and copies ran while one was open for 4% of the time, Pallas kernels for 0%

profile of v3, /device:TPU:0, one launch (start us, length us, event | category | flops | bytes accessed | tf_op | source)
XLA Modules:
  0.0 189.7 jit_solution(15357902775250512763)
XLA Ops:
  0.6 0.0 copy-start
  0.7 1.1 constant_dynamic-slice_fusion
  1.8 3.4 %collective-permute-start = (bf16[48,10,320]{2,0,1:T(8,128)(2,1)S(1)}, bf16[48,10,320]{2,0,1:T(8,128)(2,1)S(1)}, u32[]{:S(2)}, u32[]{:S(2)}) collective-permute-start(bf16[48,10,320]{2,0,1:T(8,128)(2,1)S(1)} %constant_dynamic-slice_fusion), channel_id=1, source_target_pairs={{0,2},{1,3},{2,0},{3,1},{4,6},{5,7},{6,4},{7,5},{8,10},{9,11},{10,... | collective-permute-start | bytes 921608 | tf_op jit(solution)/shard_map/ppermute | solution.py:63
  5.2 0.7 compare_select_fusion
  5.9 7.9 %collective-permute-done = bf16[48,10,320]{2,0,1:T(8,128)(2,1)S(1)} collective-permute-done((bf16[48,10,320]{2,0,1:T(8,128)(2,1)S(1)}, bf16[48,10,320]{2,0,1:T(8,128)(2,1)S(1)}, u32[]{:S(2)}, u32[]{:S(2)}) %collective-permute-start) | collective-permute-done | bytes 307232 | tf_op jit(solution)/shard_map/ppermute | solution.py:63
  13.8 1.1 select_bitcast_fusion.1
  14.9 0.1 pad_maximum_fusion
  15.0 0.2 copy.53
  15.2 1.9 %broadcast_in_dim.4 = bf16[256,10,320]{2,1,0:T(8,128)(2,1)} broadcast(bf16[]{:T(256)} %constant.20.clone.1), dimensions={} | broadcast | bytes 1638402 | tf_op jit(solution)/shard_map/broadcast_in_dim | solution.py:67
  17.2 11.8 %scatter_fusion = bf16[256,10,320]{2,1,0:T(8,128)(2,1)} fusion(bf16[256,10,320]{2,1,0:T(8,128)(2,1)} %broadcast_in_dim.4, s32[96]{0:T(128)S(1)} %compare_select_fusion, bf16[96,10,320]{2,1,0:T(8,128)(2,1)S(1)} %bitcast.32), kind=kCustom, calls=%fused_computation.1 | custom fusion | bytes 1843584 | tf_op jit(solution)/shard_map/scatter | solution.py:67
  29.0 51.9 %all_to_all.10 = bf16[256,10,320]{2,1,0:T(8,128)(2,1)S(1)} all-to-all(bf16[256,10,320]{2,1,0:T(8,128)(2,1)} %scatter_fusion), channel_id=1, replica_groups=mesh['shard'=32,'tensor'=4] {'shard','tensor'}, dimensions={0} | all-to-all | bytes 3276800 | tf_op jit(solution)/shard_map/all_to_all | solution.py:11
  80.9 2.8 %copy.72 = bf16[32,2,2,2,10,320]{5,2,4,1,0,3:T(2,128)(2,1)} copy(bf16[32,2,2,2,10,320]{5,4,3,2,1,0:T(8,128)(2,1)S(1)} %bitcast.28) | data formatting | bytes 3276800 | tf_op jit(solution)/shard_map/transpose | solution.py:70
  83.7 4.2 %reshape.43 = bf16[2,640,640]{2,1,0:T(8,128)(2,1)S(1)} reshape(bf16[2,32,2,10,2,320]{5,4,3,2,1,0:T(2,128)(2,1)} %bitcast.29) | data formatting | bytes 3276800 | tf_op jit(solution)/shard_map/reshape | solution.py:70
  87.9 5.4 %fusion.2 = (f32[2]{0:T(128)S(1)}, f32[2,640,640]{2,1,0:T(8,128)}) fusion(bf16[2,640,640]{2,1,0:T(8,128)(2,1)S(1)} %reshape.43, f32[2,640,640]{2,1,0:T(8,128)} %param.15), kind=kLoop, calls=%fused_computation.10 | loop fusion | flops 7372798 | bytes 8192008 | tf_op jit(solution)/shard_map/reduce_sum | solution.py:40
  93.3 0.0 copy-done
  93.3 6.3 %multiply_reduce_fusion = (f32[2]{0:T(128)S(1)}, f32[2,640,640]{2,1,0:T(8,128)}) fusion(bf16[2,640,640]{2,1,0:T(8,128)(2,1)S(1)} %copy-done, bf16[2,640,640]{2,1,0:T(8,128)(2,1)S(1)} %reshape.43, bf16[2,640,640]{2,1,0:T(8,128)(2,1)} %param.13), kind=kOutput, calls=%fused_computation.9 | convolution fusion | flops 2099609600 | bytes 8192008 | tf_op jit(solution)/shard_map/kij,kjl->kil/dot_general | solution.py:36
  99.7 3.4 %multiply_convert_fusion = bf16[2,640,640]{2,1,0:T(8,128)(2,1)} fusion(f32[2,640,640]{2,1,0:T(8,128)} %get-tuple-element.19, f32[2]{0:T(128)S(1)} %rsqrt_multiply_fusion), kind=kLoop, calls=%fused_computation.8 | loop fusion | flops 1638400 | bytes 4915208 | tf_op jit(solution)/shard_map/convert_element_type | solution.py:43
  103.1 5.3 %reshape.44 = bf16[2,32,2,10,2,320]{5,4,3,2,1,0:T(2,128)(2,1)} reshape(bf16[2,640,640]{2,1,0:T(8,128)(2,1)} %multiply_convert_fusion) | data formatting | bytes 3276800 | tf_op jit(solution)/shard_map/reshape | solution.py:73
  108.4 3.9 %copy.56 = bf16[32,2,2,2,10,320]{5,4,3,2,1,0:T(8,128)(2,1)} copy(bf16[32,2,2,2,10,320]{5,2,4,1,0,3:T(2,128)(2,1)} %bitcast.30) | data formatting | bytes 3276800 | tf_op jit(solution)/shard_map/reshape | solution.py:76
  112.3 6.0 %all-to-all-start.1 = ((bf16[256,10,320]{2,1,0:T(8,128)(2,1)}), bf16[256,10,320]{2,1,0:T(8,128)(2,1)}, u32[]{:S(2)}, u32[]{:S(2)}) async-start(bf16[256,10,320]{2,1,0:T(8,128)(2,1)} %bitcast.27), calls=%async_computation.1 | async-start | bytes 6291456 | tf_op jit(solution)/shard_map/all_to_all | solution.py:16
  118.3 40.2 %all-to-all-done.1 = bf16[256,10,320]{2,1,0:T(8,128)(2,1)} async-done(((bf16[256,10,320]{2,1,0:T(8,128)(2,1)}), bf16[256,10,320]{2,1,0:T(8,128)(2,1)}, u32[]{:S(2)}, u32[]{:S(2)}) %all-to-all-start.1) | async-done | bytes 1638432 | tf_op jit(solution)/shard_map/all_to_all | solution.py:16
  158.5 3.7 %gather_fusion = bf16[96,10,320]{2,1,0:T(8,128)(2,1)} fusion(bf16[256,10,320]{2,1,0:T(8,128)(2,1)} %all-to-all-done.1, s32[1024]{0:T(1024)S(1)} %pad_clamp_fusion), kind=kCustom, calls=%fused_computation | custom fusion | bytes 1229184 | tf_op jit(solution)/shard_map/gather | solution.py:78
  162.2 1.4 fusion.6
  163.6 1.5 broadcast_select_fusion.1
  165.1 0.0 copy-start.1
  165.1 0.1 copy.73
  165.2 1.0 collective-permute-start.1
  166.2 11.4 %collective-permute-done.1 = bf16[48,10,320]{2,0,1:T(8,128)(2,1)S(1)} collective-permute-done((bf16[48,10,320]{2,0,1:T(8,128)(2,1)S(1)}, bf16[48,10,320]{2,0,1:T(8,128)(2,1)S(1)}, u32[]{:S(2)}, u32[]{:S(2)}) %collective-permute-start.1) | collective-permute-done | bytes 307232 | tf_op jit(solution)/shard_map/ppermute | solution.py:81
  177.6 0.0 copy-start.2
  177.6 0.1 bitcast_select_fusion.1
  177.7 0.0 copy-done.1
  177.7 0.4 multiply_reduce_fusion.1
  178.1 0.7 collective-permute-start.2
  178.8 0.7 copy-done.2
  179.5 0.0 copy-start.3
  179.5 3.5 %multiply_add_fusion = f32[2,640,640]{2,1,0:T(8,128)} fusion(f32[2,640,640]{2,1,0:T(8,128)S(1)} %copy-done.2, bf16[2,640,640]{2,1,0:T(8,128)(2,1)S(1)} %reshape.43), kind=kOutput, calls=%fused_computation.6 | convolution fusion | flops 1051033600 | bytes 8192000 | tf_op jit(solution)/shard_map/kji,kjl->kil/dot_general | solution.py:24
  183.0 0.0 collective-permute-done.2
  183.0 0.3 collective-permute-start.3
  183.3 0.0 copy-done.3
  183.3 3.5 %multiply_add_fusion.1 = f32[2,640,640]{2,1,0:T(8,128)} fusion(f32[2,640,640]{2,1,0:T(8,128)S(1)} %copy-done.3, bf16[2,640,640]{2,1,0:T(8,128)(2,1)S(1)} %reshape.43), kind=kOutput, calls=%fused_computation.7 | convolution fusion | flops 1051033600 | bytes 8192000 | tf_op jit(solution)/shard_map/kij,klj->kil/dot_general | solution.py:21
  186.8 1.5 collective-permute-done.3
  188.2 1.5 fusion.4
  (4 shorter events, 0.0 us)
Async XLA Ops:
  0.6 92.7 %copy-start = (bf16[2,640,640]{2,1,0:T(8,128)(2,1)S(1)}, bf16[2,640,640]{2,1,0:T(8,128)(2,1)}, u32[]{:S(2)}) copy-start(bf16[2,640,640]{2,1,0:T(8,128)(2,1)} %param.14) | copy-start | bytes 4915204
  1.8 12.0 %collective-permute-start = (bf16[48,10,320]{2,0,1:T(8,128)(2,1)S(1)}, bf16[48,10,320]{2,0,1:T(8,128)(2,1)S(1)}, u32[]{:S(2)}, u32[]{:S(2)}) collective-permute-start(bf16[48,10,320]{2,0,1:T(8,128)(2,1)S(1)} %constant_dynamic-slice_fusion), channel_id=1, source_target_pairs={{0,2},{1,3},{2,0},{3,1},{4,6},{5,7},{6,4},{7,5},{8,10},{9,11},{10,... | collective-permute-start | bytes 921608 | tf_op jit(solution)/shard_map/ppermute | solution.py:63
  112.3 46.2 %all-to-all-start.1 = ((bf16[256,10,320]{2,1,0:T(8,128)(2,1)}), bf16[256,10,320]{2,1,0:T(8,128)(2,1)}, u32[]{:S(2)}, u32[]{:S(2)}) async-start(bf16[256,10,320]{2,1,0:T(8,128)(2,1)} %bitcast.27), calls=%async_computation.1 | async-start | bytes 6291456 | tf_op jit(solution)/shard_map/all_to_all | solution.py:16
  165.1 12.6 %copy-start.1 = (f32[48,20,320]{2,0,1:T(8,128)S(1)}, f32[48,20,320]{2,0,1:T(8,128)}, u32[]{:S(2)}) copy-start(f32[48,20,320]{2,0,1:T(8,128)} %param.8) | copy-start | bytes 3686404
  165.2 12.4 %collective-permute-start.1 = (bf16[48,10,320]{2,0,1:T(8,128)(2,1)S(1)}, bf16[48,10,320]{2,0,1:T(8,128)(2,1)S(1)}, u32[]{:S(2)}, u32[]{:S(2)}) collective-permute-start(bf16[48,10,320]{2,0,1:T(8,128)(2,1)S(1)} %bitcast.33), channel_id=1, source_target_pairs={{0,2},{1,3},{2,0},{3,1},{4,6},{5,7},{6,4},{7,5},{8,10},{9,11},{10,... | collective-permute-start | bytes 921608 | tf_op jit(solution)/shard_map/ppermute | solution.py:81
  177.6 1.9 %copy-start.2 = (f32[2,640,640]{2,1,0:T(8,128)S(1)}, f32[2,640,640]{2,1,0:T(8,128)}, u32[]{:S(2)}) copy-start(f32[2,640,640]{2,1,0:T(8,128)} %param.12) | copy-start | bytes 9830404
  178.1 4.9 %collective-permute-start.2 = (f32[48,20]{0,1:T(8,128)S(1)}, f32[48,20]{0,1:T(8,128)S(1)}, u32[]{:S(2)}, u32[]{:S(2)}) collective-permute-start(f32[48,20]{0,1:T(8,128)S(1)} %multiply_reduce_fusion.1), channel_id=1, source_target_pairs={{0,1},{1,0},{2,3},{3,2},{4,5},{5,4},{6,7},{7,6},{8,9},{9,8},{10,11... | collective-permute-start | bytes 11528 | tf_op jit(solution)/shard_map/ppermute | solution.py:90
  179.5 3.8 %copy-start.3 = (f32[2,640,640]{2,1,0:T(8,128)S(1)}, f32[2,640,640]{2,1,0:T(8,128)}, u32[]{:S(2)}) copy-start(f32[2,640,640]{2,1,0:T(8,128)} %param.11) | copy-start | bytes 9830404
  183.0 5.2 %collective-permute-start.3 = (f32[48,20]{0,1:T(8,128)S(1)}, f32[48,20]{0,1:T(8,128)S(1)}, u32[]{:S(2)}, u32[]{:S(2)}) collective-permute-start(f32[48,20]{0,1:T(8,128)S(1)} %add.52), channel_id=1, source_target_pairs={{0,2},{1,3},{2,0},{3,1},{4,6},{5,7},{6,4},{7,5},{8,10},{9,11},{10,... | collective-permute-start | bytes 11528 | tf_op jit(solution)/shard_map/ppermute | solution.py:90

commit v4 on v3

--- a/solution.py
+++ b/solution.py
@@ -63,9 +63,17 @@
     got = lax.ppermute(give, "tensor", partner)
     first = jnp.where(mine_col == 0, keep, got)
     second = jnp.where(mine_col == 0, got, keep)
-    slabs = jnp.stack([first, second], axis=1).reshape(row_blocks * col_blocks, half, shard_cols)
-    outgoing = jnp.zeros((total_slots, half, shard_cols), jnp.bfloat16).at[owner_slot].set(slabs)
-    arrived = route_out(outgoing)
+    block_count = owner_slot.shape[0]
+    slab_size = half * shard_cols
+    chunk = slots * slab_size
+    lanes = 128 if chunk % 128 == 0 else chunk
+    slabs = jnp.stack([first, second], axis=1).reshape(row_blocks * col_blocks, slab_size)
+    slot_block = jnp.zeros((total_slots,), jnp.int32).at[owner_slot].set(
+        jnp.arange(block_count, dtype=jnp.int32)
+    )
+    slot_used = jnp.zeros((total_slots,), jnp.bool_).at[owner_slot].set(True)
+    outgoing = jnp.where(slot_used[:, None], slabs[slot_block], jnp.zeros((), jnp.bfloat16))
+    arrived = route_out(outgoing.reshape(owners, chunk // lanes, lanes))
     arrived = arrived.reshape(n_shard, col_blocks, per_block, slots, half, shard_cols)
     block_grads = arrived.transpose(3, 0, 1, 4, 2, 5).reshape(slots, order_size, order_size)
     new_left, new_right = refresh(block_grads, left_stats, right_stats)
@@ -73,8 +81,8 @@
     pieces = delta.reshape(slots, n_shard, col_blocks, half, per_block, shard_cols).transpose(
         1, 2, 4, 0, 3, 5
     )
-    sendback = pieces.reshape(total_slots, half, shard_cols)
-    returned = route_back(sendback)
+    sendback = pieces.reshape(owners, chunk // lanes, lanes)
+    returned = route_back(sendback).reshape(total_slots, slab_size)
     back = returned[owner_slot].reshape(row_blocks, col_blocks, half, shard_cols)
     own_part = jnp.where(mine_col == 0, back[:, 0], back[:, 1])
     other_part = jnp.where(mine_col == 0, back[:, 1], back[:, 0])

time: 191 us -> 166 us (0.87)
  waiting for transfers between devices: 60.9 us -> 44.3 us
  blocking collectives: 51.9 us -> 37.9 us
  local copies, waits for them, and re-layouts: 37.3 us -> 45 us
  other arithmetic: 14.2 us -> 11.9 us
    all_to_all x1, blocking collectives: 51.9 us -> 37.9 us  [route_out(): lax.all_to_all(outgoing, ('shard', 'tensor'), split_axis=0, concat_axis=0...]
    all_to_all x1, waiting for transfers between devices: 40.2 us -> 26.6 us  [route_back(): lax.all_to_all(outgoing, ('shard', 'tensor'), split_axis=0, concat_axis=0...]
    reshape x1 -> x4, local copies, waits for them, and re-layouts: 3.94 us -> 15.4 us  [the longest x1 5.93 us: body(): sendback = pieces.reshape(owners, chunk // lanes, lanes)]
    scatter x1 -> x2, local copies, waits for them, and re-layouts: 11.8 us -> 1.77 us  [the longest x1 0.9 us: body(): slot_used = jnp.zeros((total_slots,), jnp.bool_).at[owner_slot].set(True)]
    gather x0 -> x2, local copies, waits for them, and re-layouts: none -> 6.42 us  [body(): slabs[slot_block]]
    ppermute x1, waiting for transfers between devices: 7.93 us -> 5.69 us  [body(): got = lax.ppermute(give, 'tensor', partner)]
    gather x1, local copies, waits for them, and re-layouts: 3.71 us -> 1.78 us  [body(): returned[owner_slot].reshape(row_blocks, col_blocks, half, shard_cols)]
    reshape x1 -> x2, local copies, waits for them, and re-layouts: 5.29 us -> 6.51 us  [body(): delta.reshape(slots, n_shard, col_blocks, half, per_block, shard_cols)]
  transfers between devices with their start and end apart: 5 -> 5, of which waited for: 4 -> 4; matrix products, arithmetic and copies ran while one was open for 4% -> 6% of each run, Pallas kernels for 0% -> 0%
where the time goes in v4:
time: 166 us
  local copies, waits for them, and re-layouts  45 us (27%)
  waiting for transfers between devices  44.3 us (27%)
  blocking collectives  37.9 us (23%)
  matrix products  13.3 us (8%)
  starting transfers between devices  12.3 us (7%)
  other arithmetic  11.9 us (7%)
    all_to_all x1, blocking collectives, route_out(): lax.all_to_all(outgoing, ('shard', 'tensor'), split_axis=0, concat_axis=0...  37.9 us
    all_to_all x1, waiting for transfers between devices, route_back(): lax.all_to_all(outgoing, ('shard', 'tensor'), split_axis=0, concat_axis=0...  26.6 us
    ppermute x1, waiting for transfers between devices, body(): other_back = lax.ppermute(other_part, 'tensor', partner)  11.3 us
    reshape x2, local copies, waits for them, and re-layouts, body(): delta.reshape(slots, n_shard, col_blocks, half, per_block, shard_cols)  6.51 us
    gather x2, local copies, waits for them, and re-layouts, body(): slabs[slot_block]  6.42 us
    dot_general x1, matrix products, direction(): jnp.einsum('kij,kjl->kil', half, right_root, preferred_element_type=jnp.f...  6.34 us
    reshape x1, local copies, waits for them, and re-layouts, body(): sendback = pieces.reshape(owners, chunk // lanes, lanes)  5.93 us
    all_to_all x1, starting transfers between devices, route_back(): lax.all_to_all(outgoing, ('shard', 'tensor'), split_axis=0, concat_axis=0...  5.93 us
  transfers between devices with their start and end apart: 5, of which 4 were waited for; matrix products, arithmetic and copies ran while one was open for 6% of the time, Pallas kernels for 0%

profile of v4, /device:TPU:0, one launch (start us, length us, event | category | flops | bytes accessed | tf_op | source)
XLA Modules:
  0.0 165.5 jit_solution(2407046255578913481)
XLA Ops:
  0.6 0.0 copy-start
  0.7 1.3 constant_dynamic-slice_fusion
  2.0 3.4 %collective-permute-start = (bf16[48,10,320]{2,0,1:T(8,128)(2,1)S(1)}, bf16[48,10,320]{2,0,1:T(8,128)(2,1)S(1)}, u32[]{:S(2)}, u32[]{:S(2)}) collective-permute-start(bf16[48,10,320]{2,0,1:T(8,128)(2,1)S(1)} %get-tuple-element.22), channel_id=1, source_target_pairs={{0,2},{1,3},{2,0},{3,1},{4,6},{5,7},{6,4},{7,5},{8,10},{9,11},{10,... | collective-permute-start | bytes 921608 | tf_op jit(solution)/shard_map/ppermute | solution.py:63
  5.4 0.7 compare_select_fusion.1
  6.0 0.9 scatter_custom_fusion.1
  6.9 0.9 scatter_custom_fusion
  7.8 0.2 broadcast_in_dim.38
  8.0 0.1 copy.55
  8.1 0.1 copy.56
  8.2 5.7 %collective-permute-done = bf16[48,10,320]{2,0,1:T(8,128)(2,1)S(1)} collective-permute-done((bf16[48,10,320]{2,0,1:T(8,128)(2,1)S(1)}, bf16[48,10,320]{2,0,1:T(8,128)(2,1)S(1)}, u32[]{:S(2)}, u32[]{:S(2)}) %collective-permute-start) | collective-permute-done | bytes 307232 | tf_op jit(solution)/shard_map/ppermute | solution.py:63
  13.9 0.2 fusion.5
  14.2 0.3 pad_maximum_fusion
  14.5 0.1 copy.60
  14.6 0.7 reshape.50
  15.3 2.9 %gather_fusion = bf16[256,3200]{1,0:T(8,128)(2,1)} fusion(bf16[96,3200]{1,0:T(8,128)(2,1)S(1)} %reshape.50, s32[1024]{0:T(1024)S(1)} %pad_clamp_fusion.1), kind=kCustom, calls=%fused_computation | custom fusion | bytes 3277824 | tf_op jit(solution)/shard_map/gather | solution.py:75
  18.1 3.6 %gather.9 = bf16[128,50,128]{2,1,0:T(8,128)(2,1)S(1)} reshape(bf16[256,3200]{1,0:T(8,128)(2,1)} %gather_fusion) | data formatting | bytes 3276800 | tf_op jit(solution)/shard_map/gather | solution.py:75
  21.7 1.3 broadcast_select_fusion
  23.0 37.9 %all_to_all.10 = bf16[128,50,128]{2,1,0:T(8,128)(2,1)S(1)} all-to-all(bf16[128,50,128]{2,1,0:T(8,128)(2,1)S(1)} %broadcast_select_fusion), channel_id=1, replica_groups=mesh['shard'=32,'tensor'=4] {'shard','tensor'}, dimensions={0} | all-to-all | bytes 3276800 | tf_op jit(solution)/shard_map/all_to_all | solution.py:11
  60.9 3.9 %reshape.51 = bf16[32,2,2,2,10,320]{5,4,3,2,1,0:T(8,128)(2,1)} reshape(bf16[128,50,128]{2,1,0:T(8,128)(2,1)S(1)} %all_to_all.10) | data formatting | bytes 3276800 | tf_op jit(solution)/shard_map/reshape | solution.py:77
  64.8 4.7 %copy.61 = bf16[2,32,2,10,2,320]{5,4,3,2,1,0:T(2,128)(2,1)} copy(bf16[2,32,2,10,2,320]{5,3,0,4,2,1:T(8,128)(2,1)} %bitcast.22) | data formatting | bytes 3276800 | tf_op jit(solution)/shard_map/transpose | solution.py:78
  69.5 4.2 %reshape.52 = bf16[2,640,640]{2,1,0:T(8,128)(2,1)S(1)} reshape(bf16[2,32,2,10,2,320]{5,4,3,2,1,0:T(2,128)(2,1)} %copy.61) | data formatting | bytes 3276800 | tf_op jit(solution)/shard_map/reshape | solution.py:78
  73.7 5.4 %fusion.2 = (f32[2]{0:T(128)S(1)}, f32[2,640,640]{2,1,0:T(8,128)}) fusion(bf16[2,640,640]{2,1,0:T(8,128)(2,1)S(1)} %reshape.52, f32[2,640,640]{2,1,0:T(8,128)} %param.15), kind=kLoop, calls=%fused_computation.12 | loop fusion | flops 7372798 | bytes 8192008 | tf_op jit(solution)/shard_map/reduce_sum | solution.py:40
  79.1 6.3 %multiply_reduce_fusion = (f32[2]{0:T(128)S(1)}, f32[2,640,640]{2,1,0:T(8,128)}) fusion(bf16[2,640,640]{2,1,0:T(8,128)(2,1)S(1)} %copy-done, bf16[2,640,640]{2,1,0:T(8,128)(2,1)S(1)} %reshape.52, bf16[2,640,640]{2,1,0:T(8,128)(2,1)} %param.13), kind=kOutput, calls=%fused_computation.11 | convolution fusion | flops 2099609600 | bytes 8192008 | tf_op jit(solution)/shard_map/kij,kjl->kil/dot_general | solution.py:36
  85.5 2.2 %multiply_convert_fusion = bf16[2,640,640]{2,1,0:T(8,128)(2,1)S(1)} fusion(f32[2,640,640]{2,1,0:T(8,128)} %get-tuple-element.25, f32[2]{0:T(128)S(1)} %rsqrt_multiply_fusion), kind=kLoop, calls=%fused_computation.10 | loop fusion | flops 1638400 | bytes 4915208 | tf_op jit(solution)/shard_map/convert_element_type | solution.py:43
  87.7 2.6 %reshape.53 = bf16[2,32,2,10,2,320]{5,4,3,2,1,0:T(2,128)(2,1)} reshape(bf16[2,640,640]{2,1,0:T(8,128)(2,1)S(1)} %multiply_convert_fusion) | data formatting | bytes 3276800 | tf_op jit(solution)/shard_map/reshape | solution.py:81
  90.3 3.9 %copy.95 = bf16[2,32,2,10,2,320]{5,3,0,4,2,1:T(8,128)(2,1)} copy(bf16[2,32,2,10,2,320]{5,4,3,2,1,0:T(2,128)(2,1)} %reshape.53) | data formatting | bytes 3276800 | tf_op jit(solution)/shard_map/reshape | solution.py:81
  94.2 5.9 %reshape.54 = bf16[128,50,128]{2,1,0:T(8,128)(2,1)} reshape(bf16[32,2,2,2,10,320]{5,4,3,2,1,0:T(8,128)(2,1)} %bitcast.23) | data formatting | bytes 3276800 | tf_op jit(solution)/shard_map/reshape | solution.py:84
  100.2 5.9 %all-to-all-start.1 = ((bf16[128,50,128]{2,1,0:T(8,128)(2,1)}), bf16[128,50,128]{2,1,0:T(8,128)(2,1)}, u32[]{:S(2)}, u32[]{:S(2)}) async-start(bf16[128,50,128]{2,1,0:T(8,128)(2,1)} %reshape.54), calls=%async_computation.1 | async-start | bytes 3670016 | tf_op jit(solution)/shard_map/all_to_all | solution.py:16
  106.1 26.6 %all-to-all-done.1 = bf16[128,50,128]{2,1,0:T(8,128)(2,1)} async-done(((bf16[128,50,128]{2,1,0:T(8,128)(2,1)}), bf16[128,50,128]{2,1,0:T(8,128)(2,1)}, u32[]{:S(2)}, u32[]{:S(2)}) %all-to-all-start.1) | async-done | bytes 1638432 | tf_op jit(solution)/shard_map/all_to_all | solution.py:16
  132.7 3.5 %reshape.55 = bf16[256,3200]{1,0:T(8,128)(2,1)S(1)} reshape(bf16[128,50,128]{2,1,0:T(8,128)(2,1)} %all-to-all-done.1) | data formatting | bytes 3276800 | tf_op jit(solution)/shard_map/reshape | solution.py:85
  136.2 1.8 %gather_fusion.1 = bf16[96,3200]{1,0:T(8,128)(2,1)} fusion(bf16[256,3200]{1,0:T(8,128)(2,1)S(1)} %reshape.55, s32[1024]{0:T(1024)S(1)} %pad_clamp_fusion), kind=kCustom, calls=%fused_computation.1 | custom fusion | bytes 1229184 | tf_op jit(solution)/shard_map/gather | solution.py:86
  137.9 2.1 %reshape.56 = bf16[48,2,10,320]{3,2,1,0:T(8,128)(2,1)S(1)} reshape(bf16[96,3200]{1,0:T(8,128)(2,1)} %gather_fusion.1) | data formatting | bytes 1228800 | tf_op jit(solution)/shard_map/reshape | solution.py:86
  140.0 0.1 select_bitcast_fusion
  140.1 0.0 copy-start.2
  140.1 0.1 copy.65
  140.2 1.0 collective-permute-start.1
  141.2 11.3 %collective-permute-done.1 = bf16[48,10,320]{2,0,1:T(8,128)(2,1)S(1)} collective-permute-done((bf16[48,10,320]{2,0,1:T(8,128)(2,1)S(1)}, bf16[48,10,320]{2,0,1:T(8,128)(2,1)S(1)}, u32[]{:S(2)}, u32[]{:S(2)}) %collective-permute-start.1) | collective-permute-done | bytes 307232 | tf_op jit(solution)/shard_map/ppermute | solution.py:89
  152.5 0.2 copy_select_fusion.3
  152.7 0.8 multiply_reduce_fusion.1
  153.5 0.7 collective-permute-start.2
  154.2 0.2 copy-done.3
  154.5 3.5 %multiply_add_fusion = f32[2,640,640]{2,1,0:T(8,128)} fusion(f32[2,640,640]{2,1,0:T(8,128)S(1)} %copy-done.3, bf16[2,640,640]{2,1,0:T(8,128)(2,1)S(1)} %reshape.52), kind=kOutput, calls=%fused_computation.8 | convolution fusion | flops 1051033600 | bytes 8192000 | tf_op jit(solution)/shard_map/kji,kjl->kil/dot_general | solution.py:24
  157.9 1.2 collective-permute-start.3
  159.2 3.5 %multiply_add_fusion.1 = f32[2,640,640]{2,1,0:T(8,128)} fusion(f32[2,640,640]{2,1,0:T(8,128)S(1)} %copy-done.4, bf16[2,640,640]{2,1,0:T(8,128)(2,1)S(1)} %reshape.52), kind=kOutput, calls=%fused_computation.9 | convolution fusion | flops 1051033600 | bytes 8192000 | tf_op jit(solution)/shard_map/kij,klj->kil/dot_general | solution.py:21
  162.6 0.7 collective-permute-done.3
  163.4 0.0 copy-start.1
  163.4 0.8 fusion.3
  164.1 1.4 copy.70
  (17 shorter events, 0.1 us)
Async XLA Ops:
  0.6 78.5 %copy-start = (bf16[2,640,640]{2,1,0:T(8,128)(2,1)S(1)}, bf16[2,640,640]{2,1,0:T(8,128)(2,1)}, u32[]{:S(2)}) copy-start(bf16[2,640,640]{2,1,0:T(8,128)(2,1)} %param.14) | copy-start | bytes 4915204
  2.0 12.0 %collective-permute-start = (bf16[48,10,320]{2,0,1:T(8,128)(2,1)S(1)}, bf16[48,10,320]{2,0,1:T(8,128)(2,1)S(1)}, u32[]{:S(2)}, u32[]{:S(2)}) collective-permute-start(bf16[48,10,320]{2,0,1:T(8,128)(2,1)S(1)} %get-tuple-element.22), channel_id=1, source_target_pairs={{0,2},{1,3},{2,0},{3,1},{4,6},{5,7},{6,4},{7,5},{8,10},{9,11},{10,... | collective-permute-start | bytes 921608 | tf_op jit(solution)/shard_map/ppermute | solution.py:63
  100.2 32.5 %all-to-all-start.1 = ((bf16[128,50,128]{2,1,0:T(8,128)(2,1)}), bf16[128,50,128]{2,1,0:T(8,128)(2,1)}, u32[]{:S(2)}, u32[]{:S(2)}) async-start(bf16[128,50,128]{2,1,0:T(8,128)(2,1)} %reshape.54), calls=%async_computation.1 | async-start | bytes 3670016 | tf_op jit(solution)/shard_map/all_to_all | solution.py:16
  140.1 12.6 %copy-start.2 = (f32[48,20,320]{2,0,1:T(8,128)S(1)}, f32[48,20,320]{2,0,1:T(8,128)}, u32[]{:S(2)}) copy-start(f32[48,20,320]{2,0,1:T(8,128)} %param.8) | copy-start | bytes 3686404
  140.2 12.3 %collective-permute-start.1 = (bf16[48,10,320]{2,0,1:T(8,128)(2,1)S(1)}, bf16[48,10,320]{2,0,1:T(8,128)(2,1)S(1)}, u32[]{:S(2)}, u32[]{:S(2)}) collective-permute-start(bf16[48,10,320]{2,0,1:T(8,128)(2,1)S(1)} %copy.65), channel_id=1, source_target_pairs={{0,2},{1,3},{2,0},{3,1},{4,6},{5,7},{6,4},{7,5},{8,10},{9,11},{10,... | collective-permute-start | bytes 921608 | tf_op jit(solution)/shard_map/ppermute | solution.py:89
  152.5 1.9 %copy-start.3 = (f32[2,640,640]{2,1,0:T(8,128)S(1)}, f32[2,640,640]{2,1,0:T(8,128)}, u32[]{:S(2)}) copy-start(f32[2,640,640]{2,1,0:T(8,128)} %param.12) | copy-start | bytes 9830404
  153.5 4.4 %collective-permute-start.2 = (f32[48,20]{1,0:T(8,128)S(1)}, f32[48,20]{1,0:T(8,128)S(1)}, u32[]{:S(2)}, u32[]{:S(2)}) collective-permute-start(f32[48,20]{1,0:T(8,128)S(1)} %multiply_reduce_fusion.1), channel_id=1, source_target_pairs={{0,1},{1,0},{2,3},{3,2},{4,5},{5,4},{6,7},{7,6},{8,9},{9,8},{10,11... | collective-permute-start | bytes 11528 | tf_op jit(solution)/shard_map/ppermute | solution.py:98
  154.5 4.7 %copy-start.4 = (f32[2,640,640]{2,1,0:T(8,128)S(1)}, f32[2,640,640]{2,1,0:T(8,128)}, u32[]{:S(2)}) copy-start(f32[2,640,640]{2,1,0:T(8,128)} %param.11) | copy-start | bytes 9830404
  157.9 5.4 %collective-permute-start.3 = (f32[48,20]{1,0:T(8,128)S(1)}, f32[48,20]{1,0:T(8,128)S(1)}, u32[]{:S(2)}, u32[]{:S(2)}) collective-permute-start(f32[48,20]{1,0:T(8,128)S(1)} %add.61), channel_id=1, source_target_pairs={{0,2},{1,3},{2,0},{3,1},{4,6},{5,7},{6,4},{7,5},{8,10},{9,11},{10,... | collective-permute-start | bytes 11528 | tf_op jit(solution)/shard_map/ppermute | solution.py:98
  163.4 2.1 %copy-start.1 = (bf16[2,640,640]{2,1,0:T(8,128)(2,1)S(1)}, bf16[2,640,640]{2,1,0:T(8,128)(2,1)}, u32[]{:S(2)}) copy-start(bf16[2,640,640]{2,1,0:T(8,128)(2,1)} %param.14) | copy-start | bytes 4915204

commit v5 on v4

--- a/solution.py
+++ b/solution.py
@@ -55,41 +55,32 @@
     slots = left_stats.shape[0]
     owners = n_shard * n_tensor
     total_slots = owners * slots
-    half = shard_rows // col_blocks
-    mine_col = lax.axis_index("tensor") // per_block
-    partner = [(i, (i + per_block) % n_tensor) for i in range(n_tensor)]
-    keep = lax.dynamic_slice_in_dim(grads, mine_col * half, half, axis=1)
-    give = lax.dynamic_slice_in_dim(grads, (1 - mine_col) * half, half, axis=1)
-    got = lax.ppermute(give, "tensor", partner)
-    first = jnp.where(mine_col == 0, keep, got)
-    second = jnp.where(mine_col == 0, got, keep)
+    quarter = shard_rows // n_tensor
     block_count = owner_slot.shape[0]
-    slab_size = half * shard_cols
+    slab_size = quarter * order_size
     chunk = slots * slab_size
     lanes = 128 if chunk % 128 == 0 else chunk
-    slabs = jnp.stack([first, second], axis=1).reshape(row_blocks * col_blocks, slab_size)
+    parts = grads.reshape(row_blocks, n_tensor, quarter, shard_cols)
+    parts = lax.all_to_all(parts, "tensor", split_axis=1, concat_axis=1, tiled=True)
+    rows = parts.reshape(row_blocks, col_blocks, per_block, quarter, shard_cols).transpose(0, 1, 3, 2, 4)
+    slabs = rows.reshape(row_blocks * col_blocks, slab_size)
     slot_block = jnp.zeros((total_slots,), jnp.int32).at[owner_slot].set(
         jnp.arange(block_count, dtype=jnp.int32)
     )
     slot_used = jnp.zeros((total_slots,), jnp.bool_).at[owner_slot].set(True)
     outgoing = jnp.where(slot_used[:, None], slabs[slot_block], jnp.zeros((), jnp.bfloat16))
     arrived = route_out(outgoing.reshape(owners, chunk // lanes, lanes))
-    arrived = arrived.reshape(n_shard, col_blocks, per_block, slots, half, shard_cols)
-    block_grads = arrived.transpose(3, 0, 1, 4, 2, 5).reshape(slots, order_size, order_size)
+    arrived = arrived.reshape(owners, slots, quarter, order_size)
+    block_grads = arrived.transpose(1, 0, 2, 3).reshape(slots, order_size, order_size)
     new_left, new_right = refresh(block_grads, left_stats, right_stats)
     delta, new_moment = direction(block_grads, left_root, right_root, moment)
-    pieces = delta.reshape(slots, n_shard, col_blocks, half, per_block, shard_cols).transpose(
-        1, 2, 4, 0, 3, 5
-    )
+    pieces = delta.reshape(slots, owners, quarter, order_size).transpose(1, 0, 2, 3)
     sendback = pieces.reshape(owners, chunk // lanes, lanes)
     returned = route_back(sendback).reshape(total_slots, slab_size)
-    back = returned[owner_slot].reshape(row_blocks, col_blocks, half, shard_cols)
-    own_part = jnp.where(mine_col == 0, back[:, 0], back[:, 1])
-    other_part = jnp.where(mine_col == 0, back[:, 1], back[:, 0])
-    other_back = lax.ppermute(other_part, "tensor", partner)
-    top = jnp.where(mine_col == 0, own_part, other_back)
-    bottom = jnp.where(mine_col == 0, other_back, own_part)
-    my_delta = jnp.concatenate([top, bottom], axis=1)
+    back = returned[owner_slot].reshape(row_blocks, col_blocks, quarter, per_block, shard_cols)
+    back = back.transpose(0, 1, 3, 2, 4).reshape(row_blocks, n_tensor, quarter, shard_cols)
+    back = lax.all_to_all(back, "tensor", split_axis=1, concat_axis=1, tiled=True)
+    my_delta = back.reshape(row_blocks, shard_rows, shard_cols)
     updated = weights - step_size * my_delta.astype(jnp.float32)
     squares = jnp.sum(updated * updated, axis=2)
     step = 1

time: 166 us -> 176 us (1.060)
  blocking collectives: 37.9 us -> 50.8 us
  waiting for transfers between devices: 44.3 us -> 36 us
  local copies, waits for them, and re-layouts: 45 us -> 50 us
    ppermute x2 -> x0, waiting for transfers between devices: 17 us -> none  [the longest x1 11.3 us: body(): other_back = lax.ppermute(other_part, 'tensor', partner)]
    all_to_all x0 -> x1, blocking collectives: none -> 15 us  [body(): lax.all_to_all(back, 'tensor', split_axis=1, concat_axis=1, tiled=True)]
    all_to_all x0 -> x1, waiting for transfers between devices: none -> 8.86 us  [body(): lax.all_to_all(parts, 'tensor', split_axis=1, concat_axis=1, tiled=True)]
    transpose x1 -> x3, local copies, waits for them, and re-layouts: 4.71 us -> 13.2 us  [the longest x1 6.59 us: body(): delta.reshape(slots, owners, quarter, order_size).transpose(1, 0, 2, 3)]
    reshape x6 -> x4, local copies, waits for them, and re-layouts: 17.4 us -> 9.54 us  [the longest x1 4.84 us: body(): arrived.transpose(1, 0, 2, 3).reshape(slots, order_size, order_size)]
    all_to_all x0 -> x1, starting transfers between devices: none -> 4.72 us  [body(): lax.all_to_all(parts, 'tensor', split_axis=1, concat_axis=1, tiled=True)]
    ppermute x2 -> x0, starting transfers between devices: 4.4 us -> none  [the longest x1 3.39 us: body(): got = lax.ppermute(give, 'tensor', partner)]
    convert_element_type x0 -> x1, local copies, waits for them, and re-layouts: none -> 2.85 us  [direction(): delta = (graft[:, None, None] * precond).astype(jnp.bfloat16)]
  transfers between devices with their start and end apart: 5 -> 4, of which waited for: 4 -> 3; matrix products, arithmetic and copies ran while one was open for 6% -> 6% of each run, Pallas kernels for 0% -> 0%
where the time goes in v5:
time: 176 us; the launch traced here: 175 us
  blocking collectives  50.8 us (29%)
  local copies, waits for them, and re-layouts  50 us (28%)
  waiting for transfers between devices  36 us (20%)
  matrix products  13.6 us (8%)
  starting transfers between devices  12.2 us (7%)
  other arithmetic  11.5 us (7%)
    all_to_all x1, blocking collectives, route_out(): lax.all_to_all(outgoing, ('shard', 'tensor'), split_axis=0, concat_axis=0...  35.8 us
    all_to_all x1, waiting for transfers between devices, route_back(): lax.all_to_all(outgoing, ('shard', 'tensor'), split_axis=0, concat_axis=0...  26.4 us
    all_to_all x1, blocking collectives, body(): lax.all_to_all(back, 'tensor', split_axis=1, concat_axis=1, tiled=True)  15 us
    all_to_all x1, waiting for transfers between devices, body(): lax.all_to_all(parts, 'tensor', split_axis=1, concat_axis=1, tiled=True)  8.86 us
    dot_general x1, matrix products, direction(): jnp.einsum('kij,kjl->kil', half, right_root, preferred_element_type=jnp.f...  6.72 us
    transpose x1, local copies, waits for them, and re-layouts, body(): delta.reshape(slots, owners, quarter, order_size).transpose(1, 0, 2, 3)  6.59 us
    gather x2, local copies, waits for them, and re-layouts, body(): slabs[slot_block]  6.42 us
    transpose x1, local copies, waits for them, and re-layouts, body(): arrived.transpose(1, 0, 2, 3).reshape(slots, order_size, order_size)  6.09 us
  transfers between devices with their start and end apart: 4, of which 3 were waited for; matrix products, arithmetic and copies ran while one was open for 6% of the time, Pallas kernels for 0%

profile of v5, /device:TPU:0, one launch (start us, length us, event | category | flops | bytes accessed | tf_op | source)
XLA Modules:
  0.0 174.9 jit_solution(7733506012457795591)
XLA Ops:
  0.6 0.0 copy-start
  0.6 4.7 %all-to-all-start = ((bf16[48,4,5,320]{3,0,2,1:T(8,128)(2,1)}), bf16[48,4,5,320]{3,0,2,1:T(8,128)(2,1)S(1)}, u32[]{:S(2)}, u32[]{:S(2)}) async-start(bf16[48,4,5,320]{3,0,2,1:T(8,128)(2,1)} %bitcast.32), calls=%async_computation | async-start | bytes 1474560 | tf_op jit(solution)/shard_map/all_to_all | solution.py:64
  5.4 0.7 compare_select_fusion.1
  6.0 0.9 scatter_custom_fusion
  6.9 0.2 broadcast_in_dim.38
  7.1 0.1 copy.27
  7.2 0.1 copy.28
  7.4 0.9 scatter_custom_fusion.1
  8.3 8.9 %all-to-all-done = bf16[48,4,5,320]{3,0,2,1:T(8,128)(2,1)S(1)} async-done(((bf16[48,4,5,320]{3,0,2,1:T(8,128)(2,1)}), bf16[48,4,5,320]{3,0,2,1:T(8,128)(2,1)S(1)}, u32[]{:S(2)}, u32[]{:S(2)}) %all-to-all-start) | async-done | bytes 614432 | tf_op jit(solution)/shard_map/all_to_all | solution.py:64
  17.1 0.6 copy.29
  17.7 0.5 reshape.61
  18.2 2.9 %gather_fusion = bf16[256,3200]{1,0:T(8,128)(2,1)} fusion(bf16[96,3200]{1,0:T(8,128)(2,1)S(1)} %reshape.61, s32[1024]{0:T(1024)S(1)} %pad_clamp_fusion.1), kind=kCustom, calls=%fused_computation | custom fusion | bytes 3277824 | tf_op jit(solution)/shard_map/gather | solution.py:71
  21.1 3.6 %gather.9 = bf16[128,50,128]{2,1,0:T(8,128)(2,1)S(1)} reshape(bf16[256,3200]{1,0:T(8,128)(2,1)} %gather_fusion) | data formatting | bytes 3276800 | tf_op jit(solution)/shard_map/gather | solution.py:71
  24.7 1.3 broadcast_select_fusion
  26.0 35.8 %all_to_all.20 = bf16[128,50,128]{2,1,0:T(8,128)(2,1)S(1)} all-to-all(bf16[128,50,128]{2,1,0:T(8,128)(2,1)S(1)} %broadcast_select_fusion), channel_id=1, replica_groups=mesh['shard'=32,'tensor'=4] {'shard','tensor'}, dimensions={0} | all-to-all | bytes 3276800 | tf_op jit(solution)/shard_map/all_to_all | solution.py:11
  61.7 2.6 %copy.30 = bf16[128,50,128]{0,2,1:T(8,128)(2,1)} copy(bf16[128,50,128]{2,1,0:T(8,128)(2,1)S(1)} %all_to_all.20) | data formatting | bytes 3276800 | tf_op jit(solution)/shard_map/all_to_all | solution.py:11
  64.4 6.1 %copy.31 = bf16[2,128,5,640]{3,0,2,1:T(2,128)(2,1)S(1)} copy(bf16[2,128,5,640]{1,3,2,0:T(8,128)(2,1)} %bitcast.27) | data formatting | bytes 3276800 | tf_op jit(solution)/shard_map/transpose | solution.py:74
  70.5 4.8 %copy.33 = bf16[2,640,640]{1,2,0:T(8,128)(2,1)} copy(bf16[2,640,640]{2,0,1:T(2,128)(2,1)S(1)} %bitcast.23) | data formatting | bytes 3276800 | tf_op jit(solution)/shard_map/reshape | solution.py:74
  75.3 5.4 %fusion.2 = (f32[2]{0:T(128)S(1)}, f32[2,640,640]{2,1,0:T(8,128)}) fusion(bf16[2,640,640]{2,0,1:T(2,128)(2,1)S(1)} %bitcast.24, f32[2,640,640]{2,1,0:T(8,128)} %param.15), kind=kLoop, calls=%fused_computation.12 | loop fusion | flops 7372798 | bytes 8192008 | tf_op jit(solution)/shard_map/reduce_sum | solution.py:40
  80.7 0.0 copy-done
  80.7 6.7 %multiply_reduce_fusion = (f32[2]{0:T(128)S(1)}, f32[2,640,640]{2,1,0:T(8,128)}) fusion(bf16[2,640,640]{2,1,0:T(8,128)(2,1)S(1)} %copy-done, bf16[2,640,640]{1,2,0:T(8,128)(2,1)} %copy.33, bf16[2,640,640]{2,1,0:T(8,128)(2,1)} %param.13), kind=kOutput, calls=%fused_computation.11 | convolution fusion | flops 2099609600 | bytes 8192008 | tf_op jit(solution)/shard_map/kij,kjl->kil/dot_general | solution.py:36
  87.5 2.2 %multiply_convert_fusion = bf16[2,640,640]{2,1,0:T(8,128)(2,1)S(1)} fusion(f32[2,640,640]{2,1,0:T(8,128)} %get-tuple-element.7, f32[2]{0:T(128)S(1)} %rsqrt_multiply_fusion), kind=kLoop, calls=%fused_computation.10 | loop fusion | flops 1638400 | bytes 4915208 | tf_op jit(solution)/shard_map/convert_element_type | solution.py:43
  89.7 2.8 %copy.35 = bf16[2,640,640]{2,0,1:T(2,128)(2,1)} copy(bf16[2,640,640]{2,1,0:T(8,128)(2,1)S(1)} %multiply_convert_fusion) | data formatting | bytes 3276800 | tf_op jit(solution)/shard_map/convert_element_type | solution.py:43
  92.5 6.6 %copy.36 = bf16[128,2,5,640]{0,3,2,1:T(8,128)(2,1)} copy(bf16[128,2,5,640]{3,1,2,0:T(2,128)(2,1)} %bitcast.28) | data formatting | bytes 3276800 | tf_op jit(solution)/shard_map/transpose | solution.py:77
  99.1 3.5 %copy.37 = bf16[128,50,128]{2,1,0:T(8,128)(2,1)} copy(bf16[128,50,128]{0,2,1:T(8,128)(2,1)} %bitcast.29) | data formatting | bytes 3276800 | tf_op jit(solution)/shard_map/reshape | solution.py:78
  102.6 5.9 %all-to-all-start.2 = ((bf16[128,50,128]{2,1,0:T(8,128)(2,1)}), bf16[128,50,128]{2,1,0:T(8,128)(2,1)}, u32[]{:S(2)}, u32[]{:S(2)}) async-start(bf16[128,50,128]{2,1,0:T(8,128)(2,1)} %copy.37), calls=%async_computation.2 | async-start | bytes 3670016 | tf_op jit(solution)/shard_map/all_to_all | solution.py:16
  108.6 26.4 %all-to-all-done.2 = bf16[128,50,128]{2,1,0:T(8,128)(2,1)} async-done(((bf16[128,50,128]{2,1,0:T(8,128)(2,1)}), bf16[128,50,128]{2,1,0:T(8,128)(2,1)}, u32[]{:S(2)}, u32[]{:S(2)}) %all-to-all-start.2) | async-done | bytes 1638432 | tf_op jit(solution)/shard_map/all_to_all | solution.py:16
  134.9 4.3 %reshape.66 = bf16[256,3200]{1,0:T(8,128)(2,1)} reshape(bf16[128,50,128]{2,1,0:T(8,128)(2,1)} %all-to-all-done.2) | data formatting | bytes 3276800 | tf_op jit(solution)/shard_map/reshape | solution.py:79
  139.2 4.0 %gather_fusion.1 = bf16[96,3200]{1,0:T(8,128)(2,1)} fusion(bf16[256,3200]{1,0:T(8,128)(2,1)} %reshape.66, s32[1024]{0:T(1024)S(1)} %pad_clamp_fusion), kind=kCustom, calls=%fused_computation.1 | custom fusion | bytes 1229184 | tf_op jit(solution)/shard_map/gather | solution.py:80
  143.2 3.0 %reshape.67 = bf16[48,2,5,2,320]{4,3,2,1,0:T(2,128)(2,1)} reshape(bf16[96,3200]{1,0:T(8,128)(2,1)} %gather_fusion.1) | data formatting | bytes 1228800 | tf_op jit(solution)/shard_map/reshape | solution.py:80
  146.2 1.2 copy.38
  147.4 0.0 copy-start.4
  147.4 15.0 %all_to_all.21 = bf16[48,4,5,320]{3,0,2,1:T(8,128)(2,1)S(1)} all-to-all(bf16[48,4,5,320]{3,0,2,1:T(8,128)(2,1)S(1)} %bitcast.31), channel_id=1, replica_groups=mesh['shard'=32,'tensor'=4] {'tensor'}, dimensions={1} | all-to-all | bytes 1228800 | tf_op jit(solution)/shard_map/all_to_all | solution.py:82
  162.4 0.1 convert_multiply_fusion
  162.5 0.0 copy-start.1
  162.5 0.0 copy-start.2
  162.5 0.2 bitcast_subtract_fusion
  162.7 0.2 multiply_reduce_fusion.1
  162.9 0.0 copy-start.3
  163.0 0.6 collective-permute-start
  163.6 0.4 copy-done.1
  164.0 1.0 copy-done.2
  164.9 3.5 %multiply_add_fusion = f32[2,640,640]{2,1,0:T(8,128)} fusion(f32[2,640,640]{2,1,0:T(8,128)S(1)} %copy-done.2, bf16[2,640,640]{1,2,0:T(8,128)(2,1)S(1)} %copy-done.1, bf16[2,640,640]{2,0,1:T(2,128)(2,1)S(1)} %bitcast.25), kind=kOutput, calls=%fused_computation.8 | convolution fusion | flops 1051033600 | bytes 9830400 | tf_op jit(solution)/shard_map/kji,kjl->kil/dot_general | solution.py:24
  168.4 0.0 collective-permute-done
  168.4 1.0 collective-permute-start.1
  169.4 3.5 %multiply_add_fusion.1 = f32[2,640,640]{2,1,0:T(8,128)} fusion(f32[2,640,640]{2,1,0:T(8,128)S(1)} %copy-done.3, bf16[2,640,640]{2,0,1:T(2,128)(2,1)S(1)} %bitcast.26), kind=kOutput, calls=%fused_computation.9 | convolution fusion | flops 1051033600 | bytes 8192000 | tf_op jit(solution)/shard_map/kij,klj->kil/dot_general | solution.py:21
  172.8 0.8 collective-permute-done.1
  173.6 1.3 broadcast_multiply_fusion
  (12 shorter events, 0.1 us)
Async XLA Ops:
  0.6 80.1 %copy-start = (bf16[2,640,640]{2,1,0:T(8,128)(2,1)S(1)}, bf16[2,640,640]{2,1,0:T(8,128)(2,1)}, u32[]{:S(2)}) copy-start(bf16[2,640,640]{2,1,0:T(8,128)(2,1)} %param.14) | copy-start | bytes 4915204
  0.6 16.5 %all-to-all-start = ((bf16[48,4,5,320]{3,0,2,1:T(8,128)(2,1)}), bf16[48,4,5,320]{3,0,2,1:T(8,128)(2,1)S(1)}, u32[]{:S(2)}, u32[]{:S(2)}) async-start(bf16[48,4,5,320]{3,0,2,1:T(8,128)(2,1)} %bitcast.32), calls=%async_computation | async-start | bytes 1474560 | tf_op jit(solution)/shard_map/all_to_all | solution.py:64
  102.6 32.3 %all-to-all-start.2 = ((bf16[128,50,128]{2,1,0:T(8,128)(2,1)}), bf16[128,50,128]{2,1,0:T(8,128)(2,1)}, u32[]{:S(2)}, u32[]{:S(2)}) async-start(bf16[128,50,128]{2,1,0:T(8,128)(2,1)} %copy.37), calls=%async_computation.2 | async-start | bytes 3670016 | tf_op jit(solution)/shard_map/all_to_all | solution.py:16
  147.4 15.1 %copy-start.4 = (f32[48,20,320]{2,0,1:T(8,128)S(1)}, f32[48,20,320]{2,0,1:T(8,128)}, u32[]{:S(2)}) copy-start(f32[48,20,320]{2,0,1:T(8,128)} %param.8) | copy-start | bytes 3686404
  162.5 1.4 copy-start.1
  162.5 2.4 %copy-start.2 = (f32[2,640,640]{2,1,0:T(8,128)S(1)}, f32[2,640,640]{2,1,0:T(8,128)}, u32[]{:S(2)}) copy-start(f32[2,640,640]{2,1,0:T(8,128)} %param.12) | copy-start | bytes 9830404
  162.9 6.4 %copy-start.3 = (f32[2,640,640]{2,1,0:T(8,128)S(1)}, f32[2,640,640]{2,1,0:T(8,128)}, u32[]{:S(2)}) copy-start(f32[2,640,640]{2,1,0:T(8,128)} %param.11) | copy-start | bytes 9830404
  163.0 5.5 %collective-permute-start = (f32[48,20]{0,1:T(8,128)S(1)}, f32[48,20]{0,1:T(8,128)S(1)}, u32[]{:S(2)}, u32[]{:S(2)}) collective-permute-start(f32[48,20]{0,1:T(8,128)S(1)} %multiply_reduce_fusion.1), channel_id=1, source_target_pairs={{0,1},{1,0},{2,3},{3,2},{4,5},{5,4},{6,7},{7,6},{8,9},{9,8},{10,11... | collective-permute-start | bytes 11528 | tf_op jit(solution)/shard_map/ppermute | solution.py:89
  168.4 5.2 %collective-permute-start.1 = (f32[48,20]{0,1:T(8,128)S(1)}, f32[48,20]{0,1:T(8,128)S(1)}, u32[]{:S(2)}, u32[]{:S(2)}) collective-permute-start(f32[48,20]{0,1:T(8,128)S(1)} %add.52), channel_id=1, source_target_pairs={{0,2},{1,3},{2,0},{3,1},{4,6},{5,7},{6,4},{7,5},{8,10},{9,11},{10,... | collective-permute-start | bytes 11528 | tf_op jit(solution)/shard_map/ppermute | solution.py:89

commit v6 on v4

--- a/solution.py
+++ b/solution.py
@@ -21,10 +21,10 @@
     gram_left = jnp.einsum(
         "kij,klj->kil", block_grads, block_grads, preferred_element_type=jnp.float32
     )
+    new_left = stat_decay * left_stats + (1.0 - stat_decay) * gram_left
     gram_right = jnp.einsum(
         "kji,kjl->kil", block_grads, block_grads, preferred_element_type=jnp.float32
     )
-    new_left = stat_decay * left_stats + (1.0 - stat_decay) * gram_left
     new_right = stat_decay * right_stats + (1.0 - stat_decay) * gram_right
     return (new_left, new_right)
 
@@ -44,7 +44,7 @@
     return (delta, new_moment)
 
 
-def body(weights, grads, owner_slot, left_stats, right_stats, left_root, right_root, moment):
+def body_steps(weights, grads, owner_slot, left_stats, right_stats, left_root, right_root, moment):
     n_shard = lax.axis_size("shard")
     n_tensor = lax.axis_size("tensor")
     row_blocks, shard_rows, shard_cols = grads.shape
@@ -91,12 +91,16 @@
     bottom = jnp.where(mine_col == 0, other_back, own_part)
     my_delta = jnp.concatenate([top, bottom], axis=1)
     updated = weights - step_size * my_delta.astype(jnp.float32)
-    squares = jnp.sum(updated * updated, axis=2)
-    step = 1
-    while step < n_tensor:
-        pairs = [(i, i ^ step) for i in range(n_tensor)]
-        squares = squares + lax.ppermute(squares, "tensor", pairs)
-        step *= 2
+    partial = jnp.sum(updated * updated, axis=2)
+    shifted = [partial] + [
+        lax.ppermute(partial, "tensor", [(i, (i + k) % n_tensor) for i in range(n_tensor)])
+        for k in range(1, n_tensor)
+    ]
+    ranked = jnp.stack(shifted[:1] + shifted[:0:-1])
+    ranked = jnp.roll(ranked, lax.axis_index("tensor"), axis=0)
+    while ranked.shape[0] > 1:
+        ranked = ranked[0::2] + ranked[1::2]
+    squares = ranked[0]
     new_weights = updated * lax.rsqrt(squares / width + 1e-06)[:, :, None]
     return (new_weights, new_left, new_right, new_moment)
 
@@ -113,7 +117,7 @@
         P(("shard", "tensor"), None, None),
     )
     return jax.shard_map(
-        body,
+        body_steps,
         mesh=mesh,
         in_specs=placed,
         out_specs=(

time: 166 us -> 166 us (level)
  waiting for transfers between devices: 44.3 us -> 39.6 us
  matrix products: 13.3 us -> 15.1 us
  other arithmetic: 11.9 us -> 13.7 us
    ppermute x4 -> x5, waiting for transfers between devices: 17.7 us -> 13 us  [the longest x1 6 us: body_steps(): other_back = lax.ppermute(other_part, 'tensor', partner)]
    dot_general x1, matrix products: 3.47 us -> 5.31 us  [refresh(): jnp.einsum('kji,kjl->kil', block_grads, block_grads, preferred_element_ty...]
    mul x1, other arithmetic: 0.76 us -> 2.53 us  [body_steps(): new_weights = updated * lax.rsqrt(squares / width + 1e-06)[:, :, None]]
    ppermute x4 -> x5, starting transfers between devices: 6.32 us -> 7.14 us  [the longest x1 3.39 us: body_steps(): got = lax.ppermute(give, 'tensor', partner)]
  transfers between devices with their start and end apart: 5 -> 6, of which waited for: 4 -> 4; matrix products, arithmetic and copies ran while one was open for 6% -> 7% of each run, Pallas kernels for 0% -> 0%
where the time goes in v6:
time: 166 us
  local copies, waits for them, and re-layouts  45.4 us (27%)
  waiting for transfers between devices  39.6 us (24%)
  blocking collectives  37.9 us (23%)
  matrix products  15.1 us (9%)
  other arithmetic  13.7 us (8%)
  starting transfers between devices  13.1 us (8%)
    all_to_all x1, blocking collectives, route_out(): lax.all_to_all(outgoing, ('shard', 'tensor'), split_axis=0, concat_axis=0...  37.9 us
    all_to_all x1, waiting for transfers between devices, route_back(): lax.all_to_all(outgoing, ('shard', 'tensor'), split_axis=0, concat_axis=0...  26.6 us
    reshape x2, local copies, waits for them, and re-layouts, body_steps(): delta.reshape(slots, n_shard, col_blocks, half, per_block, shard_cols)  6.51 us
    gather x2, local copies, waits for them, and re-layouts, body_steps(): slabs[slot_block]  6.42 us
    dot_general x1, matrix products, direction(): jnp.einsum('kij,kjl->kil', half, right_root, preferred_element_type=jnp.f...  6.34 us
    ppermute x1, waiting for transfers between devices, body_steps(): other_back = lax.ppermute(other_part, 'tensor', partner)  6 us
    reshape x1, local copies, waits for them, and re-layouts, body_steps(): sendback = pieces.reshape(owners, chunk // lanes, lanes)  5.93 us
    all_to_all x1, starting transfers between devices, route_back(): lax.all_to_all(outgoing, ('shard', 'tensor'), split_axis=0, concat_axis=0...  5.93 us
  transfers between devices with their start and end apart: 6, of which 4 were waited for; matrix products, arithmetic and copies ran while one was open for 7% of the time, Pallas kernels for 0%

profile of v6, /device:TPU:0, one launch (start us, length us, event | category | flops | bytes accessed | tf_op | source)
XLA Modules:
  0.0 165.7 jit_solution(12539989682326904467)
XLA Ops:
  0.7 1.3 constant_dynamic-slice_fusion.1
  2.0 3.4 %collective-permute-start = (bf16[48,10,320]{2,0,1:T(8,128)(2,1)S(1)}, bf16[48,10,320]{2,0,1:T(8,128)(2,1)S(1)}, u32[]{:S(2)}, u32[]{:S(2)}) collective-permute-start(bf16[48,10,320]{2,0,1:T(8,128)(2,1)S(1)} %get-tuple-element.26), channel_id=1, source_target_pairs={{0,2},{1,3},{2,0},{3,1},{4,6},{5,7},{6,4},{7,5},{8,10},{9,11},{10,... | collective-permute-start | bytes 921608 | tf_op jit(solution)/shard_map/ppermute | solution.py:63
  5.4 0.7 compare_select_fusion.1
  6.0 0.9 scatter_custom_fusion.1
  6.9 0.9 scatter_custom_fusion
  7.8 0.2 broadcast_in_dim.38
  8.0 0.1 copy.85
  8.1 0.1 copy.86
  8.2 5.7 %collective-permute-done = bf16[48,10,320]{2,0,1:T(8,128)(2,1)S(1)} collective-permute-done((bf16[48,10,320]{2,0,1:T(8,128)(2,1)S(1)}, bf16[48,10,320]{2,0,1:T(8,128)(2,1)S(1)}, u32[]{:S(2)}, u32[]{:S(2)}) %collective-permute-start) | collective-permute-done | bytes 307232 | tf_op jit(solution)/shard_map/ppermute | solution.py:63
  13.9 0.2 fusion.5
  14.2 0.3 pad_maximum_fusion
  14.5 0.1 copy.90
  14.6 0.7 reshape.61
  15.3 2.9 %gather_fusion = bf16[256,3200]{1,0:T(8,128)(2,1)} fusion(bf16[96,3200]{1,0:T(8,128)(2,1)S(1)} %reshape.61, s32[1024]{0:T(1024)S(1)} %pad_clamp_fusion.1), kind=kCustom, calls=%fused_computation | custom fusion | bytes 3277824 | tf_op jit(solution)/shard_map/gather | solution.py:75
  18.1 3.6 %gather.9 = bf16[128,50,128]{2,1,0:T(8,128)(2,1)S(1)} reshape(bf16[256,3200]{1,0:T(8,128)(2,1)} %gather_fusion) | data formatting | bytes 3276800 | tf_op jit(solution)/shard_map/gather | solution.py:75
  21.7 1.3 broadcast_select_fusion
  23.0 37.9 %all_to_all.10 = bf16[128,50,128]{2,1,0:T(8,128)(2,1)S(1)} all-to-all(bf16[128,50,128]{2,1,0:T(8,128)(2,1)S(1)} %broadcast_select_fusion), channel_id=1, replica_groups=mesh['shard'=32,'tensor'=4] {'shard','tensor'}, dimensions={0} | all-to-all | bytes 3276800 | tf_op jit(solution)/shard_map/all_to_all | solution.py:11
  60.9 3.9 %reshape.62 = bf16[32,2,2,2,10,320]{5,4,3,2,1,0:T(8,128)(2,1)} reshape(bf16[128,50,128]{2,1,0:T(8,128)(2,1)S(1)} %all_to_all.10) | data formatting | bytes 3276800 | tf_op jit(solution)/shard_map/reshape | solution.py:77
  64.8 4.7 %copy.91 = bf16[2,32,2,10,2,320]{5,4,3,2,1,0:T(2,128)(2,1)} copy(bf16[2,32,2,10,2,320]{5,3,0,4,2,1:T(8,128)(2,1)} %bitcast.27) | data formatting | bytes 3276800 | tf_op jit(solution)/shard_map/transpose | solution.py:78
  69.5 4.2 %reshape.63 = bf16[2,640,640]{2,1,0:T(8,128)(2,1)S(1)} reshape(bf16[2,32,2,10,2,320]{5,4,3,2,1,0:T(2,128)(2,1)} %copy.91) | data formatting | bytes 3276800 | tf_op jit(solution)/shard_map/reshape | solution.py:78
  73.7 5.4 %fusion.2 = (f32[2]{0:T(128)S(1)}, f32[2,640,640]{2,1,0:T(8,128)}) fusion(bf16[2,640,640]{2,1,0:T(8,128)(2,1)S(1)} %reshape.63, f32[2,640,640]{2,1,0:T(8,128)} %param.15), kind=kLoop, calls=%fused_computation.12 | loop fusion | flops 7372798 | bytes 8192008 | tf_op jit(solution)/shard_map/reduce_sum | solution.py:40
  79.1 6.3 %multiply_reduce_fusion = (f32[2]{0:T(128)S(1)}, f32[2,640,640]{2,1,0:T(8,128)}) fusion(bf16[2,640,640]{2,1,0:T(8,128)(2,1)S(1)} %copy-done, bf16[2,640,640]{2,1,0:T(8,128)(2,1)S(1)} %reshape.63, bf16[2,640,640]{2,1,0:T(8,128)(2,1)} %param.13), kind=kOutput, calls=%fused_computation.11 | convolution fusion | flops 2099609600 | bytes 8192008 | tf_op jit(solution)/shard_map/kij,kjl->kil/dot_general | solution.py:36
  85.5 2.2 %multiply_convert_fusion = bf16[2,640,640]{2,1,0:T(8,128)(2,1)S(1)} fusion(f32[2,640,640]{2,1,0:T(8,128)} %get-tuple-element.29, f32[2]{0:T(128)S(1)} %rsqrt_multiply_fusion), kind=kLoop, calls=%fused_computation.10 | loop fusion | flops 1638400 | bytes 4915208 | tf_op jit(solution)/shard_map/convert_element_type | solution.py:43
  87.7 2.6 %reshape.64 = bf16[2,32,2,10,2,320]{5,4,3,2,1,0:T(2,128)(2,1)} reshape(bf16[2,640,640]{2,1,0:T(8,128)(2,1)S(1)} %multiply_convert_fusion) | data formatting | bytes 3276800 | tf_op jit(solution)/shard_map/reshape | solution.py:81
  90.3 3.9 %copy.135 = bf16[2,32,2,10,2,320]{5,3,0,4,2,1:T(8,128)(2,1)} copy(bf16[2,32,2,10,2,320]{5,4,3,2,1,0:T(2,128)(2,1)} %reshape.64) | data formatting | bytes 3276800 | tf_op jit(solution)/shard_map/reshape | solution.py:81
  94.2 5.9 %reshape.65 = bf16[128,50,128]{2,1,0:T(8,128)(2,1)} reshape(bf16[32,2,2,2,10,320]{5,4,3,2,1,0:T(8,128)(2,1)} %bitcast.28) | data formatting | bytes 3276800 | tf_op jit(solution)/shard_map/reshape | solution.py:84
  100.2 5.9 %all-to-all-start.1 = ((bf16[128,50,128]{2,1,0:T(8,128)(2,1)}), bf16[128,50,128]{2,1,0:T(8,128)(2,1)}, u32[]{:S(2)}, u32[]{:S(2)}) async-start(bf16[128,50,128]{2,1,0:T(8,128)(2,1)} %reshape.65), calls=%async_computation.1 | async-start | bytes 3670016 | tf_op jit(solution)/shard_map/all_to_all | solution.py:16
  106.1 26.6 %all-to-all-done.1 = bf16[128,50,128]{2,1,0:T(8,128)(2,1)} async-done(((bf16[128,50,128]{2,1,0:T(8,128)(2,1)}), bf16[128,50,128]{2,1,0:T(8,128)(2,1)}, u32[]{:S(2)}, u32[]{:S(2)}) %all-to-all-start.1) | async-done | bytes 1638432 | tf_op jit(solution)/shard_map/all_to_all | solution.py:16
  132.7 3.5 %reshape.66 = bf16[256,3200]{1,0:T(8,128)(2,1)S(1)} reshape(bf16[128,50,128]{2,1,0:T(8,128)(2,1)} %all-to-all-done.1) | data formatting | bytes 3276800 | tf_op jit(solution)/shard_map/reshape | solution.py:85
  136.2 1.8 %gather_fusion.1 = bf16[96,3200]{1,0:T(8,128)(2,1)} fusion(bf16[256,3200]{1,0:T(8,128)(2,1)S(1)} %reshape.66, s32[1024]{0:T(1024)S(1)} %pad_clamp_fusion), kind=kCustom, calls=%fused_computation.1 | custom fusion | bytes 1229184 | tf_op jit(solution)/shard_map/gather | solution.py:86
  137.9 2.1 %reshape.67 = bf16[48,2,10,320]{3,2,1,0:T(8,128)(2,1)S(1)} reshape(bf16[96,3200]{1,0:T(8,128)(2,1)} %gather_fusion.1) | data formatting | bytes 1228800 | tf_op jit(solution)/shard_map/reshape | solution.py:86
  140.2 1.0 collective-permute-start.1
  141.2 5.3 %multiply_add_fusion = f32[2,640,640]{2,1,0:T(8,128)} fusion(f32[2,640,640]{2,1,0:T(8,128)} %param.12, bf16[2,640,640]{2,1,0:T(8,128)(2,1)S(1)} %reshape.63), kind=kOutput, calls=%fused_computation.8 | convolution fusion | flops 1051033600 | bytes 8192000 | tf_op jit(solution)/shard_map/kji,kjl->kil/dot_general | solution.py:25
  146.5 6.0 %collective-permute-done.1 = bf16[48,10,320]{2,0,1:T(8,128)(2,1)S(1)} collective-permute-done((bf16[48,10,320]{2,0,1:T(8,128)(2,1)S(1)}, bf16[48,10,320]{2,0,1:T(8,128)(2,1)S(1)}, u32[]{:S(2)}, u32[]{:S(2)}) %collective-permute-start.1) | collective-permute-done | bytes 307232 | tf_op jit(solution)/shard_map/ppermute | solution.py:89
  152.5 0.2 copy_select_fusion.3
  152.7 0.8 multiply_reduce_fusion.1
  153.5 0.6 collective-permute-start.2
  154.2 2.1 %collective-permute-start.3 = (f32[48,20]{1,0:T(8,128)S(1)}, f32[48,20]{1,0:T(8,128)S(1)}, u32[]{:S(2)}, u32[]{:S(2)}) collective-permute-start(f32[48,20]{1,0:T(8,128)S(1)} %multiply_reduce_fusion.1), channel_id=1, source_target_pairs={{0,2},{1,3},{2,0},{3,1},{4,6},{5,7},{6,4},{7,5},{8,10},{9,11},{10,... | collective-permute-start | bytes 11528 | tf_op jit(solution)/shard_map/ppermute | solution.py:96
  156.3 3.5 %multiply_add_fusion.1 = f32[2,640,640]{2,1,0:T(8,128)} fusion(f32[2,640,640]{2,1,0:T(8,128)S(1)} %copy-done.5, bf16[2,640,640]{2,1,0:T(8,128)(2,1)S(1)} %reshape.63), kind=kOutput, calls=%fused_computation.9 | convolution fusion | flops 1051033600 | bytes 8192000 | tf_op jit(solution)/shard_map/kij,klj->kil/dot_general | solution.py:21
  159.8 0.1 copy.99
  159.8 0.1 copy.100
  159.9 0.1 copy.101
  160.0 1.3 collective-permute-done.4
  161.3 0.1 copy.102
  161.4 0.1 concatenate.9
  161.7 0.1 copy.113
  161.8 2.5 %fusion.3 = f32[48,20,320]{2,1,0:T(8,128)S(1)} fusion(f32[48,20,320]{2,0,1:T(8,128)} %param.8, f32[48,20]{1,0:T(8,128)S(1)} %bitcast.30, bf16[48,10,320]{2,1,0:T(8,128)(2,1)} %copy-done.4, bf16[48,10,320]{2,1,0:T(8,128)(2,1)} %copy-done.3), kind=kLoop, calls=%fused_computation.19 | loop fusion | flops 2150400 | bytes 3075840 | tf_op jit(solution)/shard_map/mul | solution.py:104
  164.3 1.4 copy.109
  (30 shorter events, 0.4 us)
Async XLA Ops:
  0.6 78.5 %copy-start = (bf16[2,640,640]{2,1,0:T(8,128)(2,1)S(1)}, bf16[2,640,640]{2,1,0:T(8,128)(2,1)}, u32[]{:S(2)}) copy-start(bf16[2,640,640]{2,1,0:T(8,128)(2,1)} %param.14) | copy-start | bytes 4915204
  2.0 12.0 %collective-permute-start = (bf16[48,10,320]{2,0,1:T(8,128)(2,1)S(1)}, bf16[48,10,320]{2,0,1:T(8,128)(2,1)S(1)}, u32[]{:S(2)}, u32[]{:S(2)}) collective-permute-start(bf16[48,10,320]{2,0,1:T(8,128)(2,1)S(1)} %get-tuple-element.26), channel_id=1, source_target_pairs={{0,2},{1,3},{2,0},{3,1},{4,6},{5,7},{6,4},{7,5},{8,10},{9,11},{10,... | collective-permute-start | bytes 921608 | tf_op jit(solution)/shard_map/ppermute | solution.py:63
  100.2 32.5 %all-to-all-start.1 = ((bf16[128,50,128]{2,1,0:T(8,128)(2,1)}), bf16[128,50,128]{2,1,0:T(8,128)(2,1)}, u32[]{:S(2)}, u32[]{:S(2)}) async-start(bf16[128,50,128]{2,1,0:T(8,128)(2,1)} %reshape.65), calls=%async_computation.1 | async-start | bytes 3670016 | tf_op jit(solution)/shard_map/all_to_all | solution.py:16
  140.2 12.3 %collective-permute-start.1 = (bf16[48,10,320]{2,0,1:T(8,128)(2,1)S(1)}, bf16[48,10,320]{2,0,1:T(8,128)(2,1)S(1)}, u32[]{:S(2)}, u32[]{:S(2)}) collective-permute-start(bf16[48,10,320]{2,0,1:T(8,128)(2,1)S(1)} %copy.95), channel_id=1, source_target_pairs={{0,2},{1,3},{2,0},{3,1},{4,6},{5,7},{6,4},{7,5},{8,10},{9,11},{10,... | collective-permute-start | bytes 921608 | tf_op jit(solution)/shard_map/ppermute | solution.py:89
  146.5 6.2 %copy-start.2 = (f32[48,20,320]{2,0,1:T(8,128)S(1)}, f32[48,20,320]{2,0,1:T(8,128)}, u32[]{:S(2)}) copy-start(f32[48,20,320]{2,0,1:T(8,128)} %param.8) | copy-start | bytes 3686404
  152.5 3.8 %copy-start.5 = (f32[2,640,640]{2,1,0:T(8,128)S(1)}, f32[2,640,640]{2,1,0:T(8,128)}, u32[]{:S(2)}) copy-start(f32[2,640,640]{2,1,0:T(8,128)} %param.11) | copy-start | bytes 9830404
  152.7 0.8 copy-start.3
  152.7 1.4 copy-start.4
  153.5 6.3 %collective-permute-start.2 = (f32[48,20]{1,0:T(8,128)S(1)}, f32[48,20]{1,0:T(8,128)S(1)}, u32[]{:S(2)}, u32[]{:S(2)}) collective-permute-start(f32[48,20]{1,0:T(8,128)S(1)} %multiply_reduce_fusion.1), channel_id=1, source_target_pairs={{0,3},{1,0},{2,1},{3,2},{4,7},{5,4},{6,5},{7,6},{8,11},{9,8},{10,9... | collective-permute-start | bytes 11528 | tf_op jit(solution)/shard_map/ppermute | solution.py:96
  154.2 5.8 %collective-permute-start.3 = (f32[48,20]{1,0:T(8,128)S(1)}, f32[48,20]{1,0:T(8,128)S(1)}, u32[]{:S(2)}, u32[]{:S(2)}) collective-permute-start(f32[48,20]{1,0:T(8,128)S(1)} %multiply_reduce_fusion.1), channel_id=1, source_target_pairs={{0,2},{1,3},{2,0},{3,1},{4,6},{5,7},{6,4},{7,5},{8,10},{9,11},{10,... | collective-permute-start | bytes 11528 | tf_op jit(solution)/shard_map/ppermute | solution.py:96
  156.3 5.0 %collective-permute-start.4 = (f32[48,20]{1,0:T(8,128)S(1)}, f32[48,20]{1,0:T(8,128)S(1)}, u32[]{:S(2)}, u32[]{:S(2)}) collective-permute-start(f32[48,20]{1,0:T(8,128)S(1)} %multiply_reduce_fusion.1), channel_id=1, source_target_pairs={{0,1},{1,2},{2,3},{3,0},{4,5},{5,6},{6,7},{7,4},{8,9},{9,10},{10,1... | collective-permute-start | bytes 11528 | tf_op jit(solution)/shard_map/ppermute | solution.py:96
  161.8 3.9 %copy-start.1 = (bf16[2,640,640]{2,1,0:T(8,128)(2,1)S(1)}, bf16[2,640,640]{2,1,0:T(8,128)(2,1)}, u32[]{:S(2)}) copy-start(bf16[2,640,640]{2,1,0:T(8,128)(2,1)} %param.14) | copy-start | bytes 4915204

commit v7 on v4

--- a/solution.py
+++ b/solution.py
@@ -21,10 +21,10 @@
     gram_left = jnp.einsum(
         "kij,klj->kil", block_grads, block_grads, preferred_element_type=jnp.float32
     )
+    new_left = stat_decay * left_stats + (1.0 - stat_decay) * gram_left
     gram_right = jnp.einsum(
         "kji,kjl->kil", block_grads, block_grads, preferred_element_type=jnp.float32
     )
-    new_left = stat_decay * left_stats + (1.0 - stat_decay) * gram_left
     new_right = stat_decay * right_stats + (1.0 - stat_decay) * gram_right
     return (new_left, new_right)
 
@@ -44,7 +44,7 @@
     return (delta, new_moment)
 
 
-def body(weights, grads, owner_slot, left_stats, right_stats, left_root, right_root, moment):
+def body_steps(weights, grads, owner_slot, left_stats, right_stats, left_root, right_root, moment):
     n_shard = lax.axis_size("shard")
     n_tensor = lax.axis_size("tensor")
     row_blocks, shard_rows, shard_cols = grads.shape
@@ -68,11 +68,11 @@
     chunk = slots * slab_size
     lanes = 128 if chunk % 128 == 0 else chunk
     slabs = jnp.stack([first, second], axis=1).reshape(row_blocks * col_blocks, slab_size)
-    slot_block = jnp.zeros((total_slots,), jnp.int32).at[owner_slot].set(
+    slot_block = jnp.full((total_slots,), block_count, jnp.int32).at[owner_slot].set(
         jnp.arange(block_count, dtype=jnp.int32)
     )
-    slot_used = jnp.zeros((total_slots,), jnp.bool_).at[owner_slot].set(True)
-    outgoing = jnp.where(slot_used[:, None], slabs[slot_block], jnp.zeros((), jnp.bfloat16))
+    slabs = jnp.concatenate([slabs, jnp.zeros((1, slab_size), jnp.bfloat16)], axis=0)
+    outgoing = slabs[slot_block]
     arrived = route_out(outgoing.reshape(owners, chunk // lanes, lanes))
     arrived = arrived.reshape(n_shard, col_blocks, per_block, slots, half, shard_cols)
     block_grads = arrived.transpose(3, 0, 1, 4, 2, 5).reshape(slots, order_size, order_size)
@@ -113,7 +113,7 @@
         P(("shard", "tensor"), None, None),
     )
     return jax.shard_map(
-        body,
+        body_steps,
         mesh=mesh,
         in_specs=placed,
         out_specs=(

time: 166 us -> 176 us (1.060)
  local copies, waits for them, and re-layouts: 45 us -> 52.4 us
    reshape x8 -> x9, local copies, waits for them, and re-layouts: 26.8 us -> 36.7 us  [the longest x2 9.23 us: body_steps(): delta.reshape(slots, n_shard, col_blocks, half, per_block, shard_cols)]
    gather x3 -> x2, local copies, waits for them, and re-layouts: 8.2 us -> 6.87 us  [the longest x1 4.01 us: body_steps(): returned[owner_slot].reshape(row_blocks, col_blocks, half, shard_cols)]
  transfers between devices with their start and end apart: 5 -> 5, of which waited for: 4 -> 4; matrix products, arithmetic and copies ran while one was open for 6% -> 5% of each run, Pallas kernels for 0% -> 0%
where the time goes in v7:
time: 176 us; the launch traced here: 175 us
  local copies, waits for them, and re-layouts  52.4 us (30%)
  waiting for transfers between devices  45.6 us (26%)
  blocking collectives  38 us (22%)
  matrix products  13.3 us (8%)
  other arithmetic  13.2 us (8%)
  starting transfers between devices  12 us (7%)
    all_to_all x1, blocking collectives, route_out(): lax.all_to_all(outgoing, ('shard', 'tensor'), split_axis=0, concat_axis=0...  38 us
    all_to_all x1, waiting for transfers between devices, route_back(): lax.all_to_all(outgoing, ('shard', 'tensor'), split_axis=0, concat_axis=0...  26.6 us
    ppermute x1, waiting for transfers between devices, body_steps(): other_back = lax.ppermute(other_part, 'tensor', partner)  11.3 us
    reshape x2, local copies, waits for them, and re-layouts, body_steps(): delta.reshape(slots, n_shard, col_blocks, half, per_block, shard_cols)  9.23 us
    ppermute x1, waiting for transfers between devices, body_steps(): got = lax.ppermute(give, 'tensor', partner)  7.02 us
    dot_general x1, matrix products, direction(): jnp.einsum('kij,kjl->kil', half, right_root, preferred_element_type=jnp.f...  6.34 us
    reshape x1, local copies, waits for them, and re-layouts, body_steps(): arrived.reshape(n_shard, col_blocks, per_block, slots, half, shard_cols)  6.03 us
    reshape x1, local copies, waits for them, and re-layouts, body_steps(): sendback = pieces.reshape(owners, chunk // lanes, lanes)  5.93 us
  transfers between devices with their start and end apart: 5, of which 4 were waited for; matrix products, arithmetic and copies ran while one was open for 5% of the time, Pallas kernels for 0%

profile of v7, /device:TPU:0, one launch (start us, length us, event | category | flops | bytes accessed | tf_op | source)
XLA Modules:
  0.0 175.3 jit_solution(3993127914422564046)
XLA Ops:
  0.6 0.0 copy-start
  0.7 1.3 constant_dynamic-slice_fusion
  2.0 3.4 %collective-permute-start = (bf16[48,10,320]{2,0,1:T(8,128)(2,1)S(1)}, bf16[48,10,320]{2,0,1:T(8,128)(2,1)S(1)}, u32[]{:S(2)}, u32[]{:S(2)}) collective-permute-start(bf16[48,10,320]{2,0,1:T(8,128)(2,1)S(1)} %get-tuple-element.22), channel_id=1, source_target_pairs={{0,2},{1,3},{2,0},{3,1},{4,6},{5,7},{6,4},{7,5},{8,10},{9,11},{10,... | collective-permute-start | bytes 921608 | tf_op jit(solution)/shard_map/ppermute | solution.py:63
  5.4 0.7 compare_select_fusion.1
  6.0 0.9 scatter_custom_fusion
  6.9 7.0 %collective-permute-done = bf16[48,10,320]{2,0,1:T(8,128)(2,1)S(1)} collective-permute-done((bf16[48,10,320]{2,0,1:T(8,128)(2,1)S(1)}, bf16[48,10,320]{2,0,1:T(8,128)(2,1)S(1)}, u32[]{:S(2)}, u32[]{:S(2)}) %collective-permute-start) | collective-permute-done | bytes 307232 | tf_op jit(solution)/shard_map/ppermute | solution.py:63
  13.9 0.2 fusion.5
  14.2 0.3 pad_maximum_fusion
  14.5 0.1 copy.54
  14.6 0.7 reshape.47
  15.3 2.9 %gather_fusion = bf16[256,3200]{1,0:T(8,128)(2,1)} fusion(bf16[97,3200]{1,0:T(8,128)(2,1)S(1)} %concatenate.6, s32[1024]{0:T(1024)S(1)} %pad_clamp_fusion.1), kind=kCustom, calls=%fused_computation | custom fusion | bytes 3277824 | tf_op jit(solution)/shard_map/gather | solution.py:75
  18.2 3.6 %reshape.48 = bf16[128,50,128]{2,1,0:T(8,128)(2,1)S(1)} reshape(bf16[256,3200]{1,0:T(8,128)(2,1)} %gather_fusion) | data formatting | bytes 3276800 | tf_op jit(solution)/shard_map/reshape | solution.py:76
  21.8 38.0 %all_to_all.10 = bf16[128,50,128]{2,1,0:T(8,128)(2,1)} all-to-all(bf16[128,50,128]{2,1,0:T(8,128)(2,1)S(1)} %reshape.48), channel_id=1, replica_groups=mesh['shard'=32,'tensor'=4] {'shard','tensor'}, dimensions={0} | all-to-all | bytes 3276800 | tf_op jit(solution)/shard_map/all_to_all | solution.py:11
  59.7 6.0 %reshape.49 = bf16[32,2,2,2,10,320]{5,4,3,2,1,0:T(8,128)(2,1)} reshape(bf16[128,50,128]{2,1,0:T(8,128)(2,1)} %all_to_all.10) | data formatting | bytes 3276800 | tf_op jit(solution)/shard_map/reshape | solution.py:77
  65.8 4.7 %copy.55 = bf16[2,32,2,10,2,320]{5,4,3,2,1,0:T(2,128)(2,1)} copy(bf16[2,32,2,10,2,320]{5,3,0,4,2,1:T(8,128)(2,1)} %bitcast.20) | data formatting | bytes 3276800 | tf_op jit(solution)/shard_map/transpose | solution.py:78
  70.5 4.2 %reshape.50 = bf16[2,640,640]{2,1,0:T(8,128)(2,1)S(1)} reshape(bf16[2,32,2,10,2,320]{5,4,3,2,1,0:T(2,128)(2,1)} %copy.55) | data formatting | bytes 3276800 | tf_op jit(solution)/shard_map/reshape | solution.py:78
  74.7 5.4 %fusion.2 = (f32[2]{0:T(128)S(1)}, f32[2,640,640]{2,1,0:T(8,128)}) fusion(bf16[2,640,640]{2,1,0:T(8,128)(2,1)S(1)} %reshape.50, f32[2,640,640]{2,1,0:T(8,128)} %param.15), kind=kLoop, calls=%fused_computation.11 | loop fusion | flops 7372798 | bytes 8192008 | tf_op jit(solution)/shard_map/reduce_sum | solution.py:40
  80.1 0.0 copy-done
  80.1 6.3 %multiply_reduce_fusion = (f32[2]{0:T(128)S(1)}, f32[2,640,640]{2,1,0:T(8,128)}) fusion(bf16[2,640,640]{2,1,0:T(8,128)(2,1)S(1)} %copy-done, bf16[2,640,640]{2,1,0:T(8,128)(2,1)S(1)} %reshape.50, bf16[2,640,640]{2,1,0:T(8,128)(2,1)} %param.13), kind=kOutput, calls=%fused_computation.10 | convolution fusion | flops 2099609600 | bytes 8192008 | tf_op jit(solution)/shard_map/kij,kjl->kil/dot_general | solution.py:36
  86.5 3.4 %multiply_convert_fusion = bf16[2,640,640]{2,1,0:T(8,128)(2,1)} fusion(f32[2,640,640]{2,1,0:T(8,128)} %get-tuple-element.25, f32[2]{0:T(128)S(1)} %rsqrt_multiply_fusion), kind=kLoop, calls=%fused_computation.9 | loop fusion | flops 1638400 | bytes 4915208 | tf_op jit(solution)/shard_map/convert_element_type | solution.py:43
  89.9 5.3 %reshape.51 = bf16[2,32,2,10,2,320]{5,4,3,2,1,0:T(2,128)(2,1)} reshape(bf16[2,640,640]{2,1,0:T(8,128)(2,1)} %multiply_convert_fusion) | data formatting | bytes 3276800 | tf_op jit(solution)/shard_map/reshape | solution.py:81
  95.2 3.9 %copy.89 = bf16[2,32,2,10,2,320]{5,3,0,4,2,1:T(8,128)(2,1)} copy(bf16[2,32,2,10,2,320]{5,4,3,2,1,0:T(2,128)(2,1)} %reshape.51) | data formatting | bytes 3276800 | tf_op jit(solution)/shard_map/reshape | solution.py:81
  99.1 5.9 %reshape.52 = bf16[128,50,128]{2,1,0:T(8,128)(2,1)} reshape(bf16[32,2,2,2,10,320]{5,4,3,2,1,0:T(8,128)(2,1)} %bitcast.21) | data formatting | bytes 3276800 | tf_op jit(solution)/shard_map/reshape | solution.py:84
  105.0 5.7 %all-to-all-start.1 = ((bf16[128,50,128]{2,1,0:T(8,128)(2,1)}), bf16[128,50,128]{2,1,0:T(8,128)(2,1)}, u32[]{:S(2)}, u32[]{:S(2)}) async-start(bf16[128,50,128]{2,1,0:T(8,128)(2,1)} %reshape.52), calls=%async_computation.1 | async-start | bytes 3670016 | tf_op jit(solution)/shard_map/all_to_all | solution.py:16
  110.8 26.6 %all-to-all-done.1 = bf16[128,50,128]{2,1,0:T(8,128)(2,1)} async-done(((bf16[128,50,128]{2,1,0:T(8,128)(2,1)}), bf16[128,50,128]{2,1,0:T(8,128)(2,1)}, u32[]{:S(2)}, u32[]{:S(2)}) %all-to-all-start.1) | async-done | bytes 1638432 | tf_op jit(solution)/shard_map/all_to_all | solution.py:16
  137.3 4.3 %reshape.53 = bf16[256,3200]{1,0:T(8,128)(2,1)} reshape(bf16[128,50,128]{2,1,0:T(8,128)(2,1)} %all-to-all-done.1) | data formatting | bytes 3276800 | tf_op jit(solution)/shard_map/reshape | solution.py:85
  141.6 4.0 %gather_fusion.1 = bf16[96,3200]{1,0:T(8,128)(2,1)} fusion(bf16[256,3200]{1,0:T(8,128)(2,1)} %reshape.53, s32[1024]{0:T(1024)S(1)} %pad_clamp_fusion), kind=kCustom, calls=%fused_computation.1 | custom fusion | bytes 1229184 | tf_op jit(solution)/shard_map/gather | solution.py:86
  145.6 2.8 %reshape.54 = bf16[48,2,10,320]{3,2,1,0:T(8,128)(2,1)} reshape(bf16[96,3200]{1,0:T(8,128)(2,1)} %gather_fusion.1) | data formatting | bytes 1228800 | tf_op jit(solution)/shard_map/reshape | solution.py:86
  148.5 0.0 copy-start.1
  148.5 1.4 select_bitcast_fusion
  149.9 0.0 copy-start.2
  149.9 0.1 copy.59
  150.0 1.0 collective-permute-start.1
  151.0 11.3 %collective-permute-done.1 = bf16[48,10,320]{2,0,1:T(8,128)(2,1)S(1)} collective-permute-done((bf16[48,10,320]{2,0,1:T(8,128)(2,1)S(1)}, bf16[48,10,320]{2,0,1:T(8,128)(2,1)S(1)}, u32[]{:S(2)}, u32[]{:S(2)}) %collective-permute-start.1) | collective-permute-done | bytes 307232 | tf_op jit(solution)/shard_map/ppermute | solution.py:89
  162.3 0.0 copy-done.1
  162.3 0.2 copy_select_fusion.3
  162.5 0.0 copy-done.2
  162.5 0.8 multiply_reduce_fusion.1
  163.3 0.7 collective-permute-start.2
  164.0 0.2 copy-done.3
  164.2 3.5 %multiply_add_fusion = f32[2,640,640]{2,1,0:T(8,128)} fusion(f32[2,640,640]{2,1,0:T(8,128)S(1)} %copy-done.3, bf16[2,640,640]{2,1,0:T(8,128)(2,1)S(1)} %reshape.50), kind=kOutput, calls=%fused_computation.7 | convolution fusion | flops 1051033600 | bytes 8192000 | tf_op jit(solution)/shard_map/kji,kjl->kil/dot_general | solution.py:25
  167.7 0.0 collective-permute-done.2
  167.7 1.2 collective-permute-start.3
  168.9 0.0 copy-done.4
  169.0 3.5 %multiply_add_fusion.1 = f32[2,640,640]{2,1,0:T(8,128)} fusion(f32[2,640,640]{2,1,0:T(8,128)S(1)} %copy-done.4, bf16[2,640,640]{2,1,0:T(8,128)(2,1)S(1)} %reshape.50), kind=kOutput, calls=%fused_computation.8 | convolution fusion | flops 1051033600 | bytes 8192000 | tf_op jit(solution)/shard_map/kij,klj->kil/dot_general | solution.py:21
  172.4 0.7 collective-permute-done.3
  173.1 0.8 fusion.3
  173.9 1.4 copy.64
  (10 shorter events, 0.1 us)
Async XLA Ops:
  0.6 79.5 %copy-start = (bf16[2,640,640]{2,1,0:T(8,128)(2,1)S(1)}, bf16[2,640,640]{2,1,0:T(8,128)(2,1)}, u32[]{:S(2)}) copy-start(bf16[2,640,640]{2,1,0:T(8,128)(2,1)} %param.14) | copy-start | bytes 4915204
  2.0 12.0 %collective-permute-start = (bf16[48,10,320]{2,0,1:T(8,128)(2,1)S(1)}, bf16[48,10,320]{2,0,1:T(8,128)(2,1)S(1)}, u32[]{:S(2)}, u32[]{:S(2)}) collective-permute-start(bf16[48,10,320]{2,0,1:T(8,128)(2,1)S(1)} %get-tuple-element.22), channel_id=1, source_target_pairs={{0,2},{1,3},{2,0},{3,1},{4,6},{5,7},{6,4},{7,5},{8,10},{9,11},{10,... | collective-permute-start | bytes 921608 | tf_op jit(solution)/shard_map/ppermute | solution.py:63
  105.0 32.3 %all-to-all-start.1 = ((bf16[128,50,128]{2,1,0:T(8,128)(2,1)}), bf16[128,50,128]{2,1,0:T(8,128)(2,1)}, u32[]{:S(2)}, u32[]{:S(2)}) async-start(bf16[128,50,128]{2,1,0:T(8,128)(2,1)} %reshape.52), calls=%async_computation.1 | async-start | bytes 3670016 | tf_op jit(solution)/shard_map/all_to_all | solution.py:16
  148.5 13.8 %copy-start.1 = (bf16[48,2,10,320]{3,2,1,0:T(8,128)(2,1)S(1)}, bf16[48,2,10,320]{3,2,1,0:T(8,128)(2,1)}, u32[]{:S(2)}) copy-start(bf16[48,2,10,320]{3,2,1,0:T(8,128)(2,1)} %reshape.54) | copy-start | bytes 1843204
  149.9 12.6 %copy-start.2 = (f32[48,20,320]{2,0,1:T(8,128)S(1)}, f32[48,20,320]{2,0,1:T(8,128)}, u32[]{:S(2)}) copy-start(f32[48,20,320]{2,0,1:T(8,128)} %param.8) | copy-start | bytes 3686404
  150.0 12.3 %collective-permute-start.1 = (bf16[48,10,320]{2,0,1:T(8,128)(2,1)S(1)}, bf16[48,10,320]{2,0,1:T(8,128)(2,1)S(1)}, u32[]{:S(2)}, u32[]{:S(2)}) collective-permute-start(bf16[48,10,320]{2,0,1:T(8,128)(2,1)S(1)} %copy.59), channel_id=1, source_target_pairs={{0,2},{1,3},{2,0},{3,1},{4,6},{5,7},{6,4},{7,5},{8,10},{9,11},{10,... | collective-permute-start | bytes 921608 | tf_op jit(solution)/shard_map/ppermute | solution.py:89
  162.3 1.9 %copy-start.3 = (f32[2,640,640]{2,1,0:T(8,128)S(1)}, f32[2,640,640]{2,1,0:T(8,128)}, u32[]{:S(2)}) copy-start(f32[2,640,640]{2,1,0:T(8,128)} %param.12) | copy-start | bytes 9830404
  163.3 4.4 %collective-permute-start.2 = (f32[48,20]{1,0:T(8,128)S(1)}, f32[48,20]{1,0:T(8,128)S(1)}, u32[]{:S(2)}, u32[]{:S(2)}) collective-permute-start(f32[48,20]{1,0:T(8,128)S(1)} %multiply_reduce_fusion.1), channel_id=1, source_target_pairs={{0,1},{1,0},{2,3},{3,2},{4,5},{5,4},{6,7},{7,6},{8,9},{9,8},{10,11... | collective-permute-start | bytes 11528 | tf_op jit(solution)/shard_map/ppermute | solution.py:98
  164.2 4.7 %copy-start.4 = (f32[2,640,640]{2,1,0:T(8,128)S(1)}, f32[2,640,640]{2,1,0:T(8,128)}, u32[]{:S(2)}) copy-start(f32[2,640,640]{2,1,0:T(8,128)} %param.11) | copy-start | bytes 9830404
  167.7 5.4 %collective-permute-start.3 = (f32[48,20]{1,0:T(8,128)S(1)}, f32[48,20]{1,0:T(8,128)S(1)}, u32[]{:S(2)}, u32[]{:S(2)}) collective-permute-start(f32[48,20]{1,0:T(8,128)S(1)} %add.62), channel_id=1, source_target_pairs={{0,2},{1,3},{2,0},{3,1},{4,6},{5,7},{6,4},{7,5},{8,10},{9,11},{10,... | collective-permute-start | bytes 11528 | tf_op jit(solution)/shard_map/ppermute | solution.py:98

commit v8 on v7

--- a/solution.py
+++ b/solution.py
@@ -57,7 +57,7 @@
     total_slots = owners * slots
     half = shard_rows // col_blocks
     mine_col = lax.axis_index("tensor") // per_block
-    partner = [(i, (i + per_block) % n_tensor) for i in range(n_tensor)]
+    partner = [(i, n_tensor - 1 - i) for i in range(n_tensor)]
     keep = lax.dynamic_slice_in_dim(grads, mine_col * half, half, axis=1)
     give = lax.dynamic_slice_in_dim(grads, (1 - mine_col) * half, half, axis=1)
     got = lax.ppermute(give, "tensor", partner)
@@ -68,19 +68,24 @@
     chunk = slots * slab_size
     lanes = 128 if chunk % 128 == 0 else chunk
     slabs = jnp.stack([first, second], axis=1).reshape(row_blocks * col_blocks, slab_size)
-    slot_block = jnp.full((total_slots,), block_count, jnp.int32).at[owner_slot].set(
+    slot_block = jnp.zeros((total_slots,), jnp.int32).at[owner_slot].set(
         jnp.arange(block_count, dtype=jnp.int32)
     )
-    slabs = jnp.concatenate([slabs, jnp.zeros((1, slab_size), jnp.bfloat16)], axis=0)
-    outgoing = slabs[slot_block]
+    slot_used = jnp.zeros((total_slots,), jnp.bool_).at[owner_slot].set(True)
+    outgoing = jnp.where(slot_used[:, None], slabs[slot_block], jnp.zeros((), jnp.bfloat16))
     arrived = route_out(outgoing.reshape(owners, chunk // lanes, lanes))
     arrived = arrived.reshape(n_shard, col_blocks, per_block, slots, half, shard_cols)
+    my_slots = lax.axis_index(("shard", "tensor")) * slots + jnp.arange(slots)
+    slot_col = slot_block[my_slots] % col_blocks
+    flip = (jnp.arange(col_blocks)[:, None] != slot_col[None, :])[None, :, None, :, None, None]
+    arrived = jnp.where(flip, arrived[:, :, ::-1], arrived)
     block_grads = arrived.transpose(3, 0, 1, 4, 2, 5).reshape(slots, order_size, order_size)
     new_left, new_right = refresh(block_grads, left_stats, right_stats)
     delta, new_moment = direction(block_grads, left_root, right_root, moment)
     pieces = delta.reshape(slots, n_shard, col_blocks, half, per_block, shard_cols).transpose(
         1, 2, 4, 0, 3, 5
     )
+    pieces = jnp.where(flip, pieces[:, :, ::-1], pieces)
     sendback = pieces.reshape(owners, chunk // lanes, lanes)
     returned = route_back(sendback).reshape(total_slots, slab_size)
     back = returned[owner_slot].reshape(row_blocks, col_blocks, half, shard_cols)

time: 176 us -> 171 us (0.972)
  blocking collectives: 38 us -> 0 us
  waiting for transfers between devices: 45.6 us -> 69.6 us
  starting transfers between devices: 12 us -> 22.7 us
  local copies, waits for them, and re-layouts: 52.4 us -> 42.8 us
  other arithmetic: 13.2 us -> 20.6 us
    all_to_all x1 -> x0, blocking collectives: 38 us -> none  [route_out(): lax.all_to_all(outgoing, ('shard', 'tensor'), split_axis=0, concat_axis=0...]
    all_to_all x0 -> x1, waiting for transfers between devices: none -> 26.1 us  [route_out(): lax.all_to_all(outgoing, ('shard', 'tensor'), split_axis=0, concat_axis=0...]
    all_to_all x0 -> x1, starting transfers between devices: none -> 11 us  [route_out(): lax.all_to_all(outgoing, ('shard', 'tensor'), split_axis=0, concat_axis=0...]
    select_n x2 -> x6, other arithmetic: 0.66 us -> 6.43 us  [the longest x1 3.27 us: body_steps(): pieces = jnp.where(flip, pieces[:, :, ::-1], pieces)]
    reshape x2, local copies, waits for them, and re-layouts: 9.23 us -> 4.83 us  [body_steps(): delta.reshape(slots, n_shard, col_blocks, half, per_block, shard_cols)]
    gather x1 -> x3, local copies, waits for them, and re-layouts: 2.86 us -> 7.06 us  [the longest x2 6.42 us: body_steps(): slabs[slot_block]]
    transpose x0 -> x1, other arithmetic: none -> 4.12 us  [body_steps(): arrived.transpose(3, 0, 1, 4, 2, 5).reshape(slots, order_size, order_size)]
    reshape x1 -> x0, local copies, waits for them, and re-layouts: 3.56 us -> none  [body_steps(): arrived = route_out(outgoing.reshape(owners, chunk // lanes, lanes))]
  transfers between devices with their start and end apart: 5 -> 6, of which waited for: 4 -> 5; matrix products, arithmetic and copies ran while one was open for 5% -> 6% of each run, Pallas kernels for 0% -> 0%
where the time goes in v8:
time: 171 us; the launch traced here: 170 us
  waiting for transfers between devices  69.6 us (41%)
  local copies, waits for them, and re-layouts  42.8 us (25%)
  starting transfers between devices  22.7 us (13%)
  other arithmetic  20.6 us (12%)
  matrix products  13.3 us (8%)
    all_to_all x1, waiting for transfers between devices, route_back(): lax.all_to_all(outgoing, ('shard', 'tensor'), split_axis=0, concat_axis=0...  26.6 us
    all_to_all x1, waiting for transfers between devices, route_out(): lax.all_to_all(outgoing, ('shard', 'tensor'), split_axis=0, concat_axis=0...  26.1 us
    all_to_all x1, starting transfers between devices, route_out(): lax.all_to_all(outgoing, ('shard', 'tensor'), split_axis=0, concat_axis=0...  11 us
    ppermute x1, waiting for transfers between devices, body_steps(): other_back = lax.ppermute(other_part, 'tensor', partner)  10.6 us
    gather x2, local copies, waits for them, and re-layouts, body_steps(): slabs[slot_block]  6.42 us
    dot_general x1, matrix products, direction(): jnp.einsum('kij,kjl->kil', half, right_root, preferred_element_type=jnp.f...  6.34 us
    reshape x1, local copies, waits for them, and re-layouts, body_steps(): sendback = pieces.reshape(owners, chunk // lanes, lanes)  5.93 us
    all_to_all x1, starting transfers between devices, route_back(): lax.all_to_all(outgoing, ('shard', 'tensor'), split_axis=0, concat_axis=0...  5.71 us
  transfers between devices with their start and end apart: 6, of which 5 were waited for; matrix products, arithmetic and copies ran while one was open for 6% of the time, Pallas kernels for 0%

profile of v8, /device:TPU:0, one launch (start us, length us, event | category | flops | bytes accessed | tf_op | source)
XLA Modules:
  0.0 169.8 jit_solution(17036556115191989074)
XLA Ops:
  0.7 1.3 constant_dynamic-slice_fusion
  2.0 3.2 %collective-permute-start = (bf16[48,10,320]{2,0,1:T(8,128)(2,1)S(1)}, bf16[48,10,320]{2,0,1:T(8,128)(2,1)S(1)}, u32[]{:S(2)}, u32[]{:S(2)}) collective-permute-start(bf16[48,10,320]{2,0,1:T(8,128)(2,1)S(1)} %get-tuple-element.18), channel_id=1, source_target_pairs={{0,3},{1,2},{2,1},{3,0},{4,7},{5,6},{6,5},{7,4},{8,11},{9,10},{10,... | collective-permute-start | bytes 921608 | tf_op jit(solution)/shard_map/ppermute | solution.py:63
  5.2 0.7 compare_select_fusion.2
  5.8 0.9 scatter_custom_fusion
  6.7 0.9 scatter_custom_fusion.1
  7.6 0.2 broadcast_in_dim.54
  7.8 0.1 copy.30
  7.9 0.1 copy.31
  8.1 5.7 %collective-permute-done = bf16[48,10,320]{2,0,1:T(8,128)(2,1)S(1)} collective-permute-done((bf16[48,10,320]{2,0,1:T(8,128)(2,1)S(1)}, bf16[48,10,320]{2,0,1:T(8,128)(2,1)S(1)}, u32[]{:S(2)}, u32[]{:S(2)}) %collective-permute-start) | collective-permute-done | bytes 307232 | tf_op jit(solution)/shard_map/ppermute | solution.py:63
  13.8 0.2 fusion.6
  14.0 0.3 pad_maximum_fusion
  14.3 0.1 copy.35
  14.4 0.7 reshape.100
  15.1 2.9 %gather_fusion.1 = bf16[256,3200]{1,0:T(8,128)(2,1)} fusion(bf16[96,3200]{1,0:T(8,128)(2,1)S(1)} %reshape.100, s32[1024]{0:T(1024)S(1)} %pad_clamp_fusion.1), kind=kCustom, calls=%fused_computation.1 | custom fusion | bytes 3277824 | tf_op jit(solution)/shard_map/gather | solution.py:75
  18.0 3.6 %gather.13 = bf16[128,50,128]{2,1,0:T(8,128)(2,1)S(1)} reshape(bf16[256,3200]{1,0:T(8,128)(2,1)} %gather_fusion.1) | data formatting | bytes 3276800 | tf_op jit(solution)/shard_map/gather | solution.py:75
  21.6 2.5 %broadcast_select_fusion = bf16[128,50,128]{2,1,0:T(8,128)(2,1)} fusion(bf16[128,50,128]{2,1,0:T(8,128)(2,1)S(1)} %gather.13, pred[128,50]{1,0:T(8,128)(4,1)S(1)} %copy.31), kind=kLoop, calls=%fused_computation.18 | loop fusion | flops 819200 | bytes 3283200 | tf_op jit(solution)/shard_map/jit(_where)/select_n | solution.py:75
  24.1 11.0 %all-to-all-start = ((bf16[128,50,128]{2,1,0:T(8,128)(2,1)}), bf16[128,50,128]{2,1,0:T(8,128)(2,1)S(1)}, u32[]{:S(2)}, u32[]{:S(2)}) async-start(bf16[128,50,128]{2,1,0:T(8,128)(2,1)} %broadcast_select_fusion), calls=%async_computation | async-start | bytes 3670016 | tf_op jit(solution)/shard_map/all_to_all | solution.py:11
  35.1 0.6 gather_fusion
  35.8 26.1 %all-to-all-done = bf16[128,50,128]{2,1,0:T(8,128)(2,1)S(1)} async-done(((bf16[128,50,128]{2,1,0:T(8,128)(2,1)}), bf16[128,50,128]{2,1,0:T(8,128)(2,1)S(1)}, u32[]{:S(2)}, u32[]{:S(2)}) %all-to-all-start) | async-done | bytes 1638432 | tf_op jit(solution)/shard_map/all_to_all | solution.py:11
  61.8 3.9 %reshape.101 = bf16[32,2,2,2,10,320]{5,4,3,2,1,0:T(8,128)(2,1)} reshape(bf16[128,50,128]{2,1,0:T(8,128)(2,1)S(1)} %all-to-all-done) | data formatting | bytes 3276800 | tf_op jit(solution)/shard_map/reshape | solution.py:77
  65.8 4.1 %fusion.3 = bf16[2,32,2,10,2,320]{5,3,0,4,2,1:T(8,128)(2,1)S(1)} fusion(bf16[32,2,2,2,10,320]{5,4,3,2,1,0:T(8,128)(2,1)} %reshape.101, pred[2,2]{1,0:T(4,128)(4,1)S(1)} %iota_compare_fusion), kind=kLoop, calls=%fused_computation.16 | loop fusion | flops 819200 | bytes 3276804 | tf_op jit(solution)/shard_map/transpose | solution.py:82
  69.9 2.8 %copy.36 = bf16[2,32,2,10,2,320]{5,4,3,2,1,0:T(2,128)(2,1)} copy(bf16[2,32,2,10,2,320]{5,3,0,4,2,1:T(8,128)(2,1)S(1)} %fusion.3) | data formatting | bytes 3276800 | tf_op jit(solution)/shard_map/transpose | solution.py:82
  72.7 4.2 %reshape.102 = bf16[2,640,640]{2,1,0:T(8,128)(2,1)S(1)} reshape(bf16[2,32,2,10,2,320]{5,4,3,2,1,0:T(2,128)(2,1)} %copy.36) | data formatting | bytes 3276800 | tf_op jit(solution)/shard_map/reshape | solution.py:82
  76.9 5.4 %fusion.2 = (f32[2]{0:T(128)S(1)}, f32[2,640,640]{2,1,0:T(8,128)}) fusion(bf16[2,640,640]{2,1,0:T(8,128)(2,1)S(1)} %reshape.102, f32[2,640,640]{2,1,0:T(8,128)} %param.15), kind=kLoop, calls=%fused_computation.15 | loop fusion | flops 7372798 | bytes 8192008 | tf_op jit(solution)/shard_map/reduce_sum | solution.py:40
  82.4 6.3 %multiply_reduce_fusion = (f32[2]{0:T(128)S(1)}, f32[2,640,640]{2,1,0:T(8,128)}) fusion(bf16[2,640,640]{2,1,0:T(8,128)(2,1)S(1)} %copy-done, bf16[2,640,640]{2,1,0:T(8,128)(2,1)S(1)} %reshape.102, bf16[2,640,640]{2,1,0:T(8,128)(2,1)} %param.13), kind=kOutput, calls=%fused_computation.14 | convolution fusion | flops 2099609600 | bytes 8192008 | tf_op jit(solution)/shard_map/kij,kjl->kil/dot_general | solution.py:36
  88.7 2.2 %multiply_convert_fusion = bf16[2,640,640]{2,1,0:T(8,128)(2,1)S(1)} fusion(f32[2,640,640]{2,1,0:T(8,128)} %get-tuple-element.21, f32[2]{0:T(128)S(1)} %rsqrt_multiply_fusion), kind=kLoop, calls=%fused_computation.13 | loop fusion | flops 1638400 | bytes 4915208 | tf_op jit(solution)/shard_map/convert_element_type | solution.py:43
  91.0 2.6 %reshape.103 = bf16[2,32,2,10,2,320]{5,4,3,2,1,0:T(2,128)(2,1)} reshape(bf16[2,640,640]{2,1,0:T(8,128)(2,1)S(1)} %multiply_convert_fusion) | data formatting | bytes 3276800 | tf_op jit(solution)/shard_map/reshape | solution.py:85
  93.5 2.3 %copy.70 = bf16[2,32,2,10,2,320]{5,3,0,4,2,1:T(8,128)(2,1)S(1)} copy(bf16[2,32,2,10,2,320]{5,4,3,2,1,0:T(2,128)(2,1)} %reshape.103) | data formatting | bytes 3276800 | tf_op jit(solution)/shard_map/reshape | solution.py:85
  95.8 3.3 %reverse_select_fusion = bf16[32,2,2,2,10,320]{5,4,3,2,1,0:T(8,128)(2,1)} fusion(bf16[32,2,2,2,10,320]{5,4,3,2,1,0:T(8,128)(2,1)S(1)} %bitcast.25, pred[2,2]{1,0:T(4,128)(4,1)S(1)} %iota_compare_fusion), kind=kLoop, calls=%fused_computation.6 | loop fusion | flops 819200 | bytes 3276804 | tf_op jit(solution)/shard_map/jit(_where)/select_n | solution.py:88
  99.1 5.9 %reshape.104 = bf16[128,50,128]{2,1,0:T(8,128)(2,1)} reshape(bf16[32,2,2,2,10,320]{5,4,3,2,1,0:T(8,128)(2,1)} %reverse_select_fusion) | data formatting | bytes 3276800 | tf_op jit(solution)/shard_map/reshape | solution.py:89
  105.0 5.7 %all-to-all-start.1 = ((bf16[128,50,128]{2,1,0:T(8,128)(2,1)}), bf16[128,50,128]{2,1,0:T(8,128)(2,1)}, u32[]{:S(2)}, u32[]{:S(2)}) async-start(bf16[128,50,128]{2,1,0:T(8,128)(2,1)} %reshape.104), calls=%async_computation.1 | async-start | bytes 3670016 | tf_op jit(solution)/shard_map/all_to_all | solution.py:16
  110.7 26.6 %all-to-all-done.1 = bf16[128,50,128]{2,1,0:T(8,128)(2,1)} async-done(((bf16[128,50,128]{2,1,0:T(8,128)(2,1)}), bf16[128,50,128]{2,1,0:T(8,128)(2,1)}, u32[]{:S(2)}, u32[]{:S(2)}) %all-to-all-start.1) | async-done | bytes 1638432 | tf_op jit(solution)/shard_map/all_to_all | solution.py:16
  137.3 3.5 %reshape.105 = bf16[256,3200]{1,0:T(8,128)(2,1)S(1)} reshape(bf16[128,50,128]{2,1,0:T(8,128)(2,1)} %all-to-all-done.1) | data formatting | bytes 3276800 | tf_op jit(solution)/shard_map/reshape | solution.py:90
  140.8 1.8 %gather_fusion.2 = bf16[96,3200]{1,0:T(8,128)(2,1)} fusion(bf16[256,3200]{1,0:T(8,128)(2,1)S(1)} %reshape.105, s32[1024]{0:T(1024)S(1)} %pad_clamp_fusion), kind=kCustom, calls=%fused_computation.2 | custom fusion | bytes 1229184 | tf_op jit(solution)/shard_map/gather | solution.py:91
  142.6 2.1 %reshape.106 = bf16[48,2,10,320]{3,2,1,0:T(8,128)(2,1)S(1)} reshape(bf16[96,3200]{1,0:T(8,128)(2,1)} %gather_fusion.2) | data formatting | bytes 1228800 | tf_op jit(solution)/shard_map/reshape | solution.py:91
  144.7 0.1 copy.40
  144.8 1.4 collective-permute-start.1
  146.3 10.6 %collective-permute-done.1 = bf16[48,10,320]{2,0,1:T(8,128)(2,1)S(1)} collective-permute-done((bf16[48,10,320]{2,0,1:T(8,128)(2,1)S(1)}, bf16[48,10,320]{2,0,1:T(8,128)(2,1)S(1)}, u32[]{:S(2)}, u32[]{:S(2)}) %collective-permute-start.1) | collective-permute-done | bytes 307232 | tf_op jit(solution)/shard_map/ppermute | solution.py:94
  156.9 0.2 copy_select_fusion.3
  157.1 0.8 multiply_reduce_fusion.1
  157.8 0.1 collective-permute-start.2
  157.9 0.9 copy-done.3
  158.8 3.5 %multiply_add_fusion = f32[2,640,640]{2,1,0:T(8,128)} fusion(f32[2,640,640]{2,1,0:T(8,128)S(1)} %copy-done.3, bf16[2,640,640]{2,1,0:T(8,128)(2,1)S(1)} %reshape.102), kind=kOutput, calls=%fused_computation.11 | convolution fusion | flops 1051033600 | bytes 8192000 | tf_op jit(solution)/shard_map/kji,kjl->kil/dot_general | solution.py:25
  162.3 1.2 collective-permute-start.3
  163.5 3.5 %multiply_add_fusion.1 = f32[2,640,640]{2,1,0:T(8,128)} fusion(f32[2,640,640]{2,1,0:T(8,128)S(1)} %copy-done.4, bf16[2,640,640]{2,1,0:T(8,128)(2,1)S(1)} %reshape.102), kind=kOutput, calls=%fused_computation.12 | convolution fusion | flops 1051033600 | bytes 8192000 | tf_op jit(solution)/shard_map/kij,klj->kil/dot_general | solution.py:21
  167.0 0.7 collective-permute-done.3
  167.7 0.8 fusion.4
  168.5 1.4 copy.45
  (25 shorter events, 0.2 us)
Async XLA Ops:
  0.6 81.7 %copy-start = (bf16[2,640,640]{2,1,0:T(8,128)(2,1)S(1)}, bf16[2,640,640]{2,1,0:T(8,128)(2,1)}, u32[]{:S(2)}) copy-start(bf16[2,640,640]{2,1,0:T(8,128)(2,1)} %param.14) | copy-start | bytes 4915204
  2.0 11.8 %collective-permute-start = (bf16[48,10,320]{2,0,1:T(8,128)(2,1)S(1)}, bf16[48,10,320]{2,0,1:T(8,128)(2,1)S(1)}, u32[]{:S(2)}, u32[]{:S(2)}) collective-permute-start(bf16[48,10,320]{2,0,1:T(8,128)(2,1)S(1)} %get-tuple-element.18), channel_id=1, source_target_pairs={{0,3},{1,2},{2,1},{3,0},{4,7},{5,6},{6,5},{7,4},{8,11},{9,10},{10,... | collective-permute-start | bytes 921608 | tf_op jit(solution)/shard_map/ppermute | solution.py:63
  24.1 37.8 %all-to-all-start = ((bf16[128,50,128]{2,1,0:T(8,128)(2,1)}), bf16[128,50,128]{2,1,0:T(8,128)(2,1)S(1)}, u32[]{:S(2)}, u32[]{:S(2)}) async-start(bf16[128,50,128]{2,1,0:T(8,128)(2,1)} %broadcast_select_fusion), calls=%async_computation | async-start | bytes 3670016 | tf_op jit(solution)/shard_map/all_to_all | solution.py:11
  105.0 32.3 %all-to-all-start.1 = ((bf16[128,50,128]{2,1,0:T(8,128)(2,1)}), bf16[128,50,128]{2,1,0:T(8,128)(2,1)}, u32[]{:S(2)}, u32[]{:S(2)}) async-start(bf16[128,50,128]{2,1,0:T(8,128)(2,1)} %reshape.104), calls=%async_computation.1 | async-start | bytes 3670016 | tf_op jit(solution)/shard_map/all_to_all | solution.py:16
  144.7 12.3 %copy-start.2 = (f32[48,20,320]{2,0,1:T(8,128)S(1)}, f32[48,20,320]{2,0,1:T(8,128)}, u32[]{:S(2)}) copy-start(f32[48,20,320]{2,0,1:T(8,128)} %param.8) | copy-start | bytes 3686404
  144.8 12.0 %collective-permute-start.1 = (bf16[48,10,320]{2,0,1:T(8,128)(2,1)S(1)}, bf16[48,10,320]{2,0,1:T(8,128)(2,1)S(1)}, u32[]{:S(2)}, u32[]{:S(2)}) collective-permute-start(bf16[48,10,320]{2,0,1:T(8,128)(2,1)S(1)} %copy.40), channel_id=1, source_target_pairs={{0,3},{1,2},{2,1},{3,0},{4,7},{5,6},{6,5},{7,4},{8,11},{9,10},{10,... | collective-permute-start | bytes 921608 | tf_op jit(solution)/shard_map/ppermute | solution.py:94
  156.8 1.9 %copy-start.3 = (f32[2,640,640]{2,1,0:T(8,128)S(1)}, f32[2,640,640]{2,1,0:T(8,128)}, u32[]{:S(2)}) copy-start(f32[2,640,640]{2,1,0:T(8,128)} %param.12) | copy-start | bytes 9830404
  157.8 4.4 %collective-permute-start.2 = (f32[48,20]{1,0:T(8,128)S(1)}, f32[48,20]{1,0:T(8,128)S(1)}, u32[]{:S(2)}, u32[]{:S(2)}) collective-permute-start(f32[48,20]{1,0:T(8,128)S(1)} %multiply_reduce_fusion.1), channel_id=1, source_target_pairs={{0,1},{1,0},{2,3},{3,2},{4,5},{5,4},{6,7},{7,6},{8,9},{9,8},{10,11... | collective-permute-start | bytes 11528 | tf_op jit(solution)/shard_map/ppermute | solution.py:103
  158.8 4.7 %copy-start.4 = (f32[2,640,640]{2,1,0:T(8,128)S(1)}, f32[2,640,640]{2,1,0:T(8,128)}, u32[]{:S(2)}) copy-start(f32[2,640,640]{2,1,0:T(8,128)} %param.11) | copy-start | bytes 9830404
  162.3 5.4 %collective-permute-start.3 = (f32[48,20]{1,0:T(8,128)S(1)}, f32[48,20]{1,0:T(8,128)S(1)}, u32[]{:S(2)}, u32[]{:S(2)}) collective-permute-start(f32[48,20]{1,0:T(8,128)S(1)} %add.102), channel_id=1, source_target_pairs={{0,2},{1,3},{2,0},{3,1},{4,6},{5,7},{6,4},{7,5},{8,10},{9,11},{10,... | collective-permute-start | bytes 11528 | tf_op jit(solution)/shard_map/ppermute | solution.py:103
  167.7 2.1 %copy-start.1 = (bf16[2,640,640]{2,1,0:T(8,128)(2,1)S(1)}, bf16[2,640,640]{2,1,0:T(8,128)(2,1)}, u32[]{:S(2)}) copy-start(bf16[2,640,640]{2,1,0:T(8,128)(2,1)} %param.14) | copy-start | bytes 4915204

commit v9 on v7

--- a/solution.py
+++ b/solution.py
@@ -68,12 +68,23 @@
     chunk = slots * slab_size
     lanes = 128 if chunk % 128 == 0 else chunk
     slabs = jnp.stack([first, second], axis=1).reshape(row_blocks * col_blocks, slab_size)
-    slot_block = jnp.full((total_slots,), block_count, jnp.int32).at[owner_slot].set(
+    slot_block = jnp.zeros((total_slots,), jnp.int32).at[owner_slot].set(
         jnp.arange(block_count, dtype=jnp.int32)
     )
-    slabs = jnp.concatenate([slabs, jnp.zeros((1, slab_size), jnp.bfloat16)], axis=0)
-    outgoing = slabs[slot_block]
-    arrived = route_out(outgoing.reshape(owners, chunk // lanes, lanes))
+    slot_used = jnp.zeros((total_slots,), jnp.bool_).at[owner_slot].set(True)
+    lane_rows = slab_size // lanes
+    chunk_rows = chunk // lanes
+    padded_rows = -(-chunk_rows // 8) * 8
+    flat = slabs.reshape(row_blocks * col_blocks * lane_rows, lanes)
+    blank = flat.shape[0]
+    flat = jnp.concatenate([flat, jnp.zeros((1, lanes), jnp.bfloat16)], axis=0)
+    rows_q = jnp.arange(padded_rows)
+    slot_g = jnp.minimum(
+        jnp.arange(owners)[:, None] * slots + (rows_q // lane_rows)[None, :], total_slots - 1
+    )
+    valid = (rows_q < chunk_rows)[None, :] & slot_used[slot_g]
+    source_row = jnp.where(valid, slot_block[slot_g] * lane_rows + (rows_q % lane_rows)[None, :], blank)
+    arrived = route_out(flat[source_row])[:, :chunk_rows]
     arrived = arrived.reshape(n_shard, col_blocks, per_block, slots, half, shard_cols)
     block_grads = arrived.transpose(3, 0, 1, 4, 2, 5).reshape(slots, order_size, order_size)
     new_left, new_right = refresh(block_grads, left_stats, right_stats)

time: 176 us -> 273 us (1.55)
  local copies, waits for them, and re-layouts: 52.4 us -> 158 us
  waiting for transfers between devices: 45.6 us -> 38.6 us
    gather x1 -> x4, local copies, waits for them, and re-layouts: 2.86 us -> 113 us  [the longest x1 44.7 us: body_steps(): slot_block[slot_g] * lane_rows + (rows_q % lane_rows)[None, :]]
    ppermute x1, waiting for transfers between devices: 7.02 us -> 0.01 us  [body_steps(): got = lax.ppermute(give, 'tensor', partner)]
    reshape x2 -> x0, local copies, waits for them, and re-layouts: 4.24 us -> none  [the longest x1 3.56 us: body_steps(): arrived = route_out(outgoing.reshape(owners, chunk // lanes, lanes))]
  transfers between devices with their start and end apart: 5 -> 5, of which waited for: 4 -> 3; matrix products, arithmetic and copies ran while one was open for 5% -> 36% of each run, Pallas kernels for 0% -> 0%
where the time goes in v9:
time: 273 us; the launch traced here: 272 us
  local copies, waits for them, and re-layouts  158 us (58%)
  waiting for transfers between devices  38.6 us (14%)
  blocking collectives  35.9 us (13%)
  other arithmetic  13.3 us (5%)
  matrix products  13.3 us (5%)
  starting transfers between devices  12 us (4%)
    gather x1, local copies, waits for them, and re-layouts, body_steps(): slot_block[slot_g] * lane_rows + (rows_q % lane_rows)[None, :]  44.7 us
    gather x2, local copies, waits for them, and re-layouts, body_steps(): valid = (rows_q < chunk_rows)[None, :] & slot_used[slot_g]  42.4 us
    all_to_all x1, blocking collectives, route_out(): lax.all_to_all(outgoing, ('shard', 'tensor'), split_axis=0, concat_axis=0...  35.9 us
    all_to_all x1, waiting for transfers between devices, route_back(): lax.all_to_all(outgoing, ('shard', 'tensor'), split_axis=0, concat_axis=0...  26.6 us
    gather x1, local copies, waits for them, and re-layouts, body_steps(): arrived = route_out(flat[source_row])[:, :chunk_rows]  25.8 us
    ppermute x1, waiting for transfers between devices, body_steps(): other_back = lax.ppermute(other_part, 'tensor', partner)  11.3 us
    reshape x2, local copies, waits for them, and re-layouts, body_steps(): delta.reshape(slots, n_shard, col_blocks, half, per_block, shard_cols)  9.23 us
    dot_general x1, matrix products, direction(): jnp.einsum('kij,kjl->kil', half, right_root, preferred_element_type=jnp.f...  6.34 us
  transfers between devices with their start and end apart: 5, of which 3 were waited for; matrix products, arithmetic and copies ran while one was open for 36% of the time, Pallas kernels for 0%

profile of v9, /device:TPU:0, one launch (start us, length us, event | category | flops | bytes accessed | tf_op | source)
XLA Modules:
  0.0 272.2 jit_solution(9017352145665375530)
XLA Ops:
  0.6 0.0 copy-start
  0.7 1.3 constant_dynamic-slice_fusion
  2.0 3.4 %collective-permute-start = (bf16[48,10,320]{2,0,1:T(8,128)(2,1)S(1)}, bf16[48,10,320]{2,0,1:T(8,128)(2,1)S(1)}, u32[]{:S(2)}, u32[]{:S(2)}) collective-permute-start(bf16[48,10,320]{2,0,1:T(8,128)(2,1)S(1)} %get-tuple-element.22), channel_id=1, source_target_pairs={{0,2},{1,3},{2,0},{3,1},{4,6},{5,7},{6,4},{7,5},{8,10},{9,11},{10,... | collective-permute-start | bytes 921608 | tf_op jit(solution)/shard_map/ppermute | solution.py:63
  5.4 0.1 compare_select_fusion.1
  5.5 0.1 reshape.201
  5.6 0.7 compare_select_fusion.2
  6.2 0.9 scatter_custom_fusion.1
  7.1 44.7 %gather_fusion.1 = s32[7168]{0:T(1024)S(1)} fusion(s32[256]{0:T(256)S(1)} %scatter_custom_fusion.1, s32[7168]{0:T(1024)S(1)} %broadcast_clamp_fusion.1), kind=kCustom, calls=%fused_computation.1 | custom fusion | bytes 86016 | tf_op jit(solution)/shard_map/gather | solution.py:86
  51.8 0.1 mul.93
  51.9 0.9 scatter_custom_fusion
  52.8 42.3 %gather_fusion = pred[7168]{0:T(1024)(128)(4,1)S(1)} fusion(pred[256]{0:T(512)(128)(4,1)S(1)} %scatter_custom_fusion, s32[7168]{0:T(1024)S(1)} %broadcast_clamp_fusion.1), kind=kCustom, calls=%fused_computation | custom fusion | bytes 43008 | tf_op jit(solution)/shard_map/gather | solution.py:85
  95.2 0.1 gather.15
  95.3 0.1 reshape.217
  95.4 0.2 fusion.5
  95.7 0.3 pad_maximum_fusion
  96.0 0.1 copy.54
  96.1 0.9 reshape_reshape.3
  97.1 25.8 %gather_fusion.2 = bf16[7168,128]{1,0:T(8,128)(2,1)} fusion(bf16[2401,128]{1,0:T(8,128)(2,1)S(1)} %concatenate.6, s32[7168]{0:T(1024)S(1)} %broadcast_clamp_fusion), kind=kCustom, calls=%fused_computation.2 | custom fusion | bytes 3698688 | tf_op jit(solution)/shard_map/gather | solution.py:87
  122.8 35.9 %all_to_all.10 = bf16[128,56,128]{2,1,0:T(8,128)(2,1)S(1)} all-to-all(bf16[128,56,128]{2,1,0:T(8,128)(2,1)} %bitcast.29), channel_id=1, replica_groups=mesh['shard'=32,'tensor'=4] {'shard','tensor'}, dimensions={0} | all-to-all | bytes 3670016 | tf_op jit(solution)/shard_map/all_to_all | solution.py:11
  158.7 3.9 %reshape.193 = bf16[32,2,2,2,10,320]{5,4,3,2,1,0:T(8,128)(2,1)} reshape(bf16[128,50,128]{2,1,0:T(8,128)(2,1)S(1)} %bitcast.28) | data formatting | bytes 3276800 | tf_op jit(solution)/shard_map/reshape | solution.py:88
  162.7 4.7 %copy.55 = bf16[2,32,2,10,2,320]{5,4,3,2,1,0:T(2,128)(2,1)} copy(bf16[2,32,2,10,2,320]{5,3,0,4,2,1:T(8,128)(2,1)} %bitcast.26) | data formatting | bytes 3276800 | tf_op jit(solution)/shard_map/transpose | solution.py:89
  167.4 4.2 %reshape.194 = bf16[2,640,640]{2,1,0:T(8,128)(2,1)S(1)} reshape(bf16[2,32,2,10,2,320]{5,4,3,2,1,0:T(2,128)(2,1)} %copy.55) | data formatting | bytes 3276800 | tf_op jit(solution)/shard_map/reshape | solution.py:89
  171.6 5.4 %fusion.2 = (f32[2]{0:T(128)S(1)}, f32[2,640,640]{2,1,0:T(8,128)}) fusion(bf16[2,640,640]{2,1,0:T(8,128)(2,1)S(1)} %reshape.194, f32[2,640,640]{2,1,0:T(8,128)} %param.15), kind=kLoop, calls=%fused_computation.14 | loop fusion | flops 7372798 | bytes 8192008 | tf_op jit(solution)/shard_map/reduce_sum | solution.py:40
  177.0 6.3 %multiply_reduce_fusion = (f32[2]{0:T(128)S(1)}, f32[2,640,640]{2,1,0:T(8,128)}) fusion(bf16[2,640,640]{2,1,0:T(8,128)(2,1)S(1)} %copy-done, bf16[2,640,640]{2,1,0:T(8,128)(2,1)S(1)} %reshape.194, bf16[2,640,640]{2,1,0:T(8,128)(2,1)} %param.13), kind=kOutput, calls=%fused_computation.13 | convolution fusion | flops 2099609600 | bytes 8192008 | tf_op jit(solution)/shard_map/kij,kjl->kil/dot_general | solution.py:36
  183.3 3.4 %multiply_convert_fusion = bf16[2,640,640]{2,1,0:T(8,128)(2,1)} fusion(f32[2,640,640]{2,1,0:T(8,128)} %get-tuple-element.25, f32[2]{0:T(128)S(1)} %rsqrt_multiply_fusion), kind=kLoop, calls=%fused_computation.12 | loop fusion | flops 1638400 | bytes 4915208 | tf_op jit(solution)/shard_map/convert_element_type | solution.py:43
  186.7 5.3 %reshape.195 = bf16[2,32,2,10,2,320]{5,4,3,2,1,0:T(2,128)(2,1)} reshape(bf16[2,640,640]{2,1,0:T(8,128)(2,1)} %multiply_convert_fusion) | data formatting | bytes 3276800 | tf_op jit(solution)/shard_map/reshape | solution.py:92
  192.0 3.9 %copy.89 = bf16[2,32,2,10,2,320]{5,3,0,4,2,1:T(8,128)(2,1)} copy(bf16[2,32,2,10,2,320]{5,4,3,2,1,0:T(2,128)(2,1)} %reshape.195) | data formatting | bytes 3276800 | tf_op jit(solution)/shard_map/reshape | solution.py:92
  196.0 5.9 %reshape.196 = bf16[128,50,128]{2,1,0:T(8,128)(2,1)} reshape(bf16[32,2,2,2,10,320]{5,4,3,2,1,0:T(8,128)(2,1)} %bitcast.27) | data formatting | bytes 3276800 | tf_op jit(solution)/shard_map/reshape | solution.py:95
  201.9 5.7 %all-to-all-start.1 = ((bf16[128,50,128]{2,1,0:T(8,128)(2,1)}), bf16[128,50,128]{2,1,0:T(8,128)(2,1)}, u32[]{:S(2)}, u32[]{:S(2)}) async-start(bf16[128,50,128]{2,1,0:T(8,128)(2,1)} %reshape.196), calls=%async_computation.1 | async-start | bytes 3670016 | tf_op jit(solution)/shard_map/all_to_all | solution.py:16
  207.6 26.6 %all-to-all-done.1 = bf16[128,50,128]{2,1,0:T(8,128)(2,1)} async-done(((bf16[128,50,128]{2,1,0:T(8,128)(2,1)}), bf16[128,50,128]{2,1,0:T(8,128)(2,1)}, u32[]{:S(2)}, u32[]{:S(2)}) %all-to-all-start.1) | async-done | bytes 1638432 | tf_op jit(solution)/shard_map/all_to_all | solution.py:16
  234.2 4.3 %reshape.197 = bf16[256,3200]{1,0:T(8,128)(2,1)} reshape(bf16[128,50,128]{2,1,0:T(8,128)(2,1)} %all-to-all-done.1) | data formatting | bytes 3276800 | tf_op jit(solution)/shard_map/reshape | solution.py:96
  238.5 4.0 %gather_fusion.3 = bf16[96,3200]{1,0:T(8,128)(2,1)} fusion(bf16[256,3200]{1,0:T(8,128)(2,1)} %reshape.197, s32[1024]{0:T(1024)S(1)} %pad_clamp_fusion), kind=kCustom, calls=%fused_computation.3 | custom fusion | bytes 1229184 | tf_op jit(solution)/shard_map/gather | solution.py:97
  242.5 2.8 %reshape.198 = bf16[48,2,10,320]{3,2,1,0:T(8,128)(2,1)} reshape(bf16[96,3200]{1,0:T(8,128)(2,1)} %gather_fusion.3) | data formatting | bytes 1228800 | tf_op jit(solution)/shard_map/reshape | solution.py:97
  245.4 1.4 select_bitcast_fusion
  246.8 0.0 copy-start.2
  246.8 0.1 copy.59
  246.9 1.0 collective-permute-start.1
  247.9 11.3 %collective-permute-done.1 = bf16[48,10,320]{2,0,1:T(8,128)(2,1)S(1)} collective-permute-done((bf16[48,10,320]{2,0,1:T(8,128)(2,1)S(1)}, bf16[48,10,320]{2,0,1:T(8,128)(2,1)S(1)}, u32[]{:S(2)}, u32[]{:S(2)}) %collective-permute-start.1) | collective-permute-done | bytes 307232 | tf_op jit(solution)/shard_map/ppermute | solution.py:100
  259.2 0.2 copy_select_fusion.3
  259.4 0.8 multiply_reduce_fusion.1
  260.2 0.7 collective-permute-start.2
  260.9 0.2 copy-done.3
  261.1 3.5 %multiply_add_fusion = f32[2,640,640]{2,1,0:T(8,128)} fusion(f32[2,640,640]{2,1,0:T(8,128)S(1)} %copy-done.3, bf16[2,640,640]{2,1,0:T(8,128)(2,1)S(1)} %reshape.194), kind=kOutput, calls=%fused_computation.10 | convolution fusion | flops 1051033600 | bytes 8192000 | tf_op jit(solution)/shard_map/kji,kjl->kil/dot_general | solution.py:25
  264.6 1.2 collective-permute-start.3
  265.8 3.5 %multiply_add_fusion.1 = f32[2,640,640]{2,1,0:T(8,128)} fusion(f32[2,640,640]{2,1,0:T(8,128)S(1)} %copy-done.4, bf16[2,640,640]{2,1,0:T(8,128)(2,1)S(1)} %reshape.194), kind=kOutput, calls=%fused_computation.11 | convolution fusion | flops 1051033600 | bytes 8192000 | tf_op jit(solution)/shard_map/kij,klj->kil/dot_general | solution.py:21
  269.3 0.7 collective-permute-done.3
  270.0 0.8 fusion.3
  270.8 1.4 copy.64
  (23 shorter events, 0.2 us)
Async XLA Ops:
  0.6 176.4 %copy-start = (bf16[2,640,640]{2,1,0:T(8,128)(2,1)S(1)}, bf16[2,640,640]{2,1,0:T(8,128)(2,1)}, u32[]{:S(2)}) copy-start(bf16[2,640,640]{2,1,0:T(8,128)(2,1)} %param.14) | copy-start | bytes 4915204
  2.0 93.5 %collective-permute-start = (bf16[48,10,320]{2,0,1:T(8,128)(2,1)S(1)}, bf16[48,10,320]{2,0,1:T(8,128)(2,1)S(1)}, u32[]{:S(2)}, u32[]{:S(2)}) collective-permute-start(bf16[48,10,320]{2,0,1:T(8,128)(2,1)S(1)} %get-tuple-element.22), channel_id=1, source_target_pairs={{0,2},{1,3},{2,0},{3,1},{4,6},{5,7},{6,4},{7,5},{8,10},{9,11},{10,... | collective-permute-start | bytes 921608 | tf_op jit(solution)/shard_map/ppermute | solution.py:63
  201.9 32.3 %all-to-all-start.1 = ((bf16[128,50,128]{2,1,0:T(8,128)(2,1)}), bf16[128,50,128]{2,1,0:T(8,128)(2,1)}, u32[]{:S(2)}, u32[]{:S(2)}) async-start(bf16[128,50,128]{2,1,0:T(8,128)(2,1)} %reshape.196), calls=%async_computation.1 | async-start | bytes 3670016 | tf_op jit(solution)/shard_map/all_to_all | solution.py:16
  245.4 13.8 %copy-start.1 = (bf16[48,2,10,320]{3,2,1,0:T(8,128)(2,1)S(1)}, bf16[48,2,10,320]{3,2,1,0:T(8,128)(2,1)}, u32[]{:S(2)}) copy-start(bf16[48,2,10,320]{3,2,1,0:T(8,128)(2,1)} %reshape.198) | copy-start | bytes 1843204
  246.8 12.6 %copy-start.2 = (f32[48,20,320]{2,0,1:T(8,128)S(1)}, f32[48,20,320]{2,0,1:T(8,128)}, u32[]{:S(2)}) copy-start(f32[48,20,320]{2,0,1:T(8,128)} %param.8) | copy-start | bytes 3686404
  246.9 12.3 %collective-permute-start.1 = (bf16[48,10,320]{2,0,1:T(8,128)(2,1)S(1)}, bf16[48,10,320]{2,0,1:T(8,128)(2,1)S(1)}, u32[]{:S(2)}, u32[]{:S(2)}) collective-permute-start(bf16[48,10,320]{2,0,1:T(8,128)(2,1)S(1)} %copy.59), channel_id=1, source_target_pairs={{0,2},{1,3},{2,0},{3,1},{4,6},{5,7},{6,4},{7,5},{8,10},{9,11},{10,... | collective-permute-start | bytes 921608 | tf_op jit(solution)/shard_map/ppermute | solution.py:100
  259.2 1.9 copy-start.3
  260.2 4.4 %collective-permute-start.2 = (f32[48,20]{1,0:T(8,128)S(1)}, f32[48,20]{1,0:T(8,128)S(1)}, u32[]{:S(2)}, u32[]{:S(2)}) collective-permute-start(f32[48,20]{1,0:T(8,128)S(1)} %multiply_reduce_fusion.1), channel_id=1, source_target_pairs={{0,1},{1,0},{2,3},{3,2},{4,5},{5,4},{6,7},{7,6},{8,9},{9,8},{10,11... | collective-permute-start | bytes 11528 | tf_op jit(solution)/shard_map/ppermute | solution.py:109
  261.1 4.7 %copy-start.4 = (f32[2,640,640]{2,1,0:T(8,128)S(1)}, f32[2,640,640]{2,1,0:T(8,128)}, u32[]{:S(2)}) copy-start(f32[2,640,640]{2,1,0:T(8,128)} %param.11) | copy-start | bytes 9830404
  264.6 5.4 %collective-permute-start.3 = (f32[48,20]{1,0:T(8,128)S(1)}, f32[48,20]{1,0:T(8,128)S(1)}, u32[]{:S(2)}, u32[]{:S(2)}) collective-permute-start(f32[48,20]{1,0:T(8,128)S(1)} %add.146), channel_id=1, source_target_pairs={{0,2},{1,3},{2,0},{3,1},{4,6},{5,7},{6,4},{7,5},{8,10},{9,11},{10,... | collective-permute-start | bytes 11528 | tf_op jit(solution)/shard_map/ppermute | solution.py:109

commit v10 on v7

--- a/solution.py
+++ b/solution.py
@@ -61,18 +61,17 @@
     keep = lax.dynamic_slice_in_dim(grads, mine_col * half, half, axis=1)
     give = lax.dynamic_slice_in_dim(grads, (1 - mine_col) * half, half, axis=1)
     got = lax.ppermute(give, "tensor", partner)
-    first = jnp.where(mine_col == 0, keep, got)
-    second = jnp.where(mine_col == 0, got, keep)
     block_count = owner_slot.shape[0]
     slab_size = half * shard_cols
     chunk = slots * slab_size
     lanes = 128 if chunk % 128 == 0 else chunk
-    slabs = jnp.stack([first, second], axis=1).reshape(row_blocks * col_blocks, slab_size)
-    slot_block = jnp.full((total_slots,), block_count, jnp.int32).at[owner_slot].set(
+    slabs = jnp.stack([keep, got], axis=1).reshape(row_blocks * col_blocks, slab_size)
+    slot_block = jnp.zeros((total_slots,), jnp.int32).at[owner_slot].set(
         jnp.arange(block_count, dtype=jnp.int32)
     )
-    slabs = jnp.concatenate([slabs, jnp.zeros((1, slab_size), jnp.bfloat16)], axis=0)
-    outgoing = slabs[slot_block]
+    slot_used = jnp.zeros((total_slots,), jnp.bool_).at[owner_slot].set(True)
+    slab_index = (slot_block // col_blocks) * col_blocks + (slot_block % col_blocks != mine_col)
+    outgoing = jnp.where(slot_used[:, None], slabs[slab_index], jnp.zeros((), jnp.bfloat16))
     arrived = route_out(outgoing.reshape(owners, chunk // lanes, lanes))
     arrived = arrived.reshape(n_shard, col_blocks, per_block, slots, half, shard_cols)
     block_grads = arrived.transpose(3, 0, 1, 4, 2, 5).reshape(slots, order_size, order_size)

time: 176 us -> 175 us (level)
    reshape x2 -> x1, local copies, waits for them, and re-layouts: 4.24 us -> 0.68 us  [body_steps(): jnp.stack([keep, got], axis=1).reshape(row_blocks * col_blocks, slab_size)]
    gather x1 -> x2, local copies, waits for them, and re-layouts: 2.86 us -> 6.42 us  [body_steps(): slabs[slab_index]]
    reshape x1, local copies, waits for them, and re-layouts: 6.03 us -> 3.93 us  [body_steps(): arrived.reshape(n_shard, col_blocks, per_block, slots, half, shard_cols)]
  transfers between devices with their start and end apart: 5 -> 5, of which waited for: 4 -> 4; matrix products, arithmetic and copies ran while one was open for 5% -> 6% of each run, Pallas kernels for 0% -> 0%
where the time goes in v10:
time: 175 us; the launch traced here: 174 us
  local copies, waits for them, and re-layouts  51.6 us (29%)
  waiting for transfers between devices  44.3 us (25%)
  blocking collectives  37.9 us (22%)
  other arithmetic  14.1 us (8%)
  matrix products  13.3 us (8%)
  starting transfers between devices  12 us (7%)
    all_to_all x1, blocking collectives, route_out(): lax.all_to_all(outgoing, ('shard', 'tensor'), split_axis=0, concat_axis=0...  37.9 us
    all_to_all x1, waiting for transfers between devices, route_back(): lax.all_to_all(outgoing, ('shard', 'tensor'), split_axis=0, concat_axis=0...  26.6 us
    ppermute x1, waiting for transfers between devices, body_steps(): other_back = lax.ppermute(other_part, 'tensor', partner)  11.3 us
    reshape x2, local copies, waits for them, and re-layouts, body_steps(): delta.reshape(slots, n_shard, col_blocks, half, per_block, shard_cols)  9.23 us
    gather x2, local copies, waits for them, and re-layouts, body_steps(): slabs[slab_index]  6.42 us
    dot_general x1, matrix products, direction(): jnp.einsum('kij,kjl->kil', half, right_root, preferred_element_type=jnp.f...  6.34 us
    reshape x1, local copies, waits for them, and re-layouts, body_steps(): sendback = pieces.reshape(owners, chunk // lanes, lanes)  5.93 us
    all_to_all x1, starting transfers between devices, route_back(): lax.all_to_all(outgoing, ('shard', 'tensor'), split_axis=0, concat_axis=0...  5.71 us
  transfers between devices with their start and end apart: 5, of which 4 were waited for; matrix products, arithmetic and copies ran while one was open for 6% of the time, Pallas kernels for 0%

profile of v10, /device:TPU:0, one launch (start us, length us, event | category | flops | bytes accessed | tf_op | source)
XLA Modules:
  0.0 174.0 jit_solution(8060524158780208058)
XLA Ops:
  0.6 0.0 copy-start
  0.7 1.3 dynamic-slice_bitcast_fusion
  2.0 3.4 %collective-permute-start = (bf16[48,10,320]{2,0,1:T(8,128)(2,1)S(1)}, bf16[48,10,320]{2,0,1:T(8,128)(2,1)S(1)}, u32[]{:S(2)}, u32[]{:S(2)}) collective-permute-start(bf16[48,10,320]{2,0,1:T(8,128)(2,1)S(1)} %get-tuple-element.21), channel_id=1, source_target_pairs={{0,2},{1,3},{2,0},{3,1},{4,6},{5,7},{6,4},{7,5},{8,10},{9,11},{10,... | collective-permute-start | bytes 921608 | tf_op jit(solution)/shard_map/ppermute | solution.py:63
  5.4 0.7 compare_select_fusion.1
  6.0 0.9 scatter_custom_fusion.1
  6.9 0.9 scatter_custom_fusion
  7.8 0.2 broadcast_in_dim.38
  8.0 0.1 copy.50
  8.1 0.1 copy.51
  8.3 5.7 %collective-permute-done = bf16[48,10,320]{2,0,1:T(8,128)(2,1)S(1)} collective-permute-done((bf16[48,10,320]{2,0,1:T(8,128)(2,1)S(1)}, bf16[48,10,320]{2,0,1:T(8,128)(2,1)S(1)}, u32[]{:S(2)}, u32[]{:S(2)}) %collective-permute-start) | collective-permute-done | bytes 307232 | tf_op jit(solution)/shard_map/ppermute | solution.py:63
  13.9 0.1 pad_maximum_fusion.1
  14.1 0.2 copy.52
  14.3 0.7 reshape.50
  15.0 2.9 %gather_fusion = bf16[256,3200]{1,0:T(8,128)(2,1)} fusion(bf16[96,3200]{1,0:T(8,128)(2,1)S(1)} %reshape.50, s32[1024]{0:T(1024)S(1)} %pad_clamp_fusion.1), kind=kCustom, calls=%fused_computation | custom fusion | bytes 3277824 | tf_op jit(solution)/shard_map/gather | solution.py:74
  17.9 3.6 %gather.9 = bf16[128,50,128]{2,1,0:T(8,128)(2,1)S(1)} reshape(bf16[256,3200]{1,0:T(8,128)(2,1)} %gather_fusion) | data formatting | bytes 3276800 | tf_op jit(solution)/shard_map/gather | solution.py:74
  21.4 1.3 broadcast_select_fusion
  22.7 37.9 %all_to_all.10 = bf16[128,50,128]{2,1,0:T(8,128)(2,1)S(1)} all-to-all(bf16[128,50,128]{2,1,0:T(8,128)(2,1)S(1)} %broadcast_select_fusion), channel_id=1, replica_groups=mesh['shard'=32,'tensor'=4] {'shard','tensor'}, dimensions={0} | all-to-all | bytes 3276800 | tf_op jit(solution)/shard_map/all_to_all | solution.py:11
  60.6 3.9 %reshape.51 = bf16[32,2,2,2,10,320]{5,4,3,2,1,0:T(8,128)(2,1)} reshape(bf16[128,50,128]{2,1,0:T(8,128)(2,1)S(1)} %all_to_all.10) | data formatting | bytes 3276800 | tf_op jit(solution)/shard_map/reshape | solution.py:76
  64.5 4.7 %copy.53 = bf16[2,32,2,10,2,320]{5,4,3,2,1,0:T(2,128)(2,1)} copy(bf16[2,32,2,10,2,320]{5,3,0,4,2,1:T(8,128)(2,1)} %bitcast.21) | data formatting | bytes 3276800 | tf_op jit(solution)/shard_map/transpose | solution.py:77
  69.2 4.2 %reshape.52 = bf16[2,640,640]{2,1,0:T(8,128)(2,1)S(1)} reshape(bf16[2,32,2,10,2,320]{5,4,3,2,1,0:T(2,128)(2,1)} %copy.53) | data formatting | bytes 3276800 | tf_op jit(solution)/shard_map/reshape | solution.py:77
  73.4 5.4 %fusion.2 = (f32[2]{0:T(128)S(1)}, f32[2,640,640]{2,1,0:T(8,128)}) fusion(bf16[2,640,640]{2,1,0:T(8,128)(2,1)S(1)} %reshape.52, f32[2,640,640]{2,1,0:T(8,128)} %param.15), kind=kLoop, calls=%fused_computation.12 | loop fusion | flops 7372798 | bytes 8192008 | tf_op jit(solution)/shard_map/reduce_sum | solution.py:40
  78.8 6.3 %multiply_reduce_fusion = (f32[2]{0:T(128)S(1)}, f32[2,640,640]{2,1,0:T(8,128)}) fusion(bf16[2,640,640]{2,1,0:T(8,128)(2,1)S(1)} %copy-done, bf16[2,640,640]{2,1,0:T(8,128)(2,1)S(1)} %reshape.52, bf16[2,640,640]{2,1,0:T(8,128)(2,1)} %param.13), kind=kOutput, calls=%fused_computation.11 | convolution fusion | flops 2099609600 | bytes 8192008 | tf_op jit(solution)/shard_map/kij,kjl->kil/dot_general | solution.py:36
  85.2 3.4 %multiply_convert_fusion = bf16[2,640,640]{2,1,0:T(8,128)(2,1)} fusion(f32[2,640,640]{2,1,0:T(8,128)} %get-tuple-element.23, f32[2]{0:T(128)S(1)} %rsqrt_multiply_fusion), kind=kLoop, calls=%fused_computation.10 | loop fusion | flops 1638400 | bytes 4915208 | tf_op jit(solution)/shard_map/convert_element_type | solution.py:43
  88.6 5.3 %reshape.53 = bf16[2,32,2,10,2,320]{5,4,3,2,1,0:T(2,128)(2,1)} reshape(bf16[2,640,640]{2,1,0:T(8,128)(2,1)} %multiply_convert_fusion) | data formatting | bytes 3276800 | tf_op jit(solution)/shard_map/reshape | solution.py:80
  93.9 3.9 %copy.74 = bf16[2,32,2,10,2,320]{5,3,0,4,2,1:T(8,128)(2,1)} copy(bf16[2,32,2,10,2,320]{5,4,3,2,1,0:T(2,128)(2,1)} %reshape.53) | data formatting | bytes 3276800 | tf_op jit(solution)/shard_map/reshape | solution.py:80
  97.8 5.9 %reshape.54 = bf16[128,50,128]{2,1,0:T(8,128)(2,1)} reshape(bf16[32,2,2,2,10,320]{5,4,3,2,1,0:T(8,128)(2,1)} %bitcast.22) | data formatting | bytes 3276800 | tf_op jit(solution)/shard_map/reshape | solution.py:83
  103.8 5.7 %all-to-all-start.1 = ((bf16[128,50,128]{2,1,0:T(8,128)(2,1)}), bf16[128,50,128]{2,1,0:T(8,128)(2,1)}, u32[]{:S(2)}, u32[]{:S(2)}) async-start(bf16[128,50,128]{2,1,0:T(8,128)(2,1)} %reshape.54), calls=%async_computation.1 | async-start | bytes 3670016 | tf_op jit(solution)/shard_map/all_to_all | solution.py:16
  109.5 26.6 %all-to-all-done.1 = bf16[128,50,128]{2,1,0:T(8,128)(2,1)} async-done(((bf16[128,50,128]{2,1,0:T(8,128)(2,1)}), bf16[128,50,128]{2,1,0:T(8,128)(2,1)}, u32[]{:S(2)}, u32[]{:S(2)}) %all-to-all-start.1) | async-done | bytes 1638432 | tf_op jit(solution)/shard_map/all_to_all | solution.py:16
  136.1 4.3 %reshape.55 = bf16[256,3200]{1,0:T(8,128)(2,1)} reshape(bf16[128,50,128]{2,1,0:T(8,128)(2,1)} %all-to-all-done.1) | data formatting | bytes 3276800 | tf_op jit(solution)/shard_map/reshape | solution.py:84
  140.4 4.0 %gather_fusion.1 = bf16[96,3200]{1,0:T(8,128)(2,1)} fusion(bf16[256,3200]{1,0:T(8,128)(2,1)} %reshape.55, s32[1024]{0:T(1024)S(1)} %pad_clamp_fusion), kind=kCustom, calls=%fused_computation.1 | custom fusion | bytes 1229184 | tf_op jit(solution)/shard_map/gather | solution.py:85
  144.4 2.8 %reshape.56 = bf16[48,2,10,320]{3,2,1,0:T(8,128)(2,1)} reshape(bf16[96,3200]{1,0:T(8,128)(2,1)} %gather_fusion.1) | data formatting | bytes 1228800 | tf_op jit(solution)/shard_map/reshape | solution.py:85
  147.2 1.4 select_bitcast_fusion
  148.6 0.0 copy-start.2
  148.7 0.1 copy.57
  148.7 1.0 collective-permute-start.1
  149.7 11.3 %collective-permute-done.1 = bf16[48,10,320]{2,0,1:T(8,128)(2,1)S(1)} collective-permute-done((bf16[48,10,320]{2,0,1:T(8,128)(2,1)S(1)}, bf16[48,10,320]{2,0,1:T(8,128)(2,1)S(1)}, u32[]{:S(2)}, u32[]{:S(2)}) %collective-permute-start.1) | collective-permute-done | bytes 307232 | tf_op jit(solution)/shard_map/ppermute | solution.py:88
  161.1 0.2 copy_select_fusion.1
  161.3 0.0 copy-done.2
  161.3 0.8 multiply_reduce_fusion.1
  162.0 0.7 collective-permute-start.2
  162.7 0.2 copy-done.3
  163.0 3.5 %multiply_add_fusion = f32[2,640,640]{2,1,0:T(8,128)} fusion(f32[2,640,640]{2,1,0:T(8,128)S(1)} %copy-done.3, bf16[2,640,640]{2,1,0:T(8,128)(2,1)S(1)} %reshape.52), kind=kOutput, calls=%fused_computation.8 | convolution fusion | flops 1051033600 | bytes 8192000 | tf_op jit(solution)/shard_map/kji,kjl->kil/dot_general | solution.py:25
  166.5 0.0 collective-permute-done.2
  166.5 1.2 collective-permute-start.3
  167.7 3.5 %multiply_add_fusion.1 = f32[2,640,640]{2,1,0:T(8,128)} fusion(f32[2,640,640]{2,1,0:T(8,128)S(1)} %copy-done.4, bf16[2,640,640]{2,1,0:T(8,128)(2,1)S(1)} %reshape.52), kind=kOutput, calls=%fused_computation.9 | convolution fusion | flops 1051033600 | bytes 8192000 | tf_op jit(solution)/shard_map/kij,klj->kil/dot_general | solution.py:21
  171.2 0.7 collective-permute-done.3
  171.9 0.8 fusion.3
  172.7 1.4 copy.62
  (16 shorter events, 0.1 us)
Async XLA Ops:
  0.6 78.2 %copy-start = (bf16[2,640,640]{2,1,0:T(8,128)(2,1)S(1)}, bf16[2,640,640]{2,1,0:T(8,128)(2,1)}, u32[]{:S(2)}) copy-start(bf16[2,640,640]{2,1,0:T(8,128)(2,1)} %param.14) | copy-start | bytes 4915204
  2.0 12.0 %collective-permute-start = (bf16[48,10,320]{2,0,1:T(8,128)(2,1)S(1)}, bf16[48,10,320]{2,0,1:T(8,128)(2,1)S(1)}, u32[]{:S(2)}, u32[]{:S(2)}) collective-permute-start(bf16[48,10,320]{2,0,1:T(8,128)(2,1)S(1)} %get-tuple-element.21), channel_id=1, source_target_pairs={{0,2},{1,3},{2,0},{3,1},{4,6},{5,7},{6,4},{7,5},{8,10},{9,11},{10,... | collective-permute-start | bytes 921608 | tf_op jit(solution)/shard_map/ppermute | solution.py:63
  103.8 32.3 %all-to-all-start.1 = ((bf16[128,50,128]{2,1,0:T(8,128)(2,1)}), bf16[128,50,128]{2,1,0:T(8,128)(2,1)}, u32[]{:S(2)}, u32[]{:S(2)}) async-start(bf16[128,50,128]{2,1,0:T(8,128)(2,1)} %reshape.54), calls=%async_computation.1 | async-start | bytes 3670016 | tf_op jit(solution)/shard_map/all_to_all | solution.py:16
  147.2 13.8 %copy-start.1 = (bf16[48,2,10,320]{3,2,1,0:T(8,128)(2,1)S(1)}, bf16[48,2,10,320]{3,2,1,0:T(8,128)(2,1)}, u32[]{:S(2)}) copy-start(bf16[48,2,10,320]{3,2,1,0:T(8,128)(2,1)} %reshape.56) | copy-start | bytes 1843204
  148.6 12.6 %copy-start.2 = (f32[48,20,320]{2,0,1:T(8,128)S(1)}, f32[48,20,320]{2,0,1:T(8,128)}, u32[]{:S(2)}) copy-start(f32[48,20,320]{2,0,1:T(8,128)} %param.8) | copy-start | bytes 3686404
  148.7 12.3 %collective-permute-start.1 = (bf16[48,10,320]{2,0,1:T(8,128)(2,1)S(1)}, bf16[48,10,320]{2,0,1:T(8,128)(2,1)S(1)}, u32[]{:S(2)}, u32[]{:S(2)}) collective-permute-start(bf16[48,10,320]{2,0,1:T(8,128)(2,1)S(1)} %copy.57), channel_id=1, source_target_pairs={{0,2},{1,3},{2,0},{3,1},{4,6},{5,7},{6,4},{7,5},{8,10},{9,11},{10,... | collective-permute-start | bytes 921608 | tf_op jit(solution)/shard_map/ppermute | solution.py:88
  161.1 1.9 %copy-start.3 = (f32[2,640,640]{2,1,0:T(8,128)S(1)}, f32[2,640,640]{2,1,0:T(8,128)}, u32[]{:S(2)}) copy-start(f32[2,640,640]{2,1,0:T(8,128)} %param.12) | copy-start | bytes 9830404
  162.0 4.4 %collective-permute-start.2 = (f32[48,20]{1,0:T(8,128)S(1)}, f32[48,20]{1,0:T(8,128)S(1)}, u32[]{:S(2)}, u32[]{:S(2)}) collective-permute-start(f32[48,20]{1,0:T(8,128)S(1)} %multiply_reduce_fusion.1), channel_id=1, source_target_pairs={{0,1},{1,0},{2,3},{3,2},{4,5},{5,4},{6,7},{7,6},{8,9},{9,8},{10,11... | collective-permute-start | bytes 11528 | tf_op jit(solution)/shard_map/ppermute | solution.py:97
  163.0 4.7 %copy-start.4 = (f32[2,640,640]{2,1,0:T(8,128)S(1)}, f32[2,640,640]{2,1,0:T(8,128)}, u32[]{:S(2)}) copy-start(f32[2,640,640]{2,1,0:T(8,128)} %param.11) | copy-start | bytes 9830404
  166.5 5.4 %collective-permute-start.3 = (f32[48,20]{1,0:T(8,128)S(1)}, f32[48,20]{1,0:T(8,128)S(1)}, u32[]{:S(2)}, u32[]{:S(2)}) collective-permute-start(f32[48,20]{1,0:T(8,128)S(1)} %add.73), channel_id=1, source_target_pairs={{0,2},{1,3},{2,0},{3,1},{4,6},{5,7},{6,4},{7,5},{8,10},{9,11},{10,... | collective-permute-start | bytes 11528 | tf_op jit(solution)/shard_map/ppermute | solution.py:97
